TPU v7x, 32 devices: a whole 2x2x4 slice. The times are simulated.
32 devices in a mesh: groups: 2 (over x), gx: 16 (over z, y, core).
Axes of the slice: x: 2, y: 2, z: 4, core: 2. Of those that a mesh axis runs over, the one named last changes fastest.
Arguments:
- points: bfloat16 [32, 6, 1, 128, 512], P(('groups', 'gx')), parts along dimension 0, may hold values from -6 to 6
- order: int32 [32, 6, 1, 128], P(('groups', 'gx')), parts along dimension 0, may hold values from 0 to 127, each once within a row
- masks: int32 [32, 6, 1, 26], P(('groups', 'gx')), parts along dimension 0, may hold values 0 or 1
- counts: int32 [32, 6, 1], P('groups'), parts along dimension 0, may hold values from 1 to 128
- gain: float32 [512], replicated, may hold values from 0.5 to 1.5
- shift_bias: float32 [512], replicated, may hold values from -3 to 3
- w_qkv: bfloat16 [512, 1536], replicated, may hold values from -1.5 to 1.5
- w_out: bfloat16 [512, 512], replicated, may hold values from -0.25 to 0.25
Outputs:
- result: bfloat16 [32, 6, 1, 128, 512], P(('groups', 'gx')), parts along dimension 0
There are 2 independent parts, one for each index of `groups`. A program takes and returns all parts, laid end to end along the dimension named above; an argument that names none is the same for every part. Nothing has to cross between parts.
All inputs are finite; a program needn't handle non-finite values. No bound on the sum of `masks` on one device may be relied on, other than what follows from the above.
Results may differ from a plain program's by a relative error of at most 0.012.
Values may be sent and summed in bfloat16 or wider, within the bound.
No kernel may reach another device: no remote copies, remote signals or barrier semaphores. Data moves between devices by JAX's collectives and lax.ppermute only.
A program may use at most 128 MiB of HBM per device.

v0:
```python
import jax
import jax.numpy as jnp
from jax import lax
from jax.sharding import PartitionSpec as P

HEADS = 8


neighbour_offsets = [(a, b, c) for a in (-1, 0, 1) for b in (-1, 0, 1) for c in (-1, 0, 1)]


def extended(value, sides, width):
    for axis, dim in sides:
        size, length = (lax.axis_size(axis), value.shape[dim])
        up = [(i, (i + 1) % size) for i in range(size - 1)]
        down = [(j, i) for i, j in up]
        last = lax.slice_in_dim(value, length - width, length, axis=dim)
        leading = lax.slice_in_dim(value, 0, width, axis=dim)
        before = lax.ppermute(last, axis, up)
        after = lax.ppermute(leading, axis, down)
        value = jnp.concatenate([before, value, after], axis=dim)
    return value


def column_of(a, b, c):
    index = 9 * (a + 1) + 3 * (b + 1) + (c + 1)
    return index if index < 13 else index - 1


def layer_norm(tiled, gain, shift_bias):
    values = tiled.astype(jnp.float32)
    mean = jnp.mean(values, axis=-1, keepdims=True)
    var = jnp.mean((values - mean) ** 2, axis=-1, keepdims=True)
    return ((values - mean) * lax.rsqrt(var + 1e-05) * gain + shift_bias).astype(jnp.bfloat16)


def reachable(offsets, by, bz):
    return [o for o in offsets if (by > 1 or o[1] == 0) and (bz > 1 or o[2] == 0)]


def collect_keys(slabs, counts_pad, masks, offsets, by, bz, p):
    positions = jnp.arange(p, dtype=jnp.int32)
    blocks = []
    valids = []
    for a, b, c in offsets:
        block = slabs[a + 1][1 + b : 1 + b + by, 1 + c : 1 + c + bz]
        near = counts_pad[a + 1, 1 + b : 1 + b + by, 1 + c : 1 + c + bz]
        valid = positions[None, None, :] < near[:, :, None]
        if (a, b, c) != (0, 0, 0):
            valid = valid & (masks[:, :, column_of(a, b, c)][:, :, None] == 1)
        blocks.append(block)
        valids.append(valid)
    width2 = blocks[0].shape[-1]
    keyvals = jnp.concatenate(blocks, axis=2).reshape(by * bz, -1, width2)
    valid = jnp.concatenate(valids, axis=2).reshape(by * bz, -1)
    return (keyvals, valid)


def head_major(query, keyval, heads):
    p, width = query.shape
    hd = width // heads
    qh = jnp.transpose(query.reshape(p, heads, hd), (1, 0, 2))
    kh = jnp.transpose(keyval[:, :width].reshape(-1, heads, hd), (1, 0, 2))
    vh = jnp.transpose(keyval[:, width:].reshape(-1, heads, hd), (1, 0, 2))
    return (qh, kh, vh)


def score_block(qh, kh, mask):
    scale = 1.0 / qh.shape[-1] ** 0.5
    scores = jnp.einsum("hqd,hkd->hqk", qh, kh, preferred_element_type=jnp.float32) * scale
    return jnp.where(mask[None, None, :], scores, -1e30)


def finish_block(scores, vh):
    top = jnp.max(scores, axis=-1, keepdims=True)
    probs = jnp.exp(scores - top)
    total = jnp.sum(probs, axis=-1, keepdims=True)
    accum = jnp.einsum(
        "hqk,hkd->hqd", probs.astype(jnp.bfloat16), vh, preferred_element_type=jnp.float32
    )
    out = accum / total
    heads, p, hd = out.shape
    return jnp.transpose(out, (1, 0, 2)).reshape(p, heads * hd)


def fetch_rims(operand):
    rims = extended(operand[None], (("gx", 0),), 1)
    return (rims[0], rims[2])


def pad_cross(slab):
    return jnp.pad(slab, ((1, 1), (1, 1), (0, 0), (0, 0)))


def shards(points, order, masks, counts, gain, shift_bias, w_qkv, w_out):
    _, by, bz, p, width = points.shape
    tiled = jnp.take_along_axis(points, order[..., None], axis=3)[0]
    normed = layer_norm(tiled, gain, shift_bias)
    qkv = jnp.dot(normed.reshape(-1, width), w_qkv, preferred_element_type=jnp.float32).astype(
        jnp.bfloat16
    )
    qkv = qkv.reshape(by, bz, p, 3 * width)
    queries = qkv[..., :width]
    keyvals = qkv[..., width:]
    place = lax.axis_index("gx")
    counts_pad = lax.dynamic_slice(
        jnp.pad(counts, 1), (place, jnp.int32(0), jnp.int32(0)), (3, by + 2, bz + 2)
    )
    own_masks = masks[0]
    w_keyvals = w_qkv[:, width:]
    flat_queries = queries.reshape(by * bz, p, width)

    def to_keyvals(rim):
        made = jnp.dot(rim.reshape(-1, width), w_keyvals, preferred_element_type=jnp.float32)
        return made.astype(jnp.bfloat16).reshape(by, bz, p, 2 * width)

    own_slab = pad_cross(keyvals)
    kept = reachable(neighbour_offsets, by, bz)
    below, above = fetch_rims(normed)
    slabs = (pad_cross(to_keyvals(below)), own_slab, pad_cross(to_keyvals(above)))
    gathered, valid = collect_keys(slabs, counts_pad, own_masks, kept, by, bz, p)

    def whole_block(operands):
        query, keyval, mask = operands
        qh, kh, vh = head_major(query, keyval, HEADS)
        return finish_block(score_block(qh, kh, mask), vh)

    attn = lax.map(whole_block, (flat_queries, gathered, valid))
    attn = attn.reshape(by, bz, p, width).astype(jnp.bfloat16)
    mixed = jnp.dot(attn.reshape(-1, width), w_out, preferred_element_type=jnp.float32).reshape(
        by, bz, p, width
    )
    mixed = tiled.astype(jnp.float32) + mixed
    own_counts = counts_pad[1, 1 : 1 + by, 1 : 1 + bz]
    live = jnp.arange(p, dtype=jnp.int32)[None, None, :] < own_counts[..., None]
    return jnp.where(live[..., None], mixed, 0.0).astype(jnp.bfloat16)[None]


def solution(mesh):
    placed = (
        P(("groups", "gx"), None, None, None, None),
        P(("groups", "gx"), None, None, None),
        P(("groups", "gx"), None, None, None),
        P("groups", None, None),
        P(),
        P(),
        P(),
        P(),
    )
    return jax.shard_map(
        shards,
        mesh=mesh,
        in_specs=placed,
        out_specs=P(("groups", "gx"), None, None, None, None),
        check_vma=False,
    )
```

profile of v0, /device:TPU:1, one launch (start us, length us, event | category | flops | bytes accessed | tf_op | source)
XLA Modules:
  0.0 97.5 jit_solution(1429662255774653734)
XLA Ops:
  0.8 2.3 %fusion.44 = (s32[6]{0:T(128)S(1)}, s32[6]{0:T(128)S(1)}, s32[6]{0:T(128)S(1)}, s32[6]{0:T(128)S(1)}, s32[6]{0:T(128)S(1)}, /*index=5*/s32[6]{0:T(128)S(1)}, s32[6]{0:T(128)S(1)}, s32[6]{0:T(128)S(1)}, s32[6]{0:T(128)S(1)}) fusion(s32[]{:T(128)S(6)} %add.132, s32[]{:T(128)S(6)} %add.125, s32[]{:T(128)S(6)} %add.120, s32[16,6,1]{0,2,1:T(1,128)} %param.13, ...), kind=kLoop, calls=%fused_computation.106 | loop fusion | bytes 620 | tf_op jit(solution)/shard_map/slice | solution.py:47
  3.8 5.5 %gather_fusion = bf16[768,512]{1,0:T(8,128)(2,1)S(1)} fusion(bf16[6,128,512]{2,1,0:T(8,128)(2,1)S(1)} %bitcast.81, s32[768]{0:T(1024)S(1)} %bitcast.84), kind=kCustom, calls=%fused_computation | custom fusion | bytes 1579008 | tf_op jit(solution)/shard_map/jit(take_along_axis)/gather | solution.py:97
  11.7 4.5 %collective-permute-start = (bf16[1,6,1,128,512]{4,3,1,2,0:T(8,128)(2,1)}, bf16[1,6,1,128,512]{4,3,1,2,0:T(8,128)(2,1)}, u32[]{:S(2)}, u32[]{:S(2)}) collective-permute-start(bf16[1,6,1,128,512]{4,3,1,2,0:T(8,128)(2,1)} %add_convert_fusion), channel_id=1, source_target_pairs={{0,1},{1,2},{2,3},{3,4},{4,5},{5,6},{6,7},{7,8},{8,9},{9,10},{10,1... | collective-permute-start | bytes 2359304 | tf_op jit(solution)/shard_map/ppermute | solution.py:19
  16.2 2.1 %collective-permute-start.1 = (bf16[1,6,1,128,512]{4,3,1,2,0:T(8,128)(2,1)}, bf16[1,6,1,128,512]{4,3,1,2,0:T(8,128)(2,1)}, u32[]{:S(2)}, u32[]{:S(2)}) collective-permute-start(bf16[1,6,1,128,512]{4,3,1,2,0:T(8,128)(2,1)} %add_convert_fusion), channel_id=1, source_target_pairs={{1,0},{2,1},{3,2},{4,3},{5,4},{6,5},{7,6},{8,7},{9,8},{10,9},{11,1... | collective-permute-start | bytes 2359304 | tf_op jit(solution)/shard_map/ppermute | solution.py:20
  18.3 3.0 %convolution_convert_fusion = bf16[768,1536]{1,0:T(8,128)(2,1)S(1)} fusion(bf16[512,1536]{1,0:T(8,128)(2,1)} %param.16, f32[512]{0:T(512)S(1)} %copy-done.5, f32[512]{0:T(512)S(1)} %copy-done.6, f32[768]{0:T(1024)S(1)} %get-tuple-element.75, f32[768]{0:T(1024)S(1)} %get-tuple-element.76, bf16[768,512]{1,0:T(8,128)(2,1)S(1)} %gather_fusion, ...), kind=kOutput, calls=%fused_computation.20 | convolution fusion | flops 1211891712 | bytes 4729600 | tf_op jit(solution)/shard_map/dot_general | solution.py:99
  21.3 1.4 %slice.127 = bf16[6,1,128,1024]{3,2,0,1:T(8,128)(2,1)} slice(bf16[6,1,128,1536]{3,2,0,1:T(8,128)(2,1)S(1)} %bitcast.93), slice={[0:6], [0:1], [0:128], [512:1536]} | slice | bytes 3145728 | tf_op jit(solution)/shard_map/slice | solution.py:104
  23.7 1.9 %copy.30 = bf16[6,1,128,1024]{2,3,0,1:T(8,128)(2,1)S(1)} copy(bf16[6,1,128,1024]{3,2,0,1:T(8,128)(2,1)} %slice.127) | data formatting | bytes 3145728
  25.6 2.3 %copy.29 = bf16[6,1,128,512]{2,3,0,1:T(8,128)(2,1)} copy(bf16[6,1,128,512]{3,2,0,1:T(8,128)(2,1)} %slice.126) | data formatting | bytes 1572864
  29.7 4.2 %collective-permute-done = bf16[1,6,1,128,512]{4,3,1,2,0:T(8,128)(2,1)} collective-permute-done((bf16[1,6,1,128,512]{4,3,1,2,0:T(8,128)(2,1)}, bf16[1,6,1,128,512]{4,3,1,2,0:T(8,128)(2,1)}, u32[]{:S(2)}, u32[]{:S(2)}) %collective-permute-start) | collective-permute-done | bytes 786464 | tf_op jit(solution)/shard_map/ppermute | solution.py:19
  33.8 3.6 %convolution_convert_fusion.2 = bf16[768,1024]{1,0:T(8,128)(2,1)} fusion(bf16[768,512]{1,0:T(8,128)(2,1)} %bitcast.21, bf16[512,1536]{1,0:T(8,128)(2,1)} %param.16), kind=kOutput, calls=%fused_computation.24 | convolution fusion | flops 806092800 | bytes 3407872 | tf_op jit(solution)/shard_map/dot_general | solution.py:114
  37.4 2.6 %copy.19 = bf16[6,1,128,1024]{2,3,0,1:T(8,128)(2,1)} copy(bf16[6,1,128,1024]{3,2,0,1:T(8,128)(2,1)} %bitcast.95) | data formatting | bytes 3145728 | tf_op jit(solution)/shard_map/reshape | solution.py:115
  40.0 1.7 %fusion.14 = bf16[6,1,1152,1024]{2,3,0,1:T(8,128)(2,1)S(1)} fusion(bf16[6,1,128,1024]{2,3,0,1:T(8,128)(2,1)} %copy.19), kind=kLoop, calls=%fused_computation.27 | loop fusion | bytes 3145728
  44.9 4.4 %convolution_convert_fusion.1 = bf16[768,1024]{1,0:T(8,128)(2,1)} fusion(bf16[768,512]{1,0:T(8,128)(2,1)} %bitcast.23, bf16[512,1536]{1,0:T(8,128)(2,1)S(1)} %copy-done.7), kind=kOutput, calls=%fused_computation.23 | convolution fusion | flops 806092800 | bytes 3407872 | tf_op jit(solution)/shard_map/dot_general | solution.py:114
  49.3 1.9 %copy.21 = bf16[6,1,128,1024]{2,3,0,1:T(8,128)(2,1)S(1)} copy(bf16[6,1,128,1024]{3,2,0,1:T(8,128)(2,1)} %bitcast.96) | data formatting | bytes 3145728 | tf_op jit(solution)/shard_map/reshape | solution.py:115
  52.5 1.4 %constant_dynamic-update-slice_fusion.10 = bf16[6,1,1152,1024]{2,3,0,1:T(8,128)(2,1)} fusion(bf16[6,1,1152,1024]{2,3,0,1:T(8,128)(2,1)} %fusion.18, bf16[6,1,128,1024]{2,3,0,1:T(8,128)(2,1)S(1)} %copy.21), kind=kLoop, calls=%fused_computation.67 | loop fusion | bytes 3145728
  53.9 1.3 %fusion.19 = bf16[6,1,1152,1024]{2,3,0,1:T(8,128)(2,1)} fusion(bf16[6,1,1152,1024]{2,3,0,1:T(8,128)(2,1)} %constant_dynamic-update-slice_fusion.10, bf16[6,1,128,1024]{2,3,0,1:T(8,128)(2,1)S(1)} %copy.21), kind=kLoop, calls=%fused_computation.32 | loop fusion | bytes 3145728 | tf_op jit(solution)/shard_map/concatenate | solution.py:54
  55.2 39.6 %while.10 = (s32[]{:T(128)}, bf16[6,128,512]{1,2,0:T(8,128)(2,1)}, pred[6,1152]{1,0:T(8,128)(4,1)S(1)}, bf16[6,128,512]{1,2,0:T(8,128)(2,1)}, bf16[6,1152,1024]{1,2,0:T(8,128)(2,1)}, /*index=5*/s32[]{:T(128)}) while((s32[]{:T(128)}, bf16[6,128,512]{1,2,0:T(8,128)(2,1)}, pred[6,1152]{1,0:T(8,128)(4,1)S(1)}, bf16[6,128,512]{1,2,0:T(8,128)(2,1)}, ...), condition=%wide.region_5.6_spmd, body=%wide.region_2.5_spmd.sunk | while | flops 310376448 | bytes 26763216 | solution.py:128
  55.2 1.9 %dynamic-slice_bitcast_fusion.2 = bf16[1152,1024]{0,1:T(8,128)(2,1)S(1)} fusion(bf16[6,1152,1024]{1,2,0:T(8,128)(2,1)} %get-tuple-element.135, s32[]{:T(128)} %get-tuple-element.125), kind=kLoop, calls=%fused_computation.8.clone.1 | loop fusion | bytes 4718596 | tf_op jit(solution)/shard_map/while/body/jit(dynamic_index_in_dim)/squeeze | solution.py:128
  61.9 1.8 %dynamic-slice_bitcast_fusion.2 = bf16[1152,1024]{0,1:T(8,128)(2,1)S(1)} fusion(bf16[6,1152,1024]{1,2,0:T(8,128)(2,1)} %get-tuple-element.135, s32[]{:T(128)} %get-tuple-element.125), kind=kLoop, calls=%fused_computation.8.clone.1 | loop fusion | bytes 4718596 | tf_op jit(solution)/shard_map/while/body/jit(dynamic_index_in_dim)/squeeze | solution.py:128
  68.5 1.8 %dynamic-slice_bitcast_fusion.2 = bf16[1152,1024]{0,1:T(8,128)(2,1)S(1)} fusion(bf16[6,1152,1024]{1,2,0:T(8,128)(2,1)} %get-tuple-element.135, s32[]{:T(128)} %get-tuple-element.125), kind=kLoop, calls=%fused_computation.8.clone.1 | loop fusion | bytes 4718596 | tf_op jit(solution)/shard_map/while/body/jit(dynamic_index_in_dim)/squeeze | solution.py:128
  75.1 1.8 %dynamic-slice_bitcast_fusion.2 = bf16[1152,1024]{0,1:T(8,128)(2,1)S(1)} fusion(bf16[6,1152,1024]{1,2,0:T(8,128)(2,1)} %get-tuple-element.135, s32[]{:T(128)} %get-tuple-element.125), kind=kLoop, calls=%fused_computation.8.clone.1 | loop fusion | bytes 4718596 | tf_op jit(solution)/shard_map/while/body/jit(dynamic_index_in_dim)/squeeze | solution.py:128
  81.7 1.8 %dynamic-slice_bitcast_fusion.2 = bf16[1152,1024]{0,1:T(8,128)(2,1)S(1)} fusion(bf16[6,1152,1024]{1,2,0:T(8,128)(2,1)} %get-tuple-element.135, s32[]{:T(128)} %get-tuple-element.125), kind=kLoop, calls=%fused_computation.8.clone.1 | loop fusion | bytes 4718596 | tf_op jit(solution)/shard_map/while/body/jit(dynamic_index_in_dim)/squeeze | solution.py:128
  88.3 1.8 %dynamic-slice_bitcast_fusion.2 = bf16[1152,1024]{0,1:T(8,128)(2,1)S(1)} fusion(bf16[6,1152,1024]{1,2,0:T(8,128)(2,1)} %get-tuple-element.135, s32[]{:T(128)} %get-tuple-element.125), kind=kLoop, calls=%fused_computation.8.clone.1 | loop fusion | bytes 4718596 | tf_op jit(solution)/shard_map/while/body/jit(dynamic_index_in_dim)/squeeze | solution.py:128
  94.9 2.6 %fusion.20 = bf16[1,6,1,128,512]{4,3,2,1,0:T(8,128)(2,1)} fusion(bf16[6,128,512]{1,2,0:T(8,128)(2,1)} %get-tuple-element.32, bf16[6,128,512]{2,1,0:T(8,128)(2,1)S(1)} %bitcast.91, pred[6,128]{1,0:T(8,128)(4,1)S(1)} %get-tuple-element.79, pred[6,128]{1,0:T(8,128)(4,1)S(1)} %get-tuple-element.78, bf16[512,512]{1,0:T(8,128)(2,1)S(1)} %copy-done.8), kind=kOutput, calls=%fused_computation.36 | convolution fusion | flops 404619264 | bytes 2885120 | tf_op jit(solution)/shard_map/dot_general | solution.py:130
  (88 shorter events, 39.4 us)
Async XLA Ops:
  0.0 3.8 %copy-start = (bf16[1,6,1,128,512]{4,3,2,1,0:T(8,128)(2,1)S(1)}, bf16[1,6,1,128,512]{4,3,2,1,0:T(8,128)(2,1)}, u32[]{:S(2)}) copy-start(bf16[1,6,1,128,512]{4,3,2,1,0:T(8,128)(2,1)} %param.10) | copy-start | bytes 2359300
  9.3 1.0 %copy-start.5 = (f32[512]{0:T(512)S(1)}, f32[512]{0:T(512)}, u32[]{:S(2)}) copy-start(f32[512]{0:T(512)} %param.15) | copy-start | bytes 6148
  9.3 1.0 %copy-start.6 = (f32[512]{0:T(512)S(1)}, f32[512]{0:T(512)}, u32[]{:S(2)}) copy-start(f32[512]{0:T(512)} %param.14) | copy-start | bytes 6148
  9.3 9.0 %copy-start.4 = (s32[1,6,1,128]{3,2,1,0:T(1,128)S(1)}, s32[1,6,1,128]{3,2,1,0:T(1,128)}, u32[]{:S(2)}) copy-start(s32[1,6,1,128]{3,2,1,0:T(1,128)} %param.11) | copy-start | bytes 9220
  11.7 22.2 %collective-permute-start = (bf16[1,6,1,128,512]{4,3,1,2,0:T(8,128)(2,1)}, bf16[1,6,1,128,512]{4,3,1,2,0:T(8,128)(2,1)}, u32[]{:S(2)}, u32[]{:S(2)}) collective-permute-start(bf16[1,6,1,128,512]{4,3,1,2,0:T(8,128)(2,1)} %add_convert_fusion), channel_id=1, source_target_pairs={{0,1},{1,2},{2,3},{3,4},{4,5},{5,6},{6,7},{7,8},{8,9},{9,10},{10,1... | collective-permute-start | bytes 2359304 | tf_op jit(solution)/shard_map/ppermute | solution.py:19
  16.2 27.6 %collective-permute-start.1 = (bf16[1,6,1,128,512]{4,3,1,2,0:T(8,128)(2,1)}, bf16[1,6,1,128,512]{4,3,1,2,0:T(8,128)(2,1)}, u32[]{:S(2)}, u32[]{:S(2)}) collective-permute-start(bf16[1,6,1,128,512]{4,3,1,2,0:T(8,128)(2,1)} %add_convert_fusion), channel_id=1, source_target_pairs={{1,0},{2,1},{3,2},{4,3},{5,4},{6,5},{7,6},{8,7},{9,8},{10,9},{11,1... | collective-permute-start | bytes 2359304 | tf_op jit(solution)/shard_map/ppermute | solution.py:20
  25.6 2.3 %copy-start.3 = (s32[1,6,1,26]{3,2,1,0:T(1,128)S(1)}, s32[1,6,1,26]{3,2,1,0:T(1,128)}, u32[]{:S(2)}) copy-start(s32[1,6,1,26]{3,2,1,0:T(1,128)} %param.12) | copy-start | bytes 1876
  40.0 1.8 %copy-start.1 = (bf16[6,1,128,1024]{2,3,0,1:T(8,128)(2,1)S(1)}, bf16[6,1,128,1024]{2,3,0,1:T(8,128)(2,1)}, u32[]{:S(2)}) copy-start(bf16[6,1,128,1024]{2,3,0,1:T(8,128)(2,1)} %copy.19) | copy-start | bytes 4718596
  43.4 1.6 %copy-start.7 = (bf16[512,1536]{1,0:T(8,128)(2,1)S(1)}, bf16[512,1536]{1,0:T(8,128)(2,1)}, u32[]{:S(2)}) copy-start(bf16[512,1536]{1,0:T(8,128)(2,1)} %param.16) | copy-start | bytes 4718596
  43.8 5.5 %copy-start.2 = (bf16[6,1,1152,1024]{2,3,0,1:T(8,128)(2,1)}, bf16[6,1,1152,1024]{2,3,0,1:T(8,128)(2,1)S(1)}, u32[]{:S(2)}) copy-start(bf16[6,1,1152,1024]{2,3,0,1:T(8,128)(2,1)S(1)} %fusion.17) | copy-start | bytes 42467332
  55.2 39.7 %copy-start.8 = (bf16[512,512]{1,0:T(8,128)(2,1)S(1)}, bf16[512,512]{1,0:T(8,128)(2,1)}, u32[]{:S(2)}) copy-start(bf16[512,512]{1,0:T(8,128)(2,1)} %param.17) | copy-start | bytes 1572868
where the time goes:
time: 98.4 us; the launch traced here: 97.5 us
  local copies, waits for them, and re-layouts  49.7 us (51%)
  matrix products  25.5 us (26%)
  other arithmetic  11.1 us (11%)
  starting transfers between devices  6.62 us (7%)
  waiting for transfers between devices  4.19 us (4%)
    unnamed x28, local copies, waits for them, and re-layouts  11.8 us
    squeeze x6, local copies, waits for them, and re-layouts, shards(): attn = lax.map(whole_block, (flat_queries, gathered, valid))  11.1 us
    dot_general x2, matrix products, to_keyvals(): jnp.dot(rim.reshape(-1, width), w_keyvals, preferred_element_type=jnp.flo...  7.95 us
    dot_general x6, matrix products, finish_block(): jnp.einsum('hqk,hkd->hqd', probs.astype(jnp.bfloat16), vh, preferred_elem...  6.45 us
    dynamic_slice x12, local copies, waits for them, and re-layouts, shards(): attn = lax.map(whole_block, (flat_queries, gathered, valid))  5.74 us
    reduce_sum x6, other arithmetic, finish_block(): total = jnp.sum(probs, axis=-1, keepdims=True)  5.57 us
    dot_general x6, matrix products, score_block(): jnp.einsum('hqd,hkd->hqk', qh, kh, preferred_element_type=jnp.float32)  5.49 us
    gather x1, local copies, waits for them, and re-layouts, shards(): tiled = jnp.take_along_axis(points, order[..., None], axis=3)[0]  5.47 us
  transfers between devices with their start and end apart: 2, of which 1 were waited for; matrix products, arithmetic and copies ran while one was open for 22% of the time, Pallas kernels for 0%

commit v1 on v0

v1 whole, which is shorter than its diff:
```python
import functools

import jax
import jax.numpy as jnp
from jax import lax
from jax.experimental import pallas as pl
from jax.experimental.pallas import tpu as pltpu
from jax.sharding import PartitionSpec as P

HEADS = 8
NEG = -1e30
ONES = 16
LIMIT = 24 * 1024 * 1024
BF16, F32 = jnp.bfloat16, jnp.float32


def tn(a, b):
    return lax.dot_general(a, b, (((0,), (0,)), ((), ())), preferred_element_type=F32)


def nn(a, b):
    return jnp.dot(a, b, preferred_element_type=F32)


def normalise(tiled, gain, shift):
    values = tiled.astype(F32)
    mean = jnp.mean(values, axis=-1, keepdims=True)
    var = jnp.mean((values - mean) ** 2, axis=-1, keepdims=True)
    return ((values - mean) * lax.rsqrt(var + 1e-05) * gain + shift).astype(BF16)


def gather_kernel(
    split, points, order, counts, gain, shift, tiled, first, second, norm, raw, rows, live, sems
):
    _, by, _, p, width = points.shape
    me = lax.axis_index("gx")
    small = [
        pltpu.make_async_copy(order, rows, sems.at[by]),
        pltpu.make_async_copy(counts, live, sems.at[by + 1]),
        pltpu.make_async_copy(gain, norm.at[0:1], sems.at[by + 2]),
        pltpu.make_async_copy(shift, norm.at[1:2], sems.at[by + 3]),
    ]
    large = [pltpu.make_async_copy(points.at[0, j, 0], raw.at[j], sems.at[j]) for j in range(by)]
    for copy in (*small, *large):
        copy.start()
    slot = lax.broadcasted_iota(jnp.int32, (p, p), 0)
    place = lax.broadcasted_iota(jnp.int32, (1, p), 1)
    small[0].wait()
    small[1].wait()
    picks = []
    for j in range(by):
        row = rows[0, j]
        row = jnp.where(place < live[j, 0, me], row, row[:, :1])
        picks.append((slot == row).astype(F32).astype(BF16))
    for j in range(by):
        large[j].wait()
        got = tn(picks[j], raw[j]).astype(BF16)
        tiled[j] = got
        if j < split:
            first[j] = got
        else:
            second[j - split] = got
    small[2].wait()
    small[3].wait()


def toward_near():
    return 1 - 2 * (lax.axis_index("gx") & 1)


def column(side, b):
    index = 9 * (side + 1) + 3 * (b + 1) + 1
    if isinstance(index, int):
        return index if index < 13 else index - 1
    return jnp.where(index > 13, index - 1, index)


def list_pairs(items, masks, by, sides):
    spare = sum(j1 - j0 for _, _, j0, j1, _, _ in sides)
    pairs, ends = jnp.int32(0), []
    for i in range(by):
        start, found, last = pairs, jnp.int32(0), jnp.int32(0)
        most = 0
        for side, exists, j0, j1, tile0, own in sides:
            for b in (0, -1, 1):
                j = i + b
                if not j0 <= j < j1:
                    continue
                tile = tile0 + j - j0
                items[1, 2 * start + found] = tile
                items[2, 2 * start + found] = tile
                most += 1
                if own and b == 0:
                    found = found + 1
                    last = jnp.int32(tile)
                    continue
                on = masks[0, i, 0, column(side, b)] == 1
                on = on if exists is None else on & exists
                found = found + on.astype(jnp.int32)
                last = jnp.where(on, tile, last)
        items[1, 2 * start + found] = last
        items[2, 2 * start + found] = spare
        for u in range((most + 1) // 2):
            items[0, start + u] = i
        pairs = start + ((found + 1) >> 1)
        ends.append(pairs)
    return pairs, ends


def attend(items, low, high, keys, vals, qt, top, acc):
    groups, depth, lanes = qt.shape[1:]
    hd, p = depth // 2, lanes // 2

    def step(t, carry):
        i = items[0, t]
        k0, k1 = items[1, 2 * t], items[1, 2 * t + 1]
        v0, v1 = items[2, 2 * t], items[2, 2 * t + 1]
        for g in range(groups):
            rows = slice(g * depth, (g + 1) * depth)
            cols = slice(g * lanes, (g + 1) * lanes)
            s0 = nn(keys[k0, :, rows], qt[i, g])
            s1 = nn(keys[k1, :, rows], qt[i, g])
            old = top[i, :, cols]
            new = jnp.maximum(old, jnp.max(jnp.maximum(s0, s1), axis=0, keepdims=True))
            probs = jnp.concatenate(
                [jnp.exp(s0 - new).astype(BF16), jnp.exp(s1 - new).astype(BF16)], axis=0
            )
            fade = jnp.exp(old - new)
            out = nn(jnp.concatenate([vals[v0, g], vals[v1, g]], axis=1), probs)
            both = jnp.concatenate([out[:hd, :p], out[hd:depth, p:]], axis=1)
            top[i, :, cols] = new
            acc[i, :hd, cols] = acc[i, :hd, cols] * fade + both
            acc[i, hd:, cols] = acc[i, hd:, cols] * fade + out[depth : depth + 8]
        return carry

    lax.fori_loop(low, high, step, 0)


def put_values(vals, tile, v, live):
    groups, _, p = vals.shape[1:]
    depth = v.shape[1] // groups
    flag = jnp.broadcast_to(live.astype(F32).astype(BF16), (ONES, p))
    vt = jnp.where(live, v.T, 0.0).astype(BF16)
    for g in range(groups):
        vals[tile, g, :depth] = vt[g * depth : (g + 1) * depth]
        vals[tile, g, depth:] = flag


def finish(i, tiled, acc, w_out, alive):
    hd = acc.shape[1] - 8
    p = tiled.shape[1]
    heads = acc.shape[2] // p
    attn = acc[i, :hd] * (1.0 / acc[i, hd : hd + 1])
    attn = jnp.concatenate([attn[:, h * p : (h + 1) * p] for h in range(heads)], axis=0).astype(BF16)
    mixed = tiled[i].astype(F32) + tn(attn, w_out[...])
    place = lax.broadcasted_iota(jnp.int32, (p, 1), 0)
    return jnp.where(place < alive, mixed, 0.0).astype(BF16)


def main_kernel(
    n, tiled, near, norm, masks, counts, w_qkv, w_out, qt, top, acc, w_all, w_last, keys, vals, flags, live,
    items, sems
):
    by, p, width = tiled.shape
    groups, depth = qt.shape[1:3]
    hd = depth // 2
    copies = [
        pltpu.make_async_copy(masks, flags, sems.at[0]),
        pltpu.make_async_copy(counts, live, sems.at[1]),
        pltpu.make_async_copy(w_qkv, w_all, sems.at[2]),
        pltpu.make_async_copy(w_out, w_last, sems.at[3]),
    ]
    for copy in copies:
        copy.start()
    me = lax.axis_index("gx")
    side = toward_near()
    partner = me + side
    exists = (partner >= 0) & (partner < n)
    slab = jnp.clip(partner, 0, n - 1)
    place = lax.broadcasted_iota(jnp.int32, (1, p), 1)
    gain, shift = norm[0:1], norm[1:2]
    top[...] = jnp.full_like(top, NEG)
    acc[...] = jnp.zeros_like(acc)
    vals[2 * by] = jnp.zeros(vals.shape[1:], BF16)
    copies[0].wait()
    copies[1].wait()
    pairs, _ = list_pairs(
        items, flags, by, [(0, None, 0, by, 0, True), (side, exists, 0, by, by, False)]
    )
    zeros = jnp.zeros((hd, p), BF16)
    copies[2].wait()
    for c in range(0, by, 2):
        span = range(c, min(c + 2, by))
        x = jnp.concatenate([normalise(tiled[j], gain, shift) for j in span], axis=0)
        q = (nn(x, w_all[:, :width]).astype(BF16) * BF16(1.0 / hd**0.5)).astype(F32)
        k = nn(x, w_all[:, width : 2 * width]).astype(BF16)
        v = nn(x, w_all[:, 2 * width :])
        for u, i in enumerate(span):
            rows = slice(u * p, (u + 1) * p)
            keys[i] = k[rows]
            put_values(vals, i, v[rows], place < live[i, 0, me])
            t = q[rows].T.astype(BF16)
            for g in range(groups):
                mid = g * depth + hd
                qt[i, g, :hd, :p] = t[g * depth : mid]
                qt[i, g, :hd, p:] = zeros
                qt[i, g, hd:, :p] = zeros
                qt[i, g, hd:, p:] = t[mid : mid + hd]
        x = jnp.concatenate([normalise(near[j], gain, shift) for j in span], axis=0)
        k = nn(x, w_all[:, width : 2 * width]).astype(BF16)
        v = nn(x, w_all[:, 2 * width :])
        for u, i in enumerate(span):
            rows = slice(u * p, (u + 1) * p)
            keys[by + i] = k[rows]
            put_values(vals, by + i, v[rows], place < live[i, 0, slab])
    attend(items, 0, pairs, keys, vals, qt, top, acc)
    copies[3].wait()


def far_work(n, j0, by, rim, norm, masks, counts, w_all, qt, top, acc, keys, vals, flags, live, items, sems):
    blocks, p, width = rim.shape
    copies = [
        pltpu.make_async_copy(masks, flags, sems.at[0]),
        pltpu.make_async_copy(counts, live, sems.at[1]),
    ]
    for copy in copies:
        copy.start()
    side = -toward_near()
    other = lax.axis_index("gx") + side
    exists = (other >= 0) & (other < n)
    slab = jnp.clip(other, 0, n - 1)
    place = lax.broadcasted_iota(jnp.int32, (1, p), 1)
    gain, shift = norm[0:1], norm[1:2]
    vals[blocks] = jnp.zeros(vals.shape[1:], BF16)
    copies[0].wait()
    copies[1].wait()
    pairs, _ = list_pairs(items, flags, by, [(side, exists, j0, j0 + blocks, 0, False)])
    for c in range(0, blocks, 2):
        span = range(c, min(c + 2, blocks))
        x = jnp.concatenate([normalise(rim[j], gain, shift) for j in span], axis=0)
        k = nn(x, w_all[:, width : 2 * width]).astype(BF16)
        v = nn(x, w_all[:, 2 * width :])
        for u, j in enumerate(span):
            rows = slice(u * p, (u + 1) * p)
            keys[j] = k[rows]
            put_values(vals, j, v[rows], place < live[j0 + j, 0, slab])
    attend(items, 0, pairs, keys, vals, qt, top, acc)


def hand_out(blocks, tiled, acc, w_out, live, result, out, sems):
    me = lax.axis_index("gx")
    copies = []
    for u, i in enumerate(blocks):
        out[u] = finish(i, tiled, acc, w_out, live[i, 0, me])
        copies.append(pltpu.make_async_copy(out.at[u], result.at[0, i, 0], sems.at[2 + u]))
        copies[-1].start()
    for copy in copies:
        copy.wait()


def far_kernel(
    n, j0, done, rim, norm, masks, counts, w_all, qt, top_in, acc_in, tiled, w_out, top, acc, result, keys, vals,
    flags, live, items, out, sems
):
    by = tiled.shape[0]
    far_work(n, j0, by, rim, norm, masks, counts, w_all, qt, top, acc, keys, vals, flags, live, items, sems)
    hand_out(done, tiled, acc, w_out, live, result, out, sems)


def last_kernel(
    n, j0, done, rim, norm, masks, counts, w_all, qt, top_in, acc_in, tiled, w_out, result_in, top, acc, result,
    keys, vals, flags, live, items, out, sems
):
    by = tiled.shape[0]
    far_work(n, j0, by, rim, norm, masks, counts, w_all, qt, top, acc, keys, vals, flags, live, items, sems)
    hand_out(done, tiled, acc, w_out, live, result, out, sems)


def vmem(x):
    return pltpu.with_memory_space_constraint(x, pltpu.VMEM)


def hbm(x):
    return pltpu.with_memory_space_constraint(x, pltpu.HBM)


def shards(n, points, order, masks, counts, gain, shift_bias, w_qkv, w_out):
    _, by, bz, p, width = points.shape
    hd = width // HEADS
    groups, depth, lanes = HEADS // 2, 2 * hd, 2 * p
    split = max(by - 2, 1)
    early = max(split - 1, 0)
    whole = pl.BlockSpec(memory_space=pltpu.VMEM)
    apart = pl.BlockSpec(memory_space=pltpu.HBM)
    params = pltpu.CompilerParams(vmem_limit_bytes=LIMIT)
    points, order, masks, w_qkv, w_out = map(hbm, (points, order, masks, w_qkv, w_out))
    counts = hbm(jnp.transpose(counts, (1, 2, 0)))
    live = pltpu.SMEM(counts.shape, jnp.int32)
    flags = pltpu.SMEM(masks.shape, jnp.int32)

    tiled, first, second, norm = pl.pallas_call(
        functools.partial(gather_kernel, split),
        out_shape=(
            pltpu.VMEM((by, p, width), BF16),
            pltpu.VMEM((split, p, width), BF16),
            pltpu.VMEM((by - split, p, width), BF16),
            pltpu.VMEM((2, width), F32),
        ),
        in_specs=[apart] * 5,
        out_specs=(whole,) * 4,
        scratch_shapes=[
            pltpu.VMEM((by, p, width), BF16),
            pltpu.VMEM(order.shape, jnp.int32),
            live,
            pltpu.SemaphoreType.DMA((by + 4,)),
        ],
        compiler_params=params,
        name="gather",
    )(points, order, counts, hbm(gain[None]), hbm(shift_bias[None]))
    near_pairs = [(i, i ^ 1) for i in range(n) if i ^ 1 < n]
    far_pairs = [(i, i + 1) for i in range(1, n - 1, 2)] + [(i + 1, i) for i in range(1, n - 1, 2)]
    far0 = lax.ppermute(first, "gx", far_pairs)
    far1 = lax.ppermute(second, "gx", far_pairs)
    near = lax.ppermute(tiled, "gx", near_pairs)

    state = (
        pltpu.VMEM((by, 1, groups * lanes), F32),
        pltpu.VMEM((by, hd + 8, groups * lanes), F32),
    )

    def scratch(tiles):
        return [
            pltpu.VMEM((tiles, p, width), BF16),
            pltpu.VMEM((tiles + 1, groups, depth + ONES, p), BF16),
            flags,
            live,
            pltpu.SMEM((3, 8 * by), jnp.int32),
        ]

    qt, top, acc, w_all, w_last = pl.pallas_call(
        functools.partial(main_kernel, n),
        out_shape=(
            pltpu.VMEM((by, groups, depth, lanes), BF16),
            *state,
            pltpu.VMEM(w_qkv.shape, BF16),
            pltpu.VMEM(w_out.shape, BF16),
        ),
        in_specs=[whole, whole, whole, apart, apart, apart, apart],
        out_specs=(whole,) * 5,
        scratch_shapes=[*scratch(2 * by), pltpu.SemaphoreType.DMA((4,))],
        compiler_params=params,
        name="main",
    )(vmem(tiled), vmem(near), vmem(norm), masks, counts, w_qkv, w_out)

    def far(kernel, name, j0, done, block, top, acc, result):
        ins = [block, norm, masks, counts, w_all, qt, top, acc, tiled, w_last, *result]
        spaces = [whole, whole, apart, apart, *(whole,) * 6, *(apart,) * len(result)]
        ins = [vmem(x) if s is whole else x for x, s in zip(ins, spaces)]
        return pl.pallas_call(
            functools.partial(kernel, n, j0, done),
            out_shape=(*state, pltpu.HBM((1, by, bz, p, width), BF16)),
            in_specs=spaces,
            out_specs=(whole, whole, apart),
            scratch_shapes=[
                *scratch(block.shape[0]),
                pltpu.VMEM((max(len(done), 1), p, width), BF16),
                pltpu.SemaphoreType.DMA((2 + by,)),
            ],
            input_output_aliases={6: 0, 7: 1, **({10: 2} if result else {})},
            compiler_params=params,
            name=name,
        )(*ins)

    top, acc, result = far(far_kernel, "far", 0, range(early), far0, top, acc, ())
    _, _, result = far(last_kernel, "last", split, range(early, by), far1, top, acc, (result,))
    return result


def solution(mesh):
    placed = (
        P(("groups", "gx"), None, None, None, None),
        P(("groups", "gx"), None, None, None),
        P(("groups", "gx"), None, None, None),
        P("groups", None, None),
        P(),
        P(),
        P(),
        P(),
    )
    return jax.shard_map(
        functools.partial(shards, mesh.shape["gx"]),
        mesh=mesh,
        in_specs=placed,
        out_specs=P(("groups", "gx"), None, None, None, None),
        check_vma=False,
    )
```

time: 98.4 us -> 39 us (0.40)
  the two profiles are of different devices: /device:TPU:1 before, /device:TPU:23 now
where the time goes in v1:
time: 39 us; the launch traced here: 38.7 us
  Pallas kernels  31.5 us (81%)
  starting transfers between devices  7.2 us (18%)
    pallas_call x1, Pallas kernels, shards(): pl.pallas_call(functools.partial(main_kernel, n), out_shape=(pltpu.VMEM((...  16.9 us
    pallas_call x2, Pallas kernels, far(): pl.pallas_call(functools.partial(kernel, n, j0, done), out_shape=(*state,...  12.3 us
    ppermute x1, starting transfers between devices, shards(): far1 = lax.ppermute(second, 'gx', far_pairs)  3.41 us
    ppermute x1, starting transfers between devices, shards(): far0 = lax.ppermute(first, 'gx', far_pairs)  3.04 us
    pallas_call x1, Pallas kernels, shards(): pl.pallas_call(functools.partial(gather_kernel, split), out_shape=(pltpu....  2.3 us
  transfers between devices with their start and end apart: 3, of which 0 were waited for; matrix products, arithmetic and copies ran while one was open for 0% of the time, Pallas kernels for 61%

profile of v1, /device:TPU:23, one launch (start us, length us, event | category | flops | bytes accessed | tf_op | source)
XLA Modules:
  0.0 38.7 jit_solution(6613114785532955163)
XLA Ops:
  0.0 2.3 %gather.1 = (bf16[6,128,512]{2,1,0:T(8,128)(2,1)S(1)}, bf16[4,128,512]{2,1,0:T(8,128)(2,1)S(1)}, bf16[2,128,512]{2,1,0:T(8,128)(2,1)S(1)}, f32[2,512]{1,0:T(2,128)S(1)}) custom-call(bf16[1,6,1,128,512]{4,3,2,1,0:T(8,128)(2,1)} %points.1, s32[1,6,1,128]{3,2,1,0:T(1,128)} %order.1, s32[6,1,16]{2,1,0:T(1,128)} %bitcast.3, f32[1,512]{1,0:T(1,128)} %bitcast.7, ...), custom_call_target="tpu_custom_call" | custom-call | tf_op jit(solution)/shard_map/gather/pallas_call | solution.py:301
  2.3 0.7 %collective-permute-start.1 = (bf16[6,128,512]{2,1,0:T(8,128)(2,1)S(1)}, bf16[6,128,512]{2,1,0:T(8,128)(2,1)S(1)}, u32[]{:S(2)}, u32[]{:S(2)}) collective-permute-start(bf16[6,128,512]{2,1,0:T(8,128)(2,1)S(1)} %get-tuple-element.20.tiled), channel_id=1, source_target_pairs={{0,1},{1,0},{2,3},{3,2},{4,5},{5,4},{6,7},{7,6},{8,9},{9,8},{10,11... | collective-permute-start | bytes 2359304 | tf_op jit(solution)/shard_map/ppermute | solution.py:324
  3.1 3.0 %collective-permute-start.2 = (bf16[4,128,512]{2,1,0:T(8,128)(2,1)S(1)}, bf16[4,128,512]{2,1,0:T(8,128)(2,1)S(1)}, u32[]{:S(2)}, u32[]{:S(2)}) collective-permute-start(bf16[4,128,512]{2,1,0:T(8,128)(2,1)S(1)} %get-tuple-element.23), channel_id=1, source_target_pairs={{1,2},{3,4},{5,6},{7,8},{9,10},{11,12},{13,14},{2,1},{4,3},{6,5},{... | collective-permute-start | bytes 1572872 | tf_op jit(solution)/shard_map/ppermute | solution.py:322
  6.1 3.4 %collective-permute-start = (bf16[2,128,512]{2,1,0:T(8,128)(2,1)S(1)}, bf16[2,128,512]{2,1,0:T(8,128)(2,1)S(1)}, u32[]{:S(2)}, u32[]{:S(2)}) collective-permute-start(bf16[2,128,512]{2,1,0:T(8,128)(2,1)S(1)} %get-tuple-element.18), channel_id=1, source_target_pairs={{1,2},{3,4},{5,6},{7,8},{9,10},{11,12},{13,14},{2,1},{4,3},{6,5},{... | collective-permute-start | bytes 786440 | tf_op jit(solution)/shard_map/ppermute | solution.py:323
  9.5 0.0 collective-permute-done.1.near
  9.5 16.9 %main.1 = (bf16[6,4,128,256]{3,2,1,0:T(8,128)(2,1)S(1)}, f32[6,1,1024]{2,1,0:T(1,128)S(1)}, f32[6,72,1024]{2,1,0:T(8,128)S(1)}, bf16[512,1536]{1,0:T(8,128)(2,1)S(1)}, bf16[512,512]{1,0:T(8,128)(2,1)S(1)}) custom-call(bf16[6,128,512]{2,1,0:T(8,128)(2,1)S(1)} %get-tuple-element.20.tiled, bf16[6,128,512]{2,1,0:T(8,128)(2,1)S(1)} %collective-permute-done.1.near, ...), custom_call_target="tpu_custom_call" | custom-call | tf_op jit(solution)/shard_map/main/pallas_call | solution.py:340
  26.4 0.0 collective-permute-done.2.rim
  26.5 6.8 %far.1 = (f32[6,1,1024]{2,1,0:T(1,128)S(1)}, f32[6,72,1024]{2,1,0:T(8,128)S(1)}, bf16[1,6,1,128,512]{4,3,2,1,0:T(8,128)(2,1)}) custom-call(bf16[4,128,512]{2,1,0:T(8,128)(2,1)S(1)} %collective-permute-done.2.rim, f32[2,512]{1,0:T(2,128)S(1)} %get-tuple-element.19.norm, s32[1,6,1,26]{3,2,1,0:T(1,128)} %masks.5, ...), custom_call_target="tpu_custom_call", output_to_operand_aliasing={{0}: (6, {}), {1}: (7, {})} | custom-call | tf_op jit(solution)/shard_map/far/pallas_call | solution.py:359
  33.2 0.0 collective-permute-done.rim
  33.2 5.5 %last.1 = (f32[6,1,1024]{2,1,0:T(1,128)S(1)}, f32[6,72,1024]{2,1,0:T(8,128)S(1)}, bf16[1,6,1,128,512]{4,3,2,1,0:T(8,128)(2,1)}) custom-call(bf16[2,128,512]{2,1,0:T(8,128)(2,1)S(1)} %collective-permute-done.rim, f32[2,512]{1,0:T(2,128)S(1)} %get-tuple-element.19.norm, ...), custom_call_target="tpu_custom_call", output_to_operand_aliasing={{0}: (6, {}), {1}: (7, {}), {2}: (10, {})} | custom-call | tf_op jit(solution)/shard_map/last/pallas_call | solution.py:359
Async XLA Ops:
  2.3 7.2 %collective-permute-start.1 = (bf16[6,128,512]{2,1,0:T(8,128)(2,1)S(1)}, bf16[6,128,512]{2,1,0:T(8,128)(2,1)S(1)}, u32[]{:S(2)}, u32[]{:S(2)}) collective-permute-start(bf16[6,128,512]{2,1,0:T(8,128)(2,1)S(1)} %get-tuple-element.20.tiled), channel_id=1, source_target_pairs={{0,1},{1,0},{2,3},{3,2},{4,5},{5,4},{6,7},{7,6},{8,9},{9,8},{10,11... | collective-permute-start | bytes 2359304 | tf_op jit(solution)/shard_map/ppermute | solution.py:324
  3.1 23.4 %collective-permute-start.2 = (bf16[4,128,512]{2,1,0:T(8,128)(2,1)S(1)}, bf16[4,128,512]{2,1,0:T(8,128)(2,1)S(1)}, u32[]{:S(2)}, u32[]{:S(2)}) collective-permute-start(bf16[4,128,512]{2,1,0:T(8,128)(2,1)S(1)} %get-tuple-element.23), channel_id=1, source_target_pairs={{1,2},{3,4},{5,6},{7,8},{9,10},{11,12},{13,14},{2,1},{4,3},{6,5},{... | collective-permute-start | bytes 1572872 | tf_op jit(solution)/shard_map/ppermute | solution.py:322
  6.1 27.1 %collective-permute-start = (bf16[2,128,512]{2,1,0:T(8,128)(2,1)S(1)}, bf16[2,128,512]{2,1,0:T(8,128)(2,1)S(1)}, u32[]{:S(2)}, u32[]{:S(2)}) collective-permute-start(bf16[2,128,512]{2,1,0:T(8,128)(2,1)S(1)} %get-tuple-element.18), channel_id=1, source_target_pairs={{1,2},{3,4},{5,6},{7,8},{9,10},{11,12},{13,14},{2,1},{4,3},{6,5},{... | collective-permute-start | bytes 786440 | tf_op jit(solution)/shard_map/ppermute | solution.py:323

commit v2 on v1

--- a/solution.py
+++ b/solution.py
@@ -104,36 +104,48 @@
             items[0, start + u] = i
         pairs = start + ((found + 1) >> 1)
         ends.append(pairs)
+    items[0, pairs] = 0
+    for u in range(2):
+        items[1, 2 * pairs + u] = 0
     return pairs, ends
 
 
-def attend(items, low, high, keys, vals, qt, top, acc):
+def attend(items, high, keys, vals, qt, top, acc, scores, peaks):
     groups, depth, lanes = qt.shape[1:]
     hd, p = depth // 2, lanes // 2
 
+    def score(t, g):
+        i, k0, k1 = items[0, t], items[1, 2 * t], items[1, 2 * t + 1]
+        rows = slice(g * depth, (g + 1) * depth)
+        cols = slice(g * lanes, (g + 1) * lanes)
+        s0 = nn(keys[k0, :, rows], qt[i, g])
+        s1 = nn(keys[k1, :, rows], qt[i, g])
+        scores[:p, cols] = s0
+        scores[p:, cols] = s1
+        peaks[:, cols] = jnp.max(jnp.maximum(s0, s1), axis=0, keepdims=True)
+
+    def weigh(t, g):
+        i, v0, v1 = items[0, t], items[2, 2 * t], items[2, 2 * t + 1]
+        cols = slice(g * lanes, (g + 1) * lanes)
+        old = top[i, :, cols]
+        new = jnp.maximum(old, peaks[:, cols])
+        probs = jnp.exp(scores[:, cols] - new).astype(BF16)
+        fade = jnp.exp(old - new)
+        out = nn(jnp.concatenate([vals[v0, g], vals[v1, g]], axis=1), probs)
+        both = jnp.concatenate([out[:hd, :p], out[hd:depth, p:]], axis=1)
+        top[i, :, cols] = new
+        acc[i, :hd, cols] = acc[i, :hd, cols] * fade + both
+        acc[i, hd:, cols] = acc[i, hd:, cols] * fade + out[depth : depth + 8]
+
     def step(t, carry):
-        i = items[0, t]
-        k0, k1 = items[1, 2 * t], items[1, 2 * t + 1]
-        v0, v1 = items[2, 2 * t], items[2, 2 * t + 1]
         for g in range(groups):
-            rows = slice(g * depth, (g + 1) * depth)
-            cols = slice(g * lanes, (g + 1) * lanes)
-            s0 = nn(keys[k0, :, rows], qt[i, g])
-            s1 = nn(keys[k1, :, rows], qt[i, g])
-            old = top[i, :, cols]
-            new = jnp.maximum(old, jnp.max(jnp.maximum(s0, s1), axis=0, keepdims=True))
-            probs = jnp.concatenate(
-                [jnp.exp(s0 - new).astype(BF16), jnp.exp(s1 - new).astype(BF16)], axis=0
-            )
-            fade = jnp.exp(old - new)
-            out = nn(jnp.concatenate([vals[v0, g], vals[v1, g]], axis=1), probs)
-            both = jnp.concatenate([out[:hd, :p], out[hd:depth, p:]], axis=1)
-            top[i, :, cols] = new
-            acc[i, :hd, cols] = acc[i, :hd, cols] * fade + both
-            acc[i, hd:, cols] = acc[i, hd:, cols] * fade + out[depth : depth + 8]
+            weigh(t, g)
+            score(t + 1, g)
         return carry
 
-    lax.fori_loop(low, high, step, 0)
+    for g in range(groups):
+        score(0, g)
+    lax.fori_loop(0, high, step, 0)
 
 
 def put_values(vals, tile, v, live):
@@ -159,7 +171,7 @@
 
 def main_kernel(
     n, tiled, near, norm, masks, counts, w_qkv, w_out, qt, top, acc, w_all, w_last, keys, vals, flags, live,
-    items, sems
+    items, scores, peaks, sems
 ):
     by, p, width = tiled.shape
     groups, depth = qt.shape[1:3]
@@ -213,11 +225,11 @@
             rows = slice(u * p, (u + 1) * p)
             keys[by + i] = k[rows]
             put_values(vals, by + i, v[rows], place < live[i, 0, slab])
-    attend(items, 0, pairs, keys, vals, qt, top, acc)
+    attend(items, pairs, keys, vals, qt, top, acc, scores, peaks)
     copies[3].wait()
 
 
-def far_work(n, j0, by, rim, norm, masks, counts, w_all, qt, top, acc, keys, vals, flags, live, items, sems):
+def far_work(n, j0, by, rim, norm, masks, counts, w_all, qt, top, acc, keys, vals, flags, live, items, scores, peaks, sems):
     blocks, p, width = rim.shape
     copies = [
         pltpu.make_async_copy(masks, flags, sems.at[0]),
@@ -244,7 +256,7 @@
             rows = slice(u * p, (u + 1) * p)
             keys[j] = k[rows]
             put_values(vals, j, v[rows], place < live[j0 + j, 0, slab])
-    attend(items, 0, pairs, keys, vals, qt, top, acc)
+    attend(items, pairs, keys, vals, qt, top, acc, scores, peaks)
 
 
 def hand_out(blocks, tiled, acc, w_out, live, result, out, sems):
@@ -260,19 +272,19 @@
 
 def far_kernel(
     n, j0, done, rim, norm, masks, counts, w_all, qt, top_in, acc_in, tiled, w_out, top, acc, result, keys, vals,
-    flags, live, items, out, sems
+    flags, live, items, scores, peaks, out, sems
 ):
     by = tiled.shape[0]
-    far_work(n, j0, by, rim, norm, masks, counts, w_all, qt, top, acc, keys, vals, flags, live, items, sems)
+    far_work(n, j0, by, rim, norm, masks, counts, w_all, qt, top, acc, keys, vals, flags, live, items, scores, peaks, sems)
     hand_out(done, tiled, acc, w_out, live, result, out, sems)
 
 
 def last_kernel(
     n, j0, done, rim, norm, masks, counts, w_all, qt, top_in, acc_in, tiled, w_out, result_in, top, acc, result,
-    keys, vals, flags, live, items, out, sems
+    keys, vals, flags, live, items, scores, peaks, out, sems
 ):
     by = tiled.shape[0]
-    far_work(n, j0, by, rim, norm, masks, counts, w_all, qt, top, acc, keys, vals, flags, live, items, sems)
+    far_work(n, j0, by, rim, norm, masks, counts, w_all, qt, top, acc, keys, vals, flags, live, items, scores, peaks, sems)
     hand_out(done, tiled, acc, w_out, live, result, out, sems)
 
 
@@ -335,6 +347,8 @@
             flags,
             live,
             pltpu.SMEM((3, 8 * by), jnp.int32),
+            pltpu.VMEM((2 * p, groups * lanes), F32),
+            pltpu.VMEM((1, groups * lanes), F32),
         ]
 
     qt, top, acc, w_all, w_last = pl.pallas_call(

time: 39 us -> 30.6 us (0.78)
  the two profiles are of different devices: /device:TPU:23 before, /device:TPU:27 now
where the time goes in v2:
time: 30.6 us; the launch traced here: 30.1 us
  Pallas kernels  18.5 us (60%)
  starting transfers between devices  6.29 us (21%)
  waiting for transfers between devices  5.31 us (17%)
    pallas_call x2, Pallas kernels, far(): pl.pallas_call(functools.partial(kernel, n, j0, done), out_shape=(*state,...  8.12 us
    pallas_call x1, Pallas kernels, shards(): pl.pallas_call(functools.partial(main_kernel, n), out_shape=(pltpu.VMEM((...  8.03 us
    ppermute x1, waiting for transfers between devices, shards(): far0 = lax.ppermute(first, 'gx', far_pairs)  5.3 us
    ppermute x1, starting transfers between devices, shards(): far0 = lax.ppermute(first, 'gx', far_pairs)  3.05 us
    ppermute x1, starting transfers between devices, shards(): far1 = lax.ppermute(second, 'gx', far_pairs)  2.5 us
    pallas_call x1, Pallas kernels, shards(): pl.pallas_call(functools.partial(gather_kernel, split), out_shape=(pltpu....  2.31 us
    ppermute x1, starting transfers between devices, shards(): near = lax.ppermute(tiled, 'gx', near_pairs)  0.74 us
  transfers between devices with their start and end apart: 3, of which 1 were waited for; matrix products, arithmetic and copies ran while one was open for 0% of the time, Pallas kernels for 43%

profile of v2, /device:TPU:27, one launch (start us, length us, event | category | flops | bytes accessed | tf_op | source)
XLA Modules:
  0.0 30.1 jit_solution(8421251860583343690)
XLA Ops:
  0.0 2.3 %gather.1 = (bf16[6,128,512]{2,1,0:T(8,128)(2,1)S(1)}, bf16[4,128,512]{2,1,0:T(8,128)(2,1)S(1)}, bf16[2,128,512]{2,1,0:T(8,128)(2,1)S(1)}, f32[2,512]{1,0:T(2,128)S(1)}) custom-call(bf16[1,6,1,128,512]{4,3,2,1,0:T(8,128)(2,1)} %points.1, s32[1,6,1,128]{3,2,1,0:T(1,128)} %order.1, s32[6,1,16]{2,1,0:T(1,128)} %bitcast.3, f32[1,512]{1,0:T(1,128)} %bitcast.7, ...), custom_call_target="tpu_custom_call" | custom-call | tf_op jit(solution)/shard_map/gather/pallas_call | solution.py:313
  2.3 0.7 %collective-permute-start.1 = (bf16[6,128,512]{2,1,0:T(8,128)(2,1)S(1)}, bf16[6,128,512]{2,1,0:T(8,128)(2,1)S(1)}, u32[]{:S(2)}, u32[]{:S(2)}) collective-permute-start(bf16[6,128,512]{2,1,0:T(8,128)(2,1)S(1)} %get-tuple-element.20.tiled), channel_id=1, source_target_pairs={{0,1},{1,0},{2,3},{3,2},{4,5},{5,4},{6,7},{7,6},{8,9},{9,8},{10,11... | collective-permute-start | bytes 2359304 | tf_op jit(solution)/shard_map/ppermute | solution.py:336
  3.1 3.1 %collective-permute-start.2 = (bf16[4,128,512]{2,1,0:T(8,128)(2,1)S(1)}, bf16[4,128,512]{2,1,0:T(8,128)(2,1)S(1)}, u32[]{:S(2)}, u32[]{:S(2)}) collective-permute-start(bf16[4,128,512]{2,1,0:T(8,128)(2,1)S(1)} %get-tuple-element.23), channel_id=1, source_target_pairs={{1,2},{3,4},{5,6},{7,8},{9,10},{11,12},{13,14},{2,1},{4,3},{6,5},{... | collective-permute-start | bytes 1572872 | tf_op jit(solution)/shard_map/ppermute | solution.py:334
  6.1 2.5 %collective-permute-start = (bf16[2,128,512]{2,1,0:T(8,128)(2,1)S(1)}, bf16[2,128,512]{2,1,0:T(8,128)(2,1)S(1)}, u32[]{:S(2)}, u32[]{:S(2)}) collective-permute-start(bf16[2,128,512]{2,1,0:T(8,128)(2,1)S(1)} %get-tuple-element.18), channel_id=1, source_target_pairs={{1,2},{3,4},{5,6},{7,8},{9,10},{11,12},{13,14},{2,1},{4,3},{6,5},{... | collective-permute-start | bytes 786440 | tf_op jit(solution)/shard_map/ppermute | solution.py:335
  8.6 0.0 collective-permute-done.1.near
  8.6 8.0 %main.1 = (bf16[6,4,128,256]{3,2,1,0:T(8,128)(2,1)S(1)}, f32[6,1,1024]{2,1,0:T(1,128)S(1)}, f32[6,72,1024]{2,1,0:T(8,128)S(1)}, bf16[512,1536]{1,0:T(8,128)(2,1)S(1)}, bf16[512,512]{1,0:T(8,128)(2,1)S(1)}) custom-call(bf16[6,128,512]{2,1,0:T(8,128)(2,1)S(1)} %get-tuple-element.20.tiled, bf16[6,128,512]{2,1,0:T(8,128)(2,1)S(1)} %collective-permute-done.1.near, ...), custom_call_target="tpu_custom_call" | custom-call | tf_op jit(solution)/shard_map/main/pallas_call | solution.py:354
  16.7 5.3 %collective-permute-done.2.rim = bf16[4,128,512]{2,1,0:T(8,128)(2,1)S(1)} collective-permute-done((bf16[4,128,512]{2,1,0:T(8,128)(2,1)S(1)}, bf16[4,128,512]{2,1,0:T(8,128)(2,1)S(1)}, u32[]{:S(2)}, u32[]{:S(2)}) %collective-permute-start.2) | collective-permute-done | bytes 524320 | tf_op jit(solution)/shard_map/ppermute | solution.py:334
  22.0 5.0 %far.1 = (f32[6,1,1024]{2,1,0:T(1,128)S(1)}, f32[6,72,1024]{2,1,0:T(8,128)S(1)}, bf16[1,6,1,128,512]{4,3,2,1,0:T(8,128)(2,1)}) custom-call(bf16[4,128,512]{2,1,0:T(8,128)(2,1)S(1)} %collective-permute-done.2.rim, f32[2,512]{1,0:T(2,128)S(1)} %get-tuple-element.19.norm, s32[1,6,1,26]{3,2,1,0:T(1,128)} %masks.5, ...), custom_call_target="tpu_custom_call", output_to_operand_aliasing={{0}: (6, {}), {1}: (7, {})} | custom-call | tf_op jit(solution)/shard_map/far/pallas_call | solution.py:373
  27.0 0.0 collective-permute-done.rim
  27.0 3.1 %last.1 = (f32[6,1,1024]{2,1,0:T(1,128)S(1)}, f32[6,72,1024]{2,1,0:T(8,128)S(1)}, bf16[1,6,1,128,512]{4,3,2,1,0:T(8,128)(2,1)}) custom-call(bf16[2,128,512]{2,1,0:T(8,128)(2,1)S(1)} %collective-permute-done.rim, f32[2,512]{1,0:T(2,128)S(1)} %get-tuple-element.19.norm, ...), custom_call_target="tpu_custom_call", output_to_operand_aliasing={{0}: (6, {}), {1}: (7, {}), {2}: (10, {})} | custom-call | tf_op jit(solution)/shard_map/last/pallas_call | solution.py:373
Async XLA Ops:
  2.3 6.3 %collective-permute-start.1 = (bf16[6,128,512]{2,1,0:T(8,128)(2,1)S(1)}, bf16[6,128,512]{2,1,0:T(8,128)(2,1)S(1)}, u32[]{:S(2)}, u32[]{:S(2)}) collective-permute-start(bf16[6,128,512]{2,1,0:T(8,128)(2,1)S(1)} %get-tuple-element.20.tiled), channel_id=1, source_target_pairs={{0,1},{1,0},{2,3},{3,2},{4,5},{5,4},{6,7},{7,6},{8,9},{9,8},{10,11... | collective-permute-start | bytes 2359304 | tf_op jit(solution)/shard_map/ppermute | solution.py:336
  3.1 18.9 %collective-permute-start.2 = (bf16[4,128,512]{2,1,0:T(8,128)(2,1)S(1)}, bf16[4,128,512]{2,1,0:T(8,128)(2,1)S(1)}, u32[]{:S(2)}, u32[]{:S(2)}) collective-permute-start(bf16[4,128,512]{2,1,0:T(8,128)(2,1)S(1)} %get-tuple-element.23), channel_id=1, source_target_pairs={{1,2},{3,4},{5,6},{7,8},{9,10},{11,12},{13,14},{2,1},{4,3},{6,5},{... | collective-permute-start | bytes 1572872 | tf_op jit(solution)/shard_map/ppermute | solution.py:334
  6.1 20.9 %collective-permute-start = (bf16[2,128,512]{2,1,0:T(8,128)(2,1)S(1)}, bf16[2,128,512]{2,1,0:T(8,128)(2,1)S(1)}, u32[]{:S(2)}, u32[]{:S(2)}) collective-permute-start(bf16[2,128,512]{2,1,0:T(8,128)(2,1)S(1)} %get-tuple-element.18), channel_id=1, source_target_pairs={{1,2},{3,4},{5,6},{7,8},{9,10},{11,12},{13,14},{2,1},{4,3},{6,5},{... | collective-permute-start | bytes 786440 | tf_op jit(solution)/shard_map/ppermute | solution.py:335

commit v3 on v2

--- a/solution.py
+++ b/solution.py
@@ -7,6 +7,7 @@
 from jax.experimental.pallas import tpu as pltpu
 from jax.sharding import PartitionSpec as P
 
+
 HEADS = 8
 NEG = -1e30
 ONES = 16
@@ -32,7 +33,7 @@
 def gather_kernel(
     split, points, order, counts, gain, shift, tiled, first, second, norm, raw, rows, live, sems
 ):
-    _, by, _, p, width = points.shape
+    _, by, _, p, _ = points.shape
     me = lax.axis_index("gx")
     small = [
         pltpu.make_async_copy(order, rows, sems.at[by]),
@@ -170,8 +171,8 @@
 
 
 def main_kernel(
-    n, tiled, near, norm, masks, counts, w_qkv, w_out, qt, top, acc, w_all, w_last, keys, vals, flags, live,
-    items, scores, peaks, sems
+    n, split, tiled, near, norm, masks, counts, w_qkv, w_out, qt, top, acc, w_all, w_last, plan0, plan1, keys, vals,
+    items, flags, live, scores, peaks, sems
 ):
     by, p, width = tiled.shape
     groups, depth = qt.shape[1:3]
@@ -199,6 +200,15 @@
     pairs, _ = list_pairs(
         items, flags, by, [(0, None, 0, by, 0, True), (side, exists, 0, by, by, False)]
     )
+    other = me - side
+    there = (other >= 0) & (other < n)
+    beyond = jnp.clip(other, 0, n - 1)
+    for plan, j0, j1 in ((plan0, 0, split), (plan1, split, by)):
+        plan[3, 0], _ = list_pairs(plan, flags, by, [(-side, there, j0, j1, 0, False)])
+        for i in range(by):
+            plan[3, 1 + i] = live[i, 0, me]
+        for j in range(j0, j1):
+            plan[3, 1 + by + j - j0] = live[j, 0, beyond]
     zeros = jnp.zeros((hd, p), BF16)
     copies[2].wait()
     for c in range(0, by, 2):
@@ -229,24 +239,12 @@
     copies[3].wait()
 
 
-def far_work(n, j0, by, rim, norm, masks, counts, w_all, qt, top, acc, keys, vals, flags, live, items, scores, peaks, sems):
+def far_work(rim, norm, w_all, qt, plan, top, acc, keys, vals, scores, peaks):
+    by = qt.shape[0]
     blocks, p, width = rim.shape
-    copies = [
-        pltpu.make_async_copy(masks, flags, sems.at[0]),
-        pltpu.make_async_copy(counts, live, sems.at[1]),
-    ]
-    for copy in copies:
-        copy.start()
-    side = -toward_near()
-    other = lax.axis_index("gx") + side
-    exists = (other >= 0) & (other < n)
-    slab = jnp.clip(other, 0, n - 1)
     place = lax.broadcasted_iota(jnp.int32, (1, p), 1)
     gain, shift = norm[0:1], norm[1:2]
     vals[blocks] = jnp.zeros(vals.shape[1:], BF16)
-    copies[0].wait()
-    copies[1].wait()
-    pairs, _ = list_pairs(items, flags, by, [(side, exists, j0, j0 + blocks, 0, False)])
     for c in range(0, blocks, 2):
         span = range(c, min(c + 2, blocks))
         x = jnp.concatenate([normalise(rim[j], gain, shift) for j in span], axis=0)
@@ -255,41 +253,42 @@
         for u, j in enumerate(span):
             rows = slice(u * p, (u + 1) * p)
             keys[j] = k[rows]
-            put_values(vals, j, v[rows], place < live[j0 + j, 0, slab])
-    attend(items, pairs, keys, vals, qt, top, acc, scores, peaks)
-
-
-def hand_out(blocks, tiled, acc, w_out, live, result, out, sems):
-    me = lax.axis_index("gx")
+            put_values(vals, j, v[rows], place < plan[3, 1 + by + j])
+    attend(plan, plan[3, 0], keys, vals, qt, top, acc, scores, peaks)
+
+
+def hand_out(blocks, tiled, acc, w_out, plan, result, out, sems):
     copies = []
     for u, i in enumerate(blocks):
-        out[u] = finish(i, tiled, acc, w_out, live[i, 0, me])
-        copies.append(pltpu.make_async_copy(out.at[u], result.at[0, i, 0], sems.at[2 + u]))
+        out[u] = finish(i, tiled, acc, w_out, plan[3, 1 + i])
+        copies.append(pltpu.make_async_copy(out.at[u], result.at[0, i, 0], sems.at[u]))
         copies[-1].start()
     for copy in copies:
         copy.wait()
 
 
 def far_kernel(
-    n, j0, done, rim, norm, masks, counts, w_all, qt, top_in, acc_in, tiled, w_out, top, acc, result, keys, vals,
-    flags, live, items, scores, peaks, out, sems
+    done, rim, norm, w_all, qt, top_in, acc_in, tiled, w_out, plan, top, acc, result, keys, vals, scores, peaks, out,
+    sems
 ):
-    by = tiled.shape[0]
-    far_work(n, j0, by, rim, norm, masks, counts, w_all, qt, top, acc, keys, vals, flags, live, items, scores, peaks, sems)
-    hand_out(done, tiled, acc, w_out, live, result, out, sems)
+    far_work(rim, norm, w_all, qt, plan, top, acc, keys, vals, scores, peaks)
+    hand_out(done, tiled, acc, w_out, plan, result, out, sems)
 
 
 def last_kernel(
-    n, j0, done, rim, norm, masks, counts, w_all, qt, top_in, acc_in, tiled, w_out, result_in, top, acc, result,
-    keys, vals, flags, live, items, scores, peaks, out, sems
+    done, rim, norm, w_all, qt, top_in, acc_in, tiled, w_out, plan, result_in, top, acc, result, keys, vals, scores,
+    peaks, out, sems
 ):
-    by = tiled.shape[0]
-    far_work(n, j0, by, rim, norm, masks, counts, w_all, qt, top, acc, keys, vals, flags, live, items, scores, peaks, sems)
-    hand_out(done, tiled, acc, w_out, live, result, out, sems)
+    far_work(rim, norm, w_all, qt, plan, top, acc, keys, vals, scores, peaks)
+    hand_out(done, tiled, acc, w_out, plan, result, out, sems)
 
 
 def vmem(x):
     return pltpu.with_memory_space_constraint(x, pltpu.VMEM)
+
+
+def smem(x):
+    return pltpu.with_memory_space_constraint(x, pltpu.SMEM)
 
 
 def hbm(x):
@@ -304,6 +303,8 @@
     early = max(split - 1, 0)
     whole = pl.BlockSpec(memory_space=pltpu.VMEM)
     apart = pl.BlockSpec(memory_space=pltpu.HBM)
+    words = pl.BlockSpec(memory_space=pltpu.SMEM)
+    plan = pltpu.SMEM((4, 8 * by), jnp.int32)
     params = pltpu.CompilerParams(vmem_limit_bytes=LIMIT)
     points, order, masks, w_qkv, w_out = map(hbm, (points, order, masks, w_qkv, w_out))
     counts = hbm(jnp.transpose(counts, (1, 2, 0)))
@@ -331,9 +332,13 @@
     )(points, order, counts, hbm(gain[None]), hbm(shift_bias[None]))
     near_pairs = [(i, i ^ 1) for i in range(n) if i ^ 1 < n]
     far_pairs = [(i, i + 1) for i in range(1, n - 1, 2)] + [(i + 1, i) for i in range(1, n - 1, 2)]
-    far0 = lax.ppermute(first, "gx", far_pairs)
-    far1 = lax.ppermute(second, "gx", far_pairs)
-    near = lax.ppermute(tiled, "gx", near_pairs)
+
+    def moved(value, pairs):
+        return lax.ppermute(value, "gx", pairs)
+
+    far0 = moved(first, far_pairs)
+    near = moved(tiled, near_pairs)
+    far1 = moved(second, far_pairs)
 
     state = (
         pltpu.VMEM((by, 1, groups * lanes), F32),
@@ -344,49 +349,48 @@
         return [
             pltpu.VMEM((tiles, p, width), BF16),
             pltpu.VMEM((tiles + 1, groups, depth + ONES, p), BF16),
-            flags,
-            live,
-            pltpu.SMEM((3, 8 * by), jnp.int32),
-            pltpu.VMEM((2 * p, groups * lanes), F32),
-            pltpu.VMEM((1, groups * lanes), F32),
         ]
 
-    qt, top, acc, w_all, w_last = pl.pallas_call(
-        functools.partial(main_kernel, n),
+    ahead = [
+        pltpu.VMEM((2 * p, groups * lanes), F32),
+        pltpu.VMEM((1, groups * lanes), F32),
+    ]
+    qt, top, acc, w_all, w_last, plan0, plan1 = pl.pallas_call(
+        functools.partial(main_kernel, n, split),
         out_shape=(
             pltpu.VMEM((by, groups, depth, lanes), BF16),
             *state,
             pltpu.VMEM(w_qkv.shape, BF16),
             pltpu.VMEM(w_out.shape, BF16),
+            plan,
+            plan,
         ),
         in_specs=[whole, whole, whole, apart, apart, apart, apart],
-        out_specs=(whole,) * 5,
-        scratch_shapes=[*scratch(2 * by), pltpu.SemaphoreType.DMA((4,))],
+        out_specs=(whole,) * 5 + (words,) * 2,
+        scratch_shapes=[*scratch(2 * by), plan, flags, live, *ahead, pltpu.SemaphoreType.DMA((4,))],
         compiler_params=params,
         name="main",
     )(vmem(tiled), vmem(near), vmem(norm), masks, counts, w_qkv, w_out)
 
-    def far(kernel, name, j0, done, block, top, acc, result):
-        ins = [block, norm, masks, counts, w_all, qt, top, acc, tiled, w_last, *result]
-        spaces = [whole, whole, apart, apart, *(whole,) * 6, *(apart,) * len(result)]
-        ins = [vmem(x) if s is whole else x for x, s in zip(ins, spaces)]
+    def far(kernel, done, block, plan, top, acc, result):
+        ins = [block, norm, w_all, qt, top, acc, tiled, w_last]
         return pl.pallas_call(
-            functools.partial(kernel, n, j0, done),
+            functools.partial(kernel, done),
             out_shape=(*state, pltpu.HBM((1, by, bz, p, width), BF16)),
-            in_specs=spaces,
+            in_specs=[*(whole,) * len(ins), words, *(apart,) * len(result)],
             out_specs=(whole, whole, apart),
             scratch_shapes=[
                 *scratch(block.shape[0]),
+                *ahead,
                 pltpu.VMEM((max(len(done), 1), p, width), BF16),
-                pltpu.SemaphoreType.DMA((2 + by,)),
+                pltpu.SemaphoreType.DMA((by,)),
             ],
-            input_output_aliases={6: 0, 7: 1, **({10: 2} if result else {})},
+            input_output_aliases={4: 0, 5: 1, **({9: 2} if result else {})},
             compiler_params=params,
-            name=name,
-        )(*ins)
-
-    top, acc, result = far(far_kernel, "far", 0, range(early), far0, top, acc, ())
-    _, _, result = far(last_kernel, "last", split, range(early, by), far1, top, acc, (result,))
+        )(*map(vmem, ins), smem(plan), *result)
+
+    top, acc, result = far(far_kernel, range(early), far0, plan0, top, acc, ())
+    _, _, result = far(last_kernel, range(early, by), far1, plan1, top, acc, (result,))
     return result
 
 

time: 30.6 us -> 29.1 us (0.951); the launches traced: 30.1 us -> 28.9 us
  Pallas kernels: 18.5 us -> 17.7 us
  waiting for transfers between devices: 5.31 us -> 4.91 us
    pallas_call x3, Pallas kernels: 16.1 us -> 15.4 us  [the longest x1 8.42 us: shards(): pl.pallas_call(functools.partial(main_kernel, n, split), out_shape=(pltpu...]
    ppermute x3, waiting for transfers between devices: 5.31 us -> 4.91 us  [moved(): return lax.ppermute(value, 'gx', pairs)]
  transfers between devices with their start and end apart: 3 -> 3, of which waited for: 1 -> 1; matrix products, arithmetic and copies ran while one was open for 0% -> 0% of each run, Pallas kernels for 43% -> 44%
where the time goes in v3:
time: 29.1 us; the launch traced here: 28.9 us
  Pallas kernels  17.7 us (61%)
  starting transfers between devices  6.29 us (22%)
  waiting for transfers between devices  4.91 us (17%)
    pallas_call x1, Pallas kernels, shards(): pl.pallas_call(functools.partial(main_kernel, n, split), out_shape=(pltpu...  8.42 us
    pallas_call x2, Pallas kernels, far(): pl.pallas_call(functools.partial(kernel, done), out_shape=(*state, pltpu....  6.94 us
    ppermute x3, starting transfers between devices, moved(): return lax.ppermute(value, 'gx', pairs)  6.29 us
    ppermute x3, waiting for transfers between devices, moved(): return lax.ppermute(value, 'gx', pairs)  4.91 us
    pallas_call x1, Pallas kernels, shards(): pl.pallas_call(functools.partial(gather_kernel, split), out_shape=(pltpu....  2.31 us
  transfers between devices with their start and end apart: 3, of which 1 were waited for; matrix products, arithmetic and copies ran while one was open for 0% of the time, Pallas kernels for 44%

profile of v3, /device:TPU:27, one launch (start us, length us, event | category | flops | bytes accessed | tf_op | source)
XLA Modules:
  0.0 28.9 jit_solution(9549085336778828682)
XLA Ops:
  0.0 2.3 %gather.1 = (bf16[6,128,512]{2,1,0:T(8,128)(2,1)S(1)}, bf16[4,128,512]{2,1,0:T(8,128)(2,1)S(1)}, bf16[2,128,512]{2,1,0:T(8,128)(2,1)S(1)}, f32[2,512]{1,0:T(2,128)S(1)}) custom-call(bf16[1,6,1,128,512]{4,3,2,1,0:T(8,128)(2,1)} %points.1, s32[1,6,1,128]{3,2,1,0:T(1,128)} %order.1, s32[6,1,16]{2,1,0:T(1,128)} %bitcast.3, f32[1,512]{1,0:T(1,128)} %bitcast.5, ...), custom_call_target="tpu_custom_call" | custom-call | tf_op jit(solution)/shard_map/gather/pallas_call | solution.py:314
  2.3 0.7 %collective-permute-start.1 = (bf16[6,128,512]{2,1,0:T(8,128)(2,1)S(1)}, bf16[6,128,512]{2,1,0:T(8,128)(2,1)S(1)}, u32[]{:S(2)}, u32[]{:S(2)}) collective-permute-start(bf16[6,128,512]{2,1,0:T(8,128)(2,1)S(1)} %get-tuple-element.22.tiled), channel_id=1, source_target_pairs={{0,1},{1,0},{2,3},{3,2},{4,5},{5,4},{6,7},{7,6},{8,9},{9,8},{10,11... | collective-permute-start | bytes 2359304 | tf_op jit(solution)/shard_map/ppermute | solution.py:337
  3.1 3.1 %collective-permute-start.2 = (bf16[4,128,512]{2,1,0:T(8,128)(2,1)S(1)}, bf16[4,128,512]{2,1,0:T(8,128)(2,1)S(1)}, u32[]{:S(2)}, u32[]{:S(2)}) collective-permute-start(bf16[4,128,512]{2,1,0:T(8,128)(2,1)S(1)} %get-tuple-element.25), channel_id=1, source_target_pairs={{1,2},{3,4},{5,6},{7,8},{9,10},{11,12},{13,14},{2,1},{4,3},{6,5},{... | collective-permute-start | bytes 1572872 | tf_op jit(solution)/shard_map/ppermute | solution.py:337
  6.1 2.5 %collective-permute-start = (bf16[2,128,512]{2,1,0:T(8,128)(2,1)S(1)}, bf16[2,128,512]{2,1,0:T(8,128)(2,1)S(1)}, u32[]{:S(2)}, u32[]{:S(2)}) collective-permute-start(bf16[2,128,512]{2,1,0:T(8,128)(2,1)S(1)} %get-tuple-element.20), channel_id=1, source_target_pairs={{1,2},{3,4},{5,6},{7,8},{9,10},{11,12},{13,14},{2,1},{4,3},{6,5},{... | collective-permute-start | bytes 786440 | tf_op jit(solution)/shard_map/ppermute | solution.py:337
  8.6 0.0 collective-permute-done.1.near
  8.6 8.4 %main.1 = (bf16[6,4,128,256]{3,2,1,0:T(8,128)(2,1)S(1)}, f32[6,1,1024]{2,1,0:T(1,128)S(1)}, f32[6,72,1024]{2,1,0:T(8,128)S(1)}, bf16[512,1536]{1,0:T(8,128)(2,1)...) custom-call(bf16[6,128,512]{2,1,0:T(8,128)(2,1)S(1)} %get-tuple-element.22.tiled, ...), custom_call_target="tpu_custom_call" | custom-call | tf_op jit(solution)/shard_map/main/pallas_call | solution.py:358
  17.1 4.9 %collective-permute-done.2.rim = bf16[4,128,512]{2,1,0:T(8,128)(2,1)S(1)} collective-permute-done((bf16[4,128,512]{2,1,0:T(8,128)(2,1)S(1)}, bf16[4,128,512]{2,1,0:T(8,128)(2,1)S(1)}, u32[]{:S(2)}, u32[]{:S(2)}) %collective-permute-start.2) | collective-permute-done | bytes 524320 | tf_op jit(solution)/shard_map/ppermute | solution.py:337
  22.0 4.2 %shard_map.82 = (f32[6,1,1024]{2,1,0:T(1,128)S(1)}, f32[6,72,1024]{2,1,0:T(8,128)S(1)}, bf16[1,6,1,128,512]{4,3,2,1,0:T(8,128)(2,1)}) custom-call(bf16[4,128,512]{2,1,0:T(8,128)(2,1)S(1)} %collective-permute-done.2.rim, f32[2,512]{1,0:T(2,128)S(1)} %get-tuple-element.21.norm, ...), custom_call_target="tpu_custom_call", output_to_operand_aliasing={{0}: (4, {}), {1}: (5, {})} | custom-call | tf_op jit(solution)/shard_map/pallas_call | solution.py:377
  26.2 0.0 collective-permute-done.rim
  26.2 2.7 %shard_map.83 = (f32[6,1,1024]{2,1,0:T(1,128)S(1)}, f32[6,72,1024]{2,1,0:T(8,128)S(1)}, bf16[1,6,1,128,512]{4,3,2,1,0:T(8,128)(2,1)}) custom-call(bf16[2,128,512]{2,1,0:T(8,128)(2,1)S(1)} %collective-permute-done.rim, f32[2,512]{1,0:T(2,128)S(1)} %get-tuple-element.21.norm, ...), custom_call_target="tpu_custom_call", output_to_operand_aliasing={{0}: (4, {}), {1}: (5, {}), {2}: (9, {})} | custom-call | tf_op jit(solution)/shard_map/pallas_call | solution.py:377
Async XLA Ops:
  2.3 6.3 %collective-permute-start.1 = (bf16[6,128,512]{2,1,0:T(8,128)(2,1)S(1)}, bf16[6,128,512]{2,1,0:T(8,128)(2,1)S(1)}, u32[]{:S(2)}, u32[]{:S(2)}) collective-permute-start(bf16[6,128,512]{2,1,0:T(8,128)(2,1)S(1)} %get-tuple-element.22.tiled), channel_id=1, source_target_pairs={{0,1},{1,0},{2,3},{3,2},{4,5},{5,4},{6,7},{7,6},{8,9},{9,8},{10,11... | collective-permute-start | bytes 2359304 | tf_op jit(solution)/shard_map/ppermute | solution.py:337
  3.1 18.9 %collective-permute-start.2 = (bf16[4,128,512]{2,1,0:T(8,128)(2,1)S(1)}, bf16[4,128,512]{2,1,0:T(8,128)(2,1)S(1)}, u32[]{:S(2)}, u32[]{:S(2)}) collective-permute-start(bf16[4,128,512]{2,1,0:T(8,128)(2,1)S(1)} %get-tuple-element.25), channel_id=1, source_target_pairs={{1,2},{3,4},{5,6},{7,8},{9,10},{11,12},{13,14},{2,1},{4,3},{6,5},{... | collective-permute-start | bytes 1572872 | tf_op jit(solution)/shard_map/ppermute | solution.py:337
  6.1 20.1 %collective-permute-start = (bf16[2,128,512]{2,1,0:T(8,128)(2,1)S(1)}, bf16[2,128,512]{2,1,0:T(8,128)(2,1)S(1)}, u32[]{:S(2)}, u32[]{:S(2)}) collective-permute-start(bf16[2,128,512]{2,1,0:T(8,128)(2,1)S(1)} %get-tuple-element.20), channel_id=1, source_target_pairs={{1,2},{3,4},{5,6},{7,8},{9,10},{11,12},{13,14},{2,1},{4,3},{6,5},{... | collective-permute-start | bytes 786440 | tf_op jit(solution)/shard_map/ppermute | solution.py:337

commit v4 on v3

--- a/solution.py
+++ b/solution.py
@@ -355,7 +355,7 @@
         pltpu.VMEM((2 * p, groups * lanes), F32),
         pltpu.VMEM((1, groups * lanes), F32),
     ]
-    qt, top, acc, w_all, w_last, plan0, plan1 = pl.pallas_call(
+    main = pl.pallas_call(
         functools.partial(main_kernel, n, split),
         out_shape=(
             pltpu.VMEM((by, groups, depth, lanes), BF16),
@@ -370,7 +370,8 @@
         scratch_shapes=[*scratch(2 * by), plan, flags, live, *ahead, pltpu.SemaphoreType.DMA((4,))],
         compiler_params=params,
         name="main",
-    )(vmem(tiled), vmem(near), vmem(norm), masks, counts, w_qkv, w_out)
+    )
+    qt, top, acc, w_all, w_last, plan0, plan1 = main(vmem(tiled), vmem(near), vmem(norm), masks, counts, w_qkv, w_out)
 
     def far(kernel, done, block, plan, top, acc, result):
         ins = [block, norm, w_all, qt, top, acc, tiled, w_last]

time: 29.1 us -> 29.1 us (level)
  no operation moved by 1% of the time
where the time goes in v4:
time: 29.1 us; the launch traced here: 28.9 us
  Pallas kernels  17.7 us (61%)
  starting transfers between devices  6.29 us (22%)
  waiting for transfers between devices  4.91 us (17%)
    pallas_call x1, Pallas kernels, shards(): main(vmem(tiled), vmem(near), vmem(norm), masks, counts, w_qkv, w_out)  8.42 us
    pallas_call x2, Pallas kernels, far(): pl.pallas_call(functools.partial(kernel, done), out_shape=(*state, pltpu....  6.94 us
    ppermute x3, starting transfers between devices, moved(): return lax.ppermute(value, 'gx', pairs)  6.29 us
    ppermute x3, waiting for transfers between devices, moved(): return lax.ppermute(value, 'gx', pairs)  4.91 us
    pallas_call x1, Pallas kernels, shards(): pl.pallas_call(functools.partial(gather_kernel, split), out_shape=(pltpu....  2.31 us
  transfers between devices with their start and end apart: 3, of which 1 were waited for; matrix products, arithmetic and copies ran while one was open for 0% of the time, Pallas kernels for 44%

profile of v4, /device:TPU:27, one launch (start us, length us, event | category | flops | bytes accessed | tf_op | source)
XLA Modules:
  0.0 28.9 jit_solution(9549085336778828682)
XLA Ops:
  0.0 2.3 %gather.1 = (bf16[6,128,512]{2,1,0:T(8,128)(2,1)S(1)}, bf16[4,128,512]{2,1,0:T(8,128)(2,1)S(1)}, bf16[2,128,512]{2,1,0:T(8,128)(2,1)S(1)}, f32[2,512]{1,0:T(2,128)S(1)}) custom-call(bf16[1,6,1,128,512]{4,3,2,1,0:T(8,128)(2,1)} %points.1, s32[1,6,1,128]{3,2,1,0:T(1,128)} %order.1, s32[6,1,16]{2,1,0:T(1,128)} %bitcast.3, f32[1,512]{1,0:T(1,128)} %bitcast.5, ...), custom_call_target="tpu_custom_call" | custom-call | tf_op jit(solution)/shard_map/gather/pallas_call | solution.py:314
  2.3 0.7 %collective-permute-start.1 = (bf16[6,128,512]{2,1,0:T(8,128)(2,1)S(1)}, bf16[6,128,512]{2,1,0:T(8,128)(2,1)S(1)}, u32[]{:S(2)}, u32[]{:S(2)}) collective-permute-start(bf16[6,128,512]{2,1,0:T(8,128)(2,1)S(1)} %get-tuple-element.22.tiled), channel_id=1, source_target_pairs={{0,1},{1,0},{2,3},{3,2},{4,5},{5,4},{6,7},{7,6},{8,9},{9,8},{10,11... | collective-permute-start | bytes 2359304 | tf_op jit(solution)/shard_map/ppermute | solution.py:337
  3.1 3.1 %collective-permute-start.2 = (bf16[4,128,512]{2,1,0:T(8,128)(2,1)S(1)}, bf16[4,128,512]{2,1,0:T(8,128)(2,1)S(1)}, u32[]{:S(2)}, u32[]{:S(2)}) collective-permute-start(bf16[4,128,512]{2,1,0:T(8,128)(2,1)S(1)} %get-tuple-element.25), channel_id=1, source_target_pairs={{1,2},{3,4},{5,6},{7,8},{9,10},{11,12},{13,14},{2,1},{4,3},{6,5},{... | collective-permute-start | bytes 1572872 | tf_op jit(solution)/shard_map/ppermute | solution.py:337
  6.1 2.5 %collective-permute-start = (bf16[2,128,512]{2,1,0:T(8,128)(2,1)S(1)}, bf16[2,128,512]{2,1,0:T(8,128)(2,1)S(1)}, u32[]{:S(2)}, u32[]{:S(2)}) collective-permute-start(bf16[2,128,512]{2,1,0:T(8,128)(2,1)S(1)} %get-tuple-element.20), channel_id=1, source_target_pairs={{1,2},{3,4},{5,6},{7,8},{9,10},{11,12},{13,14},{2,1},{4,3},{6,5},{... | collective-permute-start | bytes 786440 | tf_op jit(solution)/shard_map/ppermute | solution.py:337
  8.6 0.0 collective-permute-done.1.near
  8.6 8.4 %main.1 = (bf16[6,4,128,256]{3,2,1,0:T(8,128)(2,1)S(1)}, f32[6,1,1024]{2,1,0:T(1,128)S(1)}, f32[6,72,1024]{2,1,0:T(8,128)S(1)}, bf16[512,1536]{1,0:T(8,128)(2,1)...) custom-call(bf16[6,128,512]{2,1,0:T(8,128)(2,1)S(1)} %get-tuple-element.22.tiled, ...), custom_call_target="tpu_custom_call" | custom-call | tf_op jit(solution)/shard_map/main/pallas_call | solution.py:374
  17.1 4.9 %collective-permute-done.2.rim = bf16[4,128,512]{2,1,0:T(8,128)(2,1)S(1)} collective-permute-done((bf16[4,128,512]{2,1,0:T(8,128)(2,1)S(1)}, bf16[4,128,512]{2,1,0:T(8,128)(2,1)S(1)}, u32[]{:S(2)}, u32[]{:S(2)}) %collective-permute-start.2) | collective-permute-done | bytes 524320 | tf_op jit(solution)/shard_map/ppermute | solution.py:337
  22.0 4.2 %shard_map.82 = (f32[6,1,1024]{2,1,0:T(1,128)S(1)}, f32[6,72,1024]{2,1,0:T(8,128)S(1)}, bf16[1,6,1,128,512]{4,3,2,1,0:T(8,128)(2,1)}) custom-call(bf16[4,128,512]{2,1,0:T(8,128)(2,1)S(1)} %collective-permute-done.2.rim, f32[2,512]{1,0:T(2,128)S(1)} %get-tuple-element.21.norm, ...), custom_call_target="tpu_custom_call", output_to_operand_aliasing={{0}: (4, {}), {1}: (5, {})} | custom-call | tf_op jit(solution)/shard_map/pallas_call | solution.py:378
  26.2 0.0 collective-permute-done.rim
  26.2 2.7 %shard_map.83 = (f32[6,1,1024]{2,1,0:T(1,128)S(1)}, f32[6,72,1024]{2,1,0:T(8,128)S(1)}, bf16[1,6,1,128,512]{4,3,2,1,0:T(8,128)(2,1)}) custom-call(bf16[2,128,512]{2,1,0:T(8,128)(2,1)S(1)} %collective-permute-done.rim, f32[2,512]{1,0:T(2,128)S(1)} %get-tuple-element.21.norm, ...), custom_call_target="tpu_custom_call", output_to_operand_aliasing={{0}: (4, {}), {1}: (5, {}), {2}: (9, {})} | custom-call | tf_op jit(solution)/shard_map/pallas_call | solution.py:378
Async XLA Ops:
  2.3 6.3 %collective-permute-start.1 = (bf16[6,128,512]{2,1,0:T(8,128)(2,1)S(1)}, bf16[6,128,512]{2,1,0:T(8,128)(2,1)S(1)}, u32[]{:S(2)}, u32[]{:S(2)}) collective-permute-start(bf16[6,128,512]{2,1,0:T(8,128)(2,1)S(1)} %get-tuple-element.22.tiled), channel_id=1, source_target_pairs={{0,1},{1,0},{2,3},{3,2},{4,5},{5,4},{6,7},{7,6},{8,9},{9,8},{10,11... | collective-permute-start | bytes 2359304 | tf_op jit(solution)/shard_map/ppermute | solution.py:337
  3.1 18.9 %collective-permute-start.2 = (bf16[4,128,512]{2,1,0:T(8,128)(2,1)S(1)}, bf16[4,128,512]{2,1,0:T(8,128)(2,1)S(1)}, u32[]{:S(2)}, u32[]{:S(2)}) collective-permute-start(bf16[4,128,512]{2,1,0:T(8,128)(2,1)S(1)} %get-tuple-element.25), channel_id=1, source_target_pairs={{1,2},{3,4},{5,6},{7,8},{9,10},{11,12},{13,14},{2,1},{4,3},{6,5},{... | collective-permute-start | bytes 1572872 | tf_op jit(solution)/shard_map/ppermute | solution.py:337
  6.1 20.1 %collective-permute-start = (bf16[2,128,512]{2,1,0:T(8,128)(2,1)S(1)}, bf16[2,128,512]{2,1,0:T(8,128)(2,1)S(1)}, u32[]{:S(2)}, u32[]{:S(2)}) collective-permute-start(bf16[2,128,512]{2,1,0:T(8,128)(2,1)S(1)} %get-tuple-element.20), channel_id=1, source_target_pairs={{1,2},{3,4},{5,6},{7,8},{9,10},{11,12},{13,14},{2,1},{4,3},{6,5},{... | collective-permute-start | bytes 786440 | tf_op jit(solution)/shard_map/ppermute | solution.py:337

commit v5 on v3

--- a/solution.py
+++ b/solution.py
@@ -30,10 +30,15 @@
     return ((values - mean) * lax.rsqrt(var + 1e-05) * gain + shift).astype(BF16)
 
 
-def gather_kernel(
-    split, points, order, counts, gain, shift, tiled, first, second, norm, raw, rows, live, sems
-):
+def select(row, raw):
+    p = raw.shape[0]
+    slot = lax.broadcasted_iota(jnp.int32, (p, p), 0)
+    return tn((slot == row).astype(F32).astype(BF16), raw).astype(BF16)
+
+
+def gather_kernel(points, order, counts, gain, shift, first, rest, places, norm, raw, rows, live, sems):
     _, by, _, p, _ = points.shape
+    split = first.shape[0]
     me = lax.axis_index("gx")
     small = [
         pltpu.make_async_copy(order, rows, sems.at[by]),
@@ -41,28 +46,39 @@
         pltpu.make_async_copy(gain, norm.at[0:1], sems.at[by + 2]),
         pltpu.make_async_copy(shift, norm.at[1:2], sems.at[by + 3]),
     ]
-    large = [pltpu.make_async_copy(points.at[0, j, 0], raw.at[j], sems.at[j]) for j in range(by)]
-    for copy in (*small, *large):
+    large = [
+        pltpu.make_async_copy(
+            points.at[0, j, 0], raw.at[j] if j < split else rest.at[j - split], sems.at[j]
+        )
+        for j in range(by)
+    ]
+    for copy in (*small[:2], *large, *small[2:]):
         copy.start()
-    slot = lax.broadcasted_iota(jnp.int32, (p, p), 0)
     place = lax.broadcasted_iota(jnp.int32, (1, p), 1)
     small[0].wait()
     small[1].wait()
     picks = []
     for j in range(by):
         row = rows[0, j]
-        row = jnp.where(place < live[j, 0, me], row, row[:, :1])
-        picks.append((slot == row).astype(F32).astype(BF16))
-    for j in range(by):
+        picks.append(jnp.where(place < live[j, 0, me], row, row[:, :1]))
+        if j >= split:
+            places[j - split] = picks[j]
+    for j in range(split):
         large[j].wait()
-        got = tn(picks[j], raw[j]).astype(BF16)
-        tiled[j] = got
-        if j < split:
-            first[j] = got
-        else:
-            second[j - split] = got
-    small[2].wait()
-    small[3].wait()
+    for j in range(split):
+        first[j] = select(picks[j], raw[j])
+    for copy in (*large[split:], *small[2:]):
+        copy.wait()
+
+
+def rest_kernel(first, rest, places, tiled, second):
+    split = first.shape[0]
+    for j in range(split):
+        tiled[j] = first[j]
+    for j in range(rest.shape[0]):
+        got = select(places[j], rest[j])
+        second[j] = got
+        tiled[split + j] = got
 
 
 def toward_near():
@@ -132,31 +148,58 @@
         new = jnp.maximum(old, peaks[:, cols])
         probs = jnp.exp(scores[:, cols] - new).astype(BF16)
         fade = jnp.exp(old - new)
-        out = nn(jnp.concatenate([vals[v0, g], vals[v1, g]], axis=1), probs)
-        both = jnp.concatenate([out[:hd, :p], out[hd:depth, p:]], axis=1)
-        top[i, :, cols] = new
-        acc[i, :hd, cols] = acc[i, :hd, cols] * fade + both
-        acc[i, hd:, cols] = acc[i, hd:, cols] * fade + out[depth : depth + 8]
+        both, sums = [], []
+        for h in range(2):
+            rows = slice(h * (hd + ONES), (h + 1) * (hd + ONES))
+            val = jnp.concatenate([vals[v0, g, rows], vals[v1, g, rows]], axis=1)
+            out = nn(val, probs[:, h * p : (h + 1) * p])
+            both.append(out[:hd])
+            sums.append(out[hd : hd + 8])
+        return cols, new, fade, jnp.concatenate(both, axis=1), jnp.concatenate(sums, axis=1)
+
+    lead = groups // 2
 
     def step(t, carry):
-        for g in range(groups):
-            weigh(t, g)
-            score(t + 1, g)
+        made = []
+        for g in range(0, groups, lead):
+            for u in range(g, g + lead):
+                score(t + (u + lead) // groups, (u + lead) % groups)
+            for u in range(g, g + lead):
+                made.append(weigh(t, u))
+        i = items[0, t]
+        for cols, new, fade, both, sums in made:
+            top[i, :, cols] = new
+            acc[i, :hd, cols] = acc[i, :hd, cols] * fade + both
+            acc[i, hd:, cols] = acc[i, hd:, cols] * fade + sums
         return carry
 
-    for g in range(groups):
+    for g in range(lead):
         score(0, g)
     lax.fori_loop(0, high, step, 0)
 
 
-def put_values(vals, tile, v, live):
-    groups, _, p = vals.shape[1:]
-    depth = v.shape[1] // groups
+def put_values(vals, tile, g0, v, live):
+    p = vals.shape[3]
+    hd = vals.shape[2] // 2 - ONES
     flag = jnp.broadcast_to(live.astype(F32).astype(BF16), (ONES, p))
     vt = jnp.where(live, v.T, 0.0).astype(BF16)
-    for g in range(groups):
-        vals[tile, g, :depth] = vt[g * depth : (g + 1) * depth]
-        vals[tile, g, depth:] = flag
+    for h in range(v.shape[1] // hd):
+        g, r = g0 + h // 2, h % 2 * (hd + ONES)
+        vals[tile, g, r : r + hd] = vt[h * hd : (h + 1) * hd]
+        vals[tile, g, r + hd : r + hd + ONES] = flag
+
+
+def put_blocks(tile0, x, w_all, keys, vals, lives):
+    p, width = keys.shape[1:]
+    wide = min(256, width)
+    groups = vals.shape[1]
+    for c in range(0, width, wide):
+        k = nn(x, w_all[:, width + c : width + c + wide]).astype(BF16)
+        v = nn(x, w_all[:, 2 * width + c : 2 * width + c + wide])
+        for u, live in enumerate(lives):
+            rows = slice(u * p, (u + 1) * p)
+            keys[tile0 + u, :, c : c + wide] = k[rows]
+            put_values(vals, tile0 + u, c * groups // width, v[rows], live)
 
 
 def finish(i, tiled, acc, w_out, alive):
@@ -171,11 +214,11 @@
 
 
 def main_kernel(
-    n, split, tiled, near, norm, masks, counts, w_qkv, w_out, qt, top, acc, w_all, w_last, plan0, plan1, keys, vals,
+    n, split, tiled, near, norm, masks, counts, w_qkv, w_out, qt, top, acc, w_all, w_last, plan0, plan1, keys, vals, nrm,
     items, flags, live, scores, peaks, sems
 ):
     by, p, width = tiled.shape
-    groups, depth = qt.shape[1:3]
+    _, depth = qt.shape[1:3]
     hd = depth // 2
     copies = [
         pltpu.make_async_copy(masks, flags, sems.at[0]),
@@ -210,77 +253,62 @@
         for j in range(j0, j1):
             plan[3, 1 + by + j - j0] = live[j, 0, beyond]
     zeros = jnp.zeros((hd, p), BF16)
+    for j in range(by):
+        nrm[j * p : (j + 1) * p] = normalise(tiled[j], gain, shift)
     copies[2].wait()
-    for c in range(0, by, 2):
-        span = range(c, min(c + 2, by))
-        x = jnp.concatenate([normalise(tiled[j], gain, shift) for j in span], axis=0)
-        q = (nn(x, w_all[:, :width]).astype(BF16) * BF16(1.0 / hd**0.5)).astype(F32)
-        k = nn(x, w_all[:, width : 2 * width]).astype(BF16)
-        v = nn(x, w_all[:, 2 * width :])
-        for u, i in enumerate(span):
-            rows = slice(u * p, (u + 1) * p)
-            keys[i] = k[rows]
-            put_values(vals, i, v[rows], place < live[i, 0, me])
-            t = q[rows].T.astype(BF16)
-            for g in range(groups):
-                mid = g * depth + hd
-                qt[i, g, :hd, :p] = t[g * depth : mid]
+    wide = min(256, width)
+    for c in range(0, width, wide):
+        q = (nn(nrm[: by * p], w_all[:, c : c + wide]).astype(BF16) * BF16(1.0 / hd**0.5)).astype(F32)
+        for i in range(by):
+            t = q[i * p : (i + 1) * p].T.astype(BF16)
+            for u in range(wide // depth):
+                g, mid = c // depth + u, u * depth + hd
+                qt[i, g, :hd, :p] = t[mid - hd : mid]
                 qt[i, g, :hd, p:] = zeros
                 qt[i, g, hd:, :p] = zeros
                 qt[i, g, hd:, p:] = t[mid : mid + hd]
-        x = jnp.concatenate([normalise(near[j], gain, shift) for j in span], axis=0)
-        k = nn(x, w_all[:, width : 2 * width]).astype(BF16)
-        v = nn(x, w_all[:, 2 * width :])
-        for u, i in enumerate(span):
-            rows = slice(u * p, (u + 1) * p)
-            keys[by + i] = k[rows]
-            put_values(vals, by + i, v[rows], place < live[i, 0, slab])
+    for j in range(by):
+        nrm[(by + j) * p : (by + j + 1) * p] = normalise(near[j], gain, shift)
+    put_blocks(0, nrm[: by * p], w_all, keys, vals, [place < live[i, 0, me] for i in range(by)])
+    put_blocks(by, nrm[by * p :], w_all, keys, vals, [place < live[i, 0, slab] for i in range(by)])
     attend(items, pairs, keys, vals, qt, top, acc, scores, peaks)
     copies[3].wait()
 
 
-def far_work(rim, norm, w_all, qt, plan, top, acc, keys, vals, scores, peaks):
+def far_work(rim, norm, w_all, qt, plan, top, acc, keys, vals, nrm, scores, peaks):
     by = qt.shape[0]
-    blocks, p, width = rim.shape
+    blocks, p, _ = rim.shape
     place = lax.broadcasted_iota(jnp.int32, (1, p), 1)
-    gain, shift = norm[0:1], norm[1:2]
     vals[blocks] = jnp.zeros(vals.shape[1:], BF16)
-    for c in range(0, blocks, 2):
-        span = range(c, min(c + 2, blocks))
-        x = jnp.concatenate([normalise(rim[j], gain, shift) for j in span], axis=0)
-        k = nn(x, w_all[:, width : 2 * width]).astype(BF16)
-        v = nn(x, w_all[:, 2 * width :])
-        for u, j in enumerate(span):
-            rows = slice(u * p, (u + 1) * p)
-            keys[j] = k[rows]
-            put_values(vals, j, v[rows], place < plan[3, 1 + by + j])
+    for j in range(blocks):
+        nrm[j * p : (j + 1) * p] = normalise(rim[j], norm[0:1], norm[1:2])
+    put_blocks(0, nrm[...], w_all, keys, vals, [place < plan[3, 1 + by + j] for j in range(blocks)])
     attend(plan, plan[3, 0], keys, vals, qt, top, acc, scores, peaks)
 
 
-def hand_out(blocks, tiled, acc, w_out, plan, result, out, sems):
-    copies = []
-    for u, i in enumerate(blocks):
-        out[u] = finish(i, tiled, acc, w_out, plan[3, 1 + i])
-        copies.append(pltpu.make_async_copy(out.at[u], result.at[0, i, 0], sems.at[u]))
+def far_kernel(
+    rim, norm, w_all, qt, top_in, acc_in, tiled, w_out, plan, top, acc, held, keys, vals, nrm, scores, peaks
+):
+    far_work(rim, norm, w_all, qt, plan, top, acc, keys, vals, nrm, scores, peaks)
+    for i in range(held.shape[0]):
+        held[i] = finish(i, tiled, acc, w_out, plan[3, 1 + i])
+
+
+def last_kernel(
+    rim, norm, w_all, qt, top_in, acc_in, tiled, w_out, held, plan, top, acc, result, keys, vals, nrm, scores, peaks,
+    out, sems
+):
+    by, early = tiled.shape[0], held.shape[0]
+    copies = [pltpu.make_async_copy(held.at[i], result.at[0, i, 0], sems.at[i]) for i in range(early)]
+    for copy in copies:
+        copy.start()
+    far_work(rim, norm, w_all, qt, plan, top, acc, keys, vals, nrm, scores, peaks)
+    for i in range(early, by):
+        out[i - early] = finish(i, tiled, acc, w_out, plan[3, 1 + i])
+        copies.append(pltpu.make_async_copy(out.at[i - early], result.at[0, i, 0], sems.at[i]))
         copies[-1].start()
     for copy in copies:
         copy.wait()
-
-
-def far_kernel(
-    done, rim, norm, w_all, qt, top_in, acc_in, tiled, w_out, plan, top, acc, result, keys, vals, scores, peaks, out,
-    sems
-):
-    far_work(rim, norm, w_all, qt, plan, top, acc, keys, vals, scores, peaks)
-    hand_out(done, tiled, acc, w_out, plan, result, out, sems)
-
-
-def last_kernel(
-    done, rim, norm, w_all, qt, top_in, acc_in, tiled, w_out, plan, result_in, top, acc, result, keys, vals, scores,
-    peaks, out, sems
-):
-    far_work(rim, norm, w_all, qt, plan, top, acc, keys, vals, scores, peaks)
-    hand_out(done, tiled, acc, w_out, plan, result, out, sems)
 
 
 def vmem(x):
@@ -299,8 +327,8 @@
     _, by, bz, p, width = points.shape
     hd = width // HEADS
     groups, depth, lanes = HEADS // 2, 2 * hd, 2 * p
-    split = max(by - 2, 1)
-    early = max(split - 1, 0)
+    split = max(by // 2, 1)
+    early = max(split - 1, 1)
     whole = pl.BlockSpec(memory_space=pltpu.VMEM)
     apart = pl.BlockSpec(memory_space=pltpu.HBM)
     words = pl.BlockSpec(memory_space=pltpu.SMEM)
@@ -311,18 +339,18 @@
     live = pltpu.SMEM(counts.shape, jnp.int32)
     flags = pltpu.SMEM(masks.shape, jnp.int32)
 
-    tiled, first, second, norm = pl.pallas_call(
-        functools.partial(gather_kernel, split),
+    first, rest, places, norm = pl.pallas_call(
+        gather_kernel,
         out_shape=(
-            pltpu.VMEM((by, p, width), BF16),
             pltpu.VMEM((split, p, width), BF16),
             pltpu.VMEM((by - split, p, width), BF16),
+            pltpu.VMEM((by - split, 1, p), jnp.int32),
             pltpu.VMEM((2, width), F32),
         ),
         in_specs=[apart] * 5,
         out_specs=(whole,) * 4,
         scratch_shapes=[
-            pltpu.VMEM((by, p, width), BF16),
+            pltpu.VMEM((split, p, width), BF16),
             pltpu.VMEM(order.shape, jnp.int32),
             live,
             pltpu.SemaphoreType.DMA((by + 4,)),
@@ -330,6 +358,15 @@
         compiler_params=params,
         name="gather",
     )(points, order, counts, hbm(gain[None]), hbm(shift_bias[None]))
+    tile_rest = pl.pallas_call(
+        rest_kernel,
+        out_shape=(pltpu.VMEM((by, p, width), BF16), pltpu.VMEM((by - split, p, width), BF16)),
+        in_specs=[whole] * 3,
+        out_specs=(whole,) * 2,
+        compiler_params=params,
+        name="rest",
+    )
+    tiled, second = tile_rest(vmem(first), vmem(rest), vmem(places))
     near_pairs = [(i, i ^ 1) for i in range(n) if i ^ 1 < n]
     far_pairs = [(i, i + 1) for i in range(1, n - 1, 2)] + [(i + 1, i) for i in range(1, n - 1, 2)]
 
@@ -348,7 +385,8 @@
     def scratch(tiles):
         return [
             pltpu.VMEM((tiles, p, width), BF16),
-            pltpu.VMEM((tiles + 1, groups, depth + ONES, p), BF16),
+            pltpu.VMEM((tiles + 1, groups, depth + 2 * ONES, p), BF16),
+            pltpu.VMEM((tiles * p, width), BF16),
         ]
 
     ahead = [
@@ -372,25 +410,33 @@
         name="main",
     )(vmem(tiled), vmem(near), vmem(norm), masks, counts, w_qkv, w_out)
 
-    def far(kernel, done, block, plan, top, acc, result):
-        ins = [block, norm, w_all, qt, top, acc, tiled, w_last]
-        return pl.pallas_call(
-            functools.partial(kernel, done),
-            out_shape=(*state, pltpu.HBM((1, by, bz, p, width), BF16)),
-            in_specs=[*(whole,) * len(ins), words, *(apart,) * len(result)],
-            out_specs=(whole, whole, apart),
-            scratch_shapes=[
-                *scratch(block.shape[0]),
-                *ahead,
-                pltpu.VMEM((max(len(done), 1), p, width), BF16),
-                pltpu.SemaphoreType.DMA((by,)),
-            ],
-            input_output_aliases={4: 0, 5: 1, **({9: 2} if result else {})},
-            compiler_params=params,
-        )(*map(vmem, ins), smem(plan), *result)
-
-    top, acc, result = far(far_kernel, range(early), far0, plan0, top, acc, ())
-    _, _, result = far(last_kernel, range(early, by), far1, plan1, top, acc, (result,))
+    ins = [far0, norm, w_all, qt, top, acc, tiled, w_last]
+    top, acc, held = pl.pallas_call(
+        far_kernel,
+        out_shape=(*state, pltpu.VMEM((early, p, width), BF16)),
+        in_specs=[*(whole,) * len(ins), words],
+        out_specs=(whole,) * 3,
+        scratch_shapes=[*scratch(split), *ahead],
+        input_output_aliases={4: 0, 5: 1},
+        compiler_params=params,
+        name="far",
+    )(*map(vmem, ins), smem(plan0))
+    ins = [far1, norm, w_all, qt, top, acc, tiled, w_last, held]
+    _, _, result = pl.pallas_call(
+        last_kernel,
+        out_shape=(*state, pltpu.HBM((1, by, bz, p, width), BF16)),
+        in_specs=[*(whole,) * len(ins), words],
+        out_specs=(whole, whole, apart),
+        scratch_shapes=[
+            *scratch(by - split),
+            *ahead,
+            pltpu.VMEM((by - early, p, width), BF16),
+            pltpu.SemaphoreType.DMA((by,)),
+        ],
+        input_output_aliases={4: 0, 5: 1},
+        compiler_params=params,
+        name="last",
+    )(*map(vmem, ins), smem(plan1))
     return result
 
 

time: 29.1 us -> 28.1 us (0.966)
  the two profiles are of different devices: /device:TPU:27 before, /device:TPU:1 now
where the time goes in v5:
time: 28.1 us; the launch traced here: 27.8 us
  Pallas kernels  17 us (60%)
  starting transfers between devices  6.53 us (23%)
  waiting for transfers between devices  4.24 us (15%)
    pallas_call x1, Pallas kernels, shards(): pl.pallas_call(functools.partial(main_kernel, n, split), out_shape=(pltpu...  8.34 us
    ppermute x3, starting transfers between devices, moved(): return lax.ppermute(value, 'gx', pairs)  6.53 us
    ppermute x3, waiting for transfers between devices, moved(): return lax.ppermute(value, 'gx', pairs)  4.24 us
    pallas_call x1, Pallas kernels, shards(): pl.pallas_call(last_kernel, out_shape=(*state, pltpu.HBM((1, by, bz, p, w...  4.13 us
    pallas_call x1, Pallas kernels, shards(): pl.pallas_call(far_kernel, out_shape=(*state, pltpu.VMEM((early, p, width...  2.81 us
    pallas_call x1, Pallas kernels, shards(): pl.pallas_call(gather_kernel, out_shape=(pltpu.VMEM((split, p, width), BF...  1.43 us
  transfers between devices with their start and end apart: 3, of which 2 were waited for; matrix products, arithmetic and copies ran while one was open for 0% of the time, Pallas kernels for 40%

profile of v5, /device:TPU:1, one launch (start us, length us, event | category | flops | bytes accessed | tf_op | source)
XLA Modules:
  0.0 27.8 jit_solution(11324716143821535723)
XLA Ops:
  0.0 1.4 %gather.1 = (bf16[3,128,512]{2,1,0:T(8,128)(2,1)S(1)}, bf16[3,128,512]{2,1,0:T(8,128)(2,1)S(1)}, s32[3,1,128]{2,1,0:T(1,128)S(1)}, f32[2,512]{1,0:T(2,128)S(1)}) custom-call(bf16[1,6,1,128,512]{4,3,2,1,0:T(8,128)(2,1)} %points.1, s32[1,6,1,128]{3,2,1,0:T(1,128)} %order.1, s32[6,1,16]{2,1,0:T(1,128)} %bitcast.3, f32[1,512]{1,0:T(1,128)} %bitcast.5, ...), custom_call_target="tpu_custom_call" | custom-call | tf_op jit(solution)/shard_map/gather/pallas_call | solution.py:342
  1.4 0.3 %rest.1 = (bf16[6,128,512]{2,1,0:T(8,128)(2,1)S(1)}, bf16[3,128,512]{2,1,0:T(8,128)(2,1)S(1)}) custom-call(bf16[3,128,512]{2,1,0:T(8,128)(2,1)S(1)} %get-tuple-element.22.first, bf16[3,128,512]{2,1,0:T(8,128)(2,1)S(1)} %get-tuple-element.23.rest, s32[3,1,128]{2,1,0:T(1,128)S(1)} %get-tuple-element.24.places), custom_call_target="tpu_custom_call" | custom-call | tf_op jit(solution)/shard_map/rest/pallas_call | solution.py:369
  1.7 0.1 collective-permute-start.1
  1.8 4.5 %collective-permute-start.2 = (bf16[3,128,512]{2,1,0:T(8,128)(2,1)S(1)}, bf16[3,128,512]{2,1,0:T(8,128)(2,1)S(1)}, u32[]{:S(2)}, u32[]{:S(2)}) collective-permute-start(bf16[3,128,512]{2,1,0:T(8,128)(2,1)S(1)} %get-tuple-element.22.first), channel_id=1, source_target_pairs={{1,2},{3,4},{5,6},{7,8},{9,10},{11,12},{13,14},{2,1},{4,3},{6,5},{... | collective-permute-start | bytes 1179656 | tf_op jit(solution)/shard_map/ppermute | solution.py:374
  6.4 1.9 %collective-permute-start = (bf16[3,128,512]{2,1,0:T(8,128)(2,1)S(1)}, bf16[3,128,512]{2,1,0:T(8,128)(2,1)S(1)}, u32[]{:S(2)}, u32[]{:S(2)}) collective-permute-start(bf16[3,128,512]{2,1,0:T(8,128)(2,1)S(1)} %get-tuple-element.25), channel_id=1, source_target_pairs={{1,2},{3,4},{5,6},{7,8},{9,10},{11,12},{13,14},{2,1},{4,3},{6,5},{... | collective-permute-start | bytes 1179656 | tf_op jit(solution)/shard_map/ppermute | solution.py:374
  8.3 0.0 collective-permute-done.1.near
  8.3 8.3 %main.1 = (bf16[6,4,128,256]{3,2,1,0:T(8,128)(2,1)S(1)}, f32[6,1,1024]{2,1,0:T(1,128)S(1)}, f32[6,72,1024]{2,1,0:T(8,128)S(1)}, bf16[512,1536]{1,0:T(8,128)(2,1)...) custom-call(bf16[6,128,512]{2,1,0:T(8,128)(2,1)S(1)} %get-tuple-element.27.tiled, ...), custom_call_target="tpu_custom_call" | custom-call | tf_op jit(solution)/shard_map/main/pallas_call | solution.py:396
  16.6 2.8 %collective-permute-done.2.rim = bf16[3,128,512]{2,1,0:T(8,128)(2,1)S(1)} collective-permute-done((bf16[3,128,512]{2,1,0:T(8,128)(2,1)S(1)}, bf16[3,128,512]{2,1,0:T(8,128)(2,1)S(1)}, u32[]{:S(2)}, u32[]{:S(2)}) %collective-permute-start.2) | collective-permute-done | bytes 393248 | tf_op jit(solution)/shard_map/ppermute | solution.py:374
  19.5 2.8 %far.1 = (f32[6,1,1024]{2,1,0:T(1,128)S(1)}, f32[6,72,1024]{2,1,0:T(8,128)S(1)}, bf16[2,128,512]{2,1,0:T(8,128)(2,1)S(1)}) custom-call(bf16[3,128,512]{2,1,0:T(8,128)(2,1)S(1)} %collective-permute-done.2.rim, f32[2,512]{1,0:T(2,128)S(1)} %get-tuple-element.26.norm, ...), custom_call_target="tpu_custom_call", output_to_operand_aliasing={{0}: (4, {}), {1}: (5, {})} | custom-call | tf_op jit(solution)/shard_map/far/pallas_call | solution.py:414
  22.3 1.4 %collective-permute-done.rim = bf16[3,128,512]{2,1,0:T(8,128)(2,1)S(1)} collective-permute-done((bf16[3,128,512]{2,1,0:T(8,128)(2,1)S(1)}, bf16[3,128,512]{2,1,0:T(8,128)(2,1)S(1)}, u32[]{:S(2)}, u32[]{:S(2)}) %collective-permute-start) | collective-permute-done | bytes 393248 | tf_op jit(solution)/shard_map/ppermute | solution.py:374
  23.7 4.1 %last.1 = (f32[6,1,1024]{2,1,0:T(1,128)S(1)}, f32[6,72,1024]{2,1,0:T(8,128)S(1)}, bf16[1,6,1,128,512]{4,3,2,1,0:T(8,128)(2,1)}) custom-call(bf16[3,128,512]{2,1,0:T(8,128)(2,1)S(1)} %collective-permute-done.rim, f32[2,512]{1,0:T(2,128)S(1)} %get-tuple-element.26.norm, ...), custom_call_target="tpu_custom_call", output_to_operand_aliasing={{0}: (4, {}), {1}: (5, {})} | custom-call | tf_op jit(solution)/shard_map/last/pallas_call | solution.py:425
Async XLA Ops:
  1.7 6.5 %collective-permute-start.1 = (bf16[6,128,512]{2,1,0:T(8,128)(2,1)S(1)}, bf16[6,128,512]{2,1,0:T(8,128)(2,1)S(1)}, u32[]{:S(2)}, u32[]{:S(2)}) collective-permute-start(bf16[6,128,512]{2,1,0:T(8,128)(2,1)S(1)} %get-tuple-element.27.tiled), channel_id=1, source_target_pairs={{0,1},{1,0},{2,3},{3,2},{4,5},{5,4},{6,7},{7,6},{8,9},{9,8},{10,11... | collective-permute-start | bytes 2359304 | tf_op jit(solution)/shard_map/ppermute | solution.py:374
  1.8 17.7 %collective-permute-start.2 = (bf16[3,128,512]{2,1,0:T(8,128)(2,1)S(1)}, bf16[3,128,512]{2,1,0:T(8,128)(2,1)S(1)}, u32[]{:S(2)}, u32[]{:S(2)}) collective-permute-start(bf16[3,128,512]{2,1,0:T(8,128)(2,1)S(1)} %get-tuple-element.22.first), channel_id=1, source_target_pairs={{1,2},{3,4},{5,6},{7,8},{9,10},{11,12},{13,14},{2,1},{4,3},{6,5},{... | collective-permute-start | bytes 1179656 | tf_op jit(solution)/shard_map/ppermute | solution.py:374
  6.4 17.3 %collective-permute-start = (bf16[3,128,512]{2,1,0:T(8,128)(2,1)S(1)}, bf16[3,128,512]{2,1,0:T(8,128)(2,1)S(1)}, u32[]{:S(2)}, u32[]{:S(2)}) collective-permute-start(bf16[3,128,512]{2,1,0:T(8,128)(2,1)S(1)} %get-tuple-element.25), channel_id=1, source_target_pairs={{1,2},{3,4},{5,6},{7,8},{9,10},{11,12},{13,14},{2,1},{4,3},{6,5},{... | collective-permute-start | bytes 1179656 | tf_op jit(solution)/shard_map/ppermute | solution.py:374

commit v6 on v5

--- a/solution.py
+++ b/solution.py
@@ -71,14 +71,19 @@
         copy.wait()
 
 
-def rest_kernel(first, rest, places, tiled, second):
+def rest_kernel(first, rest, places, norm, tiled, normed, second):
     split = first.shape[0]
-    for j in range(split):
-        tiled[j] = first[j]
+    gain, shift = norm[0:1], norm[1:2]
     for j in range(rest.shape[0]):
         got = select(places[j], rest[j])
+        tiled[split + j] = got
+        got = normalise(got, gain, shift)
         second[j] = got
-        tiled[split + j] = got
+        normed[split + j] = got
+    for j in range(split):
+        got = first[j]
+        tiled[j] = got
+        normed[j] = normalise(got, gain, shift)
 
 
 def toward_near():
@@ -214,10 +219,10 @@
 
 
 def main_kernel(
-    n, split, tiled, near, norm, masks, counts, w_qkv, w_out, qt, top, acc, w_all, w_last, plan0, plan1, keys, vals, nrm,
+    n, split, own, near, masks, counts, w_qkv, w_out, qt, top, acc, w_all, w_last, plan0, plan1, keys, vals,
     items, flags, live, scores, peaks, sems
 ):
-    by, p, width = tiled.shape
+    by, p, width = own.shape
     _, depth = qt.shape[1:3]
     hd = depth // 2
     copies = [
@@ -234,7 +239,6 @@
     exists = (partner >= 0) & (partner < n)
     slab = jnp.clip(partner, 0, n - 1)
     place = lax.broadcasted_iota(jnp.int32, (1, p), 1)
-    gain, shift = norm[0:1], norm[1:2]
     top[...] = jnp.full_like(top, NEG)
     acc[...] = jnp.zeros_like(acc)
     vals[2 * by] = jnp.zeros(vals.shape[1:], BF16)
@@ -253,12 +257,11 @@
         for j in range(j0, j1):
             plan[3, 1 + by + j - j0] = live[j, 0, beyond]
     zeros = jnp.zeros((hd, p), BF16)
-    for j in range(by):
-        nrm[j * p : (j + 1) * p] = normalise(tiled[j], gain, shift)
     copies[2].wait()
+    mine, theirs = own[...].reshape(by * p, width), near[...].reshape(by * p, width)
     wide = min(256, width)
     for c in range(0, width, wide):
-        q = (nn(nrm[: by * p], w_all[:, c : c + wide]).astype(BF16) * BF16(1.0 / hd**0.5)).astype(F32)
+        q = (nn(mine, w_all[:, c : c + wide]).astype(BF16) * BF16(1.0 / hd**0.5)).astype(F32)
         for i in range(by):
             t = q[i * p : (i + 1) * p].T.astype(BF16)
             for u in range(wide // depth):
@@ -267,42 +270,40 @@
                 qt[i, g, :hd, p:] = zeros
                 qt[i, g, hd:, :p] = zeros
                 qt[i, g, hd:, p:] = t[mid : mid + hd]
-    for j in range(by):
-        nrm[(by + j) * p : (by + j + 1) * p] = normalise(near[j], gain, shift)
-    put_blocks(0, nrm[: by * p], w_all, keys, vals, [place < live[i, 0, me] for i in range(by)])
-    put_blocks(by, nrm[by * p :], w_all, keys, vals, [place < live[i, 0, slab] for i in range(by)])
+    put_blocks(0, mine, w_all, keys, vals, [place < live[i, 0, me] for i in range(by)])
+    put_blocks(by, theirs, w_all, keys, vals, [place < live[i, 0, slab] for i in range(by)])
     attend(items, pairs, keys, vals, qt, top, acc, scores, peaks)
     copies[3].wait()
 
 
-def far_work(rim, norm, w_all, qt, plan, top, acc, keys, vals, nrm, scores, peaks):
+def far_work(rim, w_all, qt, plan, top, acc, keys, vals, scores, peaks):
     by = qt.shape[0]
-    blocks, p, _ = rim.shape
+    blocks, p, width = rim.shape
     place = lax.broadcasted_iota(jnp.int32, (1, p), 1)
     vals[blocks] = jnp.zeros(vals.shape[1:], BF16)
-    for j in range(blocks):
-        nrm[j * p : (j + 1) * p] = normalise(rim[j], norm[0:1], norm[1:2])
-    put_blocks(0, nrm[...], w_all, keys, vals, [place < plan[3, 1 + by + j] for j in range(blocks)])
+    put_blocks(0, rim[...].reshape(blocks * p, width), w_all, keys, vals, [place < plan[3, 1 + by + j] for j in range(blocks)])
     attend(plan, plan[3, 0], keys, vals, qt, top, acc, scores, peaks)
 
 
 def far_kernel(
-    rim, norm, w_all, qt, top_in, acc_in, tiled, w_out, plan, top, acc, held, keys, vals, nrm, scores, peaks
+    rim, norm, w_all, qt, top_in, acc_in, tiled, w_out, plan, top, acc, held, keys, vals, scores, peaks, nrm
 ):
-    far_work(rim, norm, w_all, qt, plan, top, acc, keys, vals, nrm, scores, peaks)
+    for j in range(rim.shape[0]):
+        nrm[j] = normalise(rim[j], norm[0:1], norm[1:2])
+    far_work(nrm, w_all, qt, plan, top, acc, keys, vals, scores, peaks)
     for i in range(held.shape[0]):
         held[i] = finish(i, tiled, acc, w_out, plan[3, 1 + i])
 
 
 def last_kernel(
-    rim, norm, w_all, qt, top_in, acc_in, tiled, w_out, held, plan, top, acc, result, keys, vals, nrm, scores, peaks,
-    out, sems
+    rim, w_all, qt, top_in, acc_in, tiled, w_out, held, plan, top, acc, result, keys, vals, scores, peaks, out,
+    sems
 ):
     by, early = tiled.shape[0], held.shape[0]
     copies = [pltpu.make_async_copy(held.at[i], result.at[0, i, 0], sems.at[i]) for i in range(early)]
     for copy in copies:
         copy.start()
-    far_work(rim, norm, w_all, qt, plan, top, acc, keys, vals, nrm, scores, peaks)
+    far_work(rim, w_all, qt, plan, top, acc, keys, vals, scores, peaks)
     for i in range(early, by):
         out[i - early] = finish(i, tiled, acc, w_out, plan[3, 1 + i])
         copies.append(pltpu.make_async_copy(out.at[i - early], result.at[0, i, 0], sems.at[i]))
@@ -360,13 +361,17 @@
     )(points, order, counts, hbm(gain[None]), hbm(shift_bias[None]))
     tile_rest = pl.pallas_call(
         rest_kernel,
-        out_shape=(pltpu.VMEM((by, p, width), BF16), pltpu.VMEM((by - split, p, width), BF16)),
-        in_specs=[whole] * 3,
-        out_specs=(whole,) * 2,
+        out_shape=(
+            pltpu.VMEM((by, p, width), BF16),
+            pltpu.VMEM((by, p, width), BF16),
+            pltpu.VMEM((by - split, p, width), BF16),
+        ),
+        in_specs=[whole] * 4,
+        out_specs=(whole,) * 3,
         compiler_params=params,
         name="rest",
     )
-    tiled, second = tile_rest(vmem(first), vmem(rest), vmem(places))
+    tiled, normed, second = tile_rest(vmem(first), vmem(rest), vmem(places), vmem(norm))
     near_pairs = [(i, i ^ 1) for i in range(n) if i ^ 1 < n]
     far_pairs = [(i, i + 1) for i in range(1, n - 1, 2)] + [(i + 1, i) for i in range(1, n - 1, 2)]
 
@@ -374,7 +379,7 @@
         return lax.ppermute(value, "gx", pairs)
 
     far0 = moved(first, far_pairs)
-    near = moved(tiled, near_pairs)
+    near = moved(normed, near_pairs)
     far1 = moved(second, far_pairs)
 
     state = (
@@ -386,7 +391,6 @@
         return [
             pltpu.VMEM((tiles, p, width), BF16),
             pltpu.VMEM((tiles + 1, groups, depth + 2 * ONES, p), BF16),
-            pltpu.VMEM((tiles * p, width), BF16),
         ]
 
     ahead = [
@@ -403,12 +407,12 @@
             plan,
             plan,
         ),
-        in_specs=[whole, whole, whole, apart, apart, apart, apart],
+        in_specs=[whole, whole, apart, apart, apart, apart],
         out_specs=(whole,) * 5 + (words,) * 2,
         scratch_shapes=[*scratch(2 * by), plan, flags, live, *ahead, pltpu.SemaphoreType.DMA((4,))],
         compiler_params=params,
         name="main",
-    )(vmem(tiled), vmem(near), vmem(norm), masks, counts, w_qkv, w_out)
+    )(vmem(normed), vmem(near), masks, counts, w_qkv, w_out)
 
     ins = [far0, norm, w_all, qt, top, acc, tiled, w_last]
     top, acc, held = pl.pallas_call(
@@ -416,12 +420,12 @@
         out_shape=(*state, pltpu.VMEM((early, p, width), BF16)),
         in_specs=[*(whole,) * len(ins), words],
         out_specs=(whole,) * 3,
-        scratch_shapes=[*scratch(split), *ahead],
+        scratch_shapes=[*scratch(split), *ahead, pltpu.VMEM((split, p, width), BF16)],
         input_output_aliases={4: 0, 5: 1},
         compiler_params=params,
         name="far",
     )(*map(vmem, ins), smem(plan0))
-    ins = [far1, norm, w_all, qt, top, acc, tiled, w_last, held]
+    ins = [far1, w_all, qt, top, acc, tiled, w_last, held]
     _, _, result = pl.pallas_call(
         last_kernel,
         out_shape=(*state, pltpu.HBM((1, by, bz, p, width), BF16)),
@@ -433,7 +437,7 @@
             pltpu.VMEM((by - early, p, width), BF16),
             pltpu.SemaphoreType.DMA((by,)),
         ],
-        input_output_aliases={4: 0, 5: 1},
+        input_output_aliases={3: 0, 4: 1},
         compiler_params=params,
         name="last",
     )(*map(vmem, ins), smem(plan1))

time: 28.1 us -> 28.3 us (level)
    pallas_call x1, Pallas kernels: 0.3 us -> 0.66 us  [shards(): tile_rest(vmem(first), vmem(rest), vmem(places), vmem(norm))]
  transfers between devices with their start and end apart: 3 -> 3, of which waited for: 2 -> 2; matrix products, arithmetic and copies ran while one was open for 0% -> 0% of each run, Pallas kernels for 40% -> 39%
where the time goes in v6:
time: 28.3 us; the launch traced here: 28 us
  Pallas kernels  17.1 us (60%)
  starting transfers between devices  6.53 us (23%)
  waiting for transfers between devices  4.36 us (15%)
    pallas_call x1, Pallas kernels, shards(): pl.pallas_call(functools.partial(main_kernel, n, split), out_shape=(pltpu...  8.22 us
    ppermute x3, starting transfers between devices, moved(): return lax.ppermute(value, 'gx', pairs)  6.53 us
    ppermute x3, waiting for transfers between devices, moved(): return lax.ppermute(value, 'gx', pairs)  4.36 us
    pallas_call x1, Pallas kernels, shards(): pl.pallas_call(last_kernel, out_shape=(*state, pltpu.HBM((1, by, bz, p, w...  3.93 us
    pallas_call x1, Pallas kernels, shards(): pl.pallas_call(far_kernel, out_shape=(*state, pltpu.VMEM((early, p, width...  2.82 us
    pallas_call x1, Pallas kernels, shards(): pl.pallas_call(gather_kernel, out_shape=(pltpu.VMEM((split, p, width), BF...  1.43 us
    pallas_call x1, Pallas kernels, shards(): tile_rest(vmem(first), vmem(rest), vmem(places), vmem(norm))  0.66 us
  transfers between devices with their start and end apart: 3, of which 2 were waited for; matrix products, arithmetic and copies ran while one was open for 0% of the time, Pallas kernels for 39%

profile of v6, /device:TPU:1, one launch (start us, length us, event | category | flops | bytes accessed | tf_op | source)
XLA Modules:
  0.0 28.0 jit_solution(16316969020649548716)
XLA Ops:
  0.0 1.4 %gather.1 = (bf16[3,128,512]{2,1,0:T(8,128)(2,1)S(1)}, bf16[3,128,512]{2,1,0:T(8,128)(2,1)S(1)}, s32[3,1,128]{2,1,0:T(1,128)S(1)}, f32[2,512]{1,0:T(2,128)S(1)}) custom-call(bf16[1,6,1,128,512]{4,3,2,1,0:T(8,128)(2,1)} %points.1, s32[1,6,1,128]{3,2,1,0:T(1,128)} %order.1, s32[6,1,16]{2,1,0:T(1,128)} %bitcast.3, f32[1,512]{1,0:T(1,128)} %bitcast.5, ...), custom_call_target="tpu_custom_call" | custom-call | tf_op jit(solution)/shard_map/gather/pallas_call | solution.py:343
  1.4 0.7 %rest.1 = (bf16[6,128,512]{2,1,0:T(8,128)(2,1)S(1)}, bf16[6,128,512]{2,1,0:T(8,128)(2,1)S(1)}, bf16[3,128,512]{2,1,0:T(8,128)(2,1)S(1)}) custom-call(bf16[3,128,512]{2,1,0:T(8,128)(2,1)S(1)} %get-tuple-element.23.first, bf16[3,128,512]{2,1,0:T(8,128)(2,1)S(1)} %get-tuple-element.24.rest, s32[3,1,128]{2,1,0:T(1,128)S(1)} %get-tuple-element.25.places, ...), custom_call_target="tpu_custom_call" | custom-call | tf_op jit(solution)/shard_map/rest/pallas_call | solution.py:374
  2.1 0.1 collective-permute-start.1
  2.2 4.5 %collective-permute-start.2 = (bf16[3,128,512]{2,1,0:T(8,128)(2,1)S(1)}, bf16[3,128,512]{2,1,0:T(8,128)(2,1)S(1)}, u32[]{:S(2)}, u32[]{:S(2)}) collective-permute-start(bf16[3,128,512]{2,1,0:T(8,128)(2,1)S(1)} %get-tuple-element.23.first), channel_id=1, source_target_pairs={{1,2},{3,4},{5,6},{7,8},{9,10},{11,12},{13,14},{2,1},{4,3},{6,5},{... | collective-permute-start | bytes 1179656 | tf_op jit(solution)/shard_map/ppermute | solution.py:379
  6.7 1.9 %collective-permute-start = (bf16[3,128,512]{2,1,0:T(8,128)(2,1)S(1)}, bf16[3,128,512]{2,1,0:T(8,128)(2,1)S(1)}, u32[]{:S(2)}, u32[]{:S(2)}) collective-permute-start(bf16[3,128,512]{2,1,0:T(8,128)(2,1)S(1)} %get-tuple-element.27), channel_id=1, source_target_pairs={{1,2},{3,4},{5,6},{7,8},{9,10},{11,12},{13,14},{2,1},{4,3},{6,5},{... | collective-permute-start | bytes 1179656 | tf_op jit(solution)/shard_map/ppermute | solution.py:379
  8.7 0.0 collective-permute-done.1.near
  8.7 8.2 %main.1 = (bf16[6,4,128,256]{3,2,1,0:T(8,128)(2,1)S(1)}, f32[6,1,1024]{2,1,0:T(1,128)S(1)}, f32[6,72,1024]{2,1,0:T(8,128)S(1)}, bf16[512,1536]{1,0:T(8,128)(2,1)...) custom-call(bf16[6,128,512]{2,1,0:T(8,128)(2,1)S(1)} %get-tuple-element.28.own, ...), custom_call_target="tpu_custom_call" | custom-call | tf_op jit(solution)/shard_map/main/pallas_call | solution.py:400
  16.9 3.0 %collective-permute-done.2.rim = bf16[3,128,512]{2,1,0:T(8,128)(2,1)S(1)} collective-permute-done((bf16[3,128,512]{2,1,0:T(8,128)(2,1)S(1)}, bf16[3,128,512]{2,1,0:T(8,128)(2,1)S(1)}, u32[]{:S(2)}, u32[]{:S(2)}) %collective-permute-start.2) | collective-permute-done | bytes 393248 | tf_op jit(solution)/shard_map/ppermute | solution.py:379
  19.9 2.8 %far.1 = (f32[6,1,1024]{2,1,0:T(1,128)S(1)}, f32[6,72,1024]{2,1,0:T(8,128)S(1)}, bf16[2,128,512]{2,1,0:T(8,128)(2,1)S(1)}) custom-call(bf16[3,128,512]{2,1,0:T(8,128)(2,1)S(1)} %collective-permute-done.2.rim, f32[2,512]{1,0:T(2,128)S(1)} %get-tuple-element.26.norm, ...), custom_call_target="tpu_custom_call", output_to_operand_aliasing={{0}: (4, {}), {1}: (5, {})} | custom-call | tf_op jit(solution)/shard_map/far/pallas_call | solution.py:418
  22.7 1.4 %collective-permute-done.rim = bf16[3,128,512]{2,1,0:T(8,128)(2,1)S(1)} collective-permute-done((bf16[3,128,512]{2,1,0:T(8,128)(2,1)S(1)}, bf16[3,128,512]{2,1,0:T(8,128)(2,1)S(1)}, u32[]{:S(2)}, u32[]{:S(2)}) %collective-permute-start) | collective-permute-done | bytes 393248 | tf_op jit(solution)/shard_map/ppermute | solution.py:379
  24.1 3.9 %last.1 = (f32[6,1,1024]{2,1,0:T(1,128)S(1)}, f32[6,72,1024]{2,1,0:T(8,128)S(1)}, bf16[1,6,1,128,512]{4,3,2,1,0:T(8,128)(2,1)}) custom-call(bf16[3,128,512]{2,1,0:T(8,128)(2,1)S(1)} %collective-permute-done.rim, bf16[512,1536]{1,0:T(8,128)(2,1)S(1)} %get-tuple-element.29.w_all, ...), custom_call_target="tpu_custom_call", output_to_operand_aliasing={{0}: (3, {}), {1}: (4, {})} | custom-call | tf_op jit(solution)/shard_map/last/pallas_call | solution.py:429
Async XLA Ops:
  2.1 6.5 %collective-permute-start.1 = (bf16[6,128,512]{2,1,0:T(8,128)(2,1)S(1)}, bf16[6,128,512]{2,1,0:T(8,128)(2,1)S(1)}, u32[]{:S(2)}, u32[]{:S(2)}) collective-permute-start(bf16[6,128,512]{2,1,0:T(8,128)(2,1)S(1)} %get-tuple-element.28.own), channel_id=1, source_target_pairs={{0,1},{1,0},{2,3},{3,2},{4,5},{5,4},{6,7},{7,6},{8,9},{9,8},{10,11... | collective-permute-start | bytes 2359304 | tf_op jit(solution)/shard_map/ppermute | solution.py:379
  2.2 17.7 %collective-permute-start.2 = (bf16[3,128,512]{2,1,0:T(8,128)(2,1)S(1)}, bf16[3,128,512]{2,1,0:T(8,128)(2,1)S(1)}, u32[]{:S(2)}, u32[]{:S(2)}) collective-permute-start(bf16[3,128,512]{2,1,0:T(8,128)(2,1)S(1)} %get-tuple-element.23.first), channel_id=1, source_target_pairs={{1,2},{3,4},{5,6},{7,8},{9,10},{11,12},{13,14},{2,1},{4,3},{6,5},{... | collective-permute-start | bytes 1179656 | tf_op jit(solution)/shard_map/ppermute | solution.py:379
  6.7 17.3 %collective-permute-start = (bf16[3,128,512]{2,1,0:T(8,128)(2,1)S(1)}, bf16[3,128,512]{2,1,0:T(8,128)(2,1)S(1)}, u32[]{:S(2)}, u32[]{:S(2)}) collective-permute-start(bf16[3,128,512]{2,1,0:T(8,128)(2,1)S(1)} %get-tuple-element.27), channel_id=1, source_target_pairs={{1,2},{3,4},{5,6},{7,8},{9,10},{11,12},{13,14},{2,1},{4,3},{6,5},{... | collective-permute-start | bytes 1179656 | tf_op jit(solution)/shard_map/ppermute | solution.py:379

commit v7 on v6

--- a/solution.py
+++ b/solution.py
@@ -99,7 +99,7 @@
 
 def list_pairs(items, masks, by, sides):
     spare = sum(j1 - j0 for _, _, j0, j1, _, _ in sides)
-    pairs, ends = jnp.int32(0), []
+    pairs = jnp.int32(0)
     for i in range(by):
         start, found, last = pairs, jnp.int32(0), jnp.int32(0)
         most = 0
@@ -125,11 +125,10 @@
         for u in range((most + 1) // 2):
             items[0, start + u] = i
         pairs = start + ((found + 1) >> 1)
-        ends.append(pairs)
     items[0, pairs] = 0
     for u in range(2):
         items[1, 2 * pairs + u] = 0
-    return pairs, ends
+    return pairs
 
 
 def attend(items, high, keys, vals, qt, top, acc, scores, peaks):
@@ -218,8 +217,8 @@
     return jnp.where(place < alive, mixed, 0.0).astype(BF16)
 
 
-def main_kernel(
-    n, split, own, near, masks, counts, w_qkv, w_out, qt, top, acc, w_all, w_last, plan0, plan1, keys, vals,
+def own_kernel(
+    n, split, own, masks, counts, w_qkv, w_out, qt, top, acc, w_all, w_last, plan_near, plan0, plan1, keys, vals,
     items, flags, live, scores, peaks, sems
 ):
     by, p, width = own.shape
@@ -235,30 +234,24 @@
         copy.start()
     me = lax.axis_index("gx")
     side = toward_near()
-    partner = me + side
-    exists = (partner >= 0) & (partner < n)
-    slab = jnp.clip(partner, 0, n - 1)
     place = lax.broadcasted_iota(jnp.int32, (1, p), 1)
     top[...] = jnp.full_like(top, NEG)
     acc[...] = jnp.zeros_like(acc)
-    vals[2 * by] = jnp.zeros(vals.shape[1:], BF16)
+    vals[by] = jnp.zeros(vals.shape[1:], BF16)
     copies[0].wait()
     copies[1].wait()
-    pairs, _ = list_pairs(
-        items, flags, by, [(0, None, 0, by, 0, True), (side, exists, 0, by, by, False)]
-    )
-    other = me - side
-    there = (other >= 0) & (other < n)
-    beyond = jnp.clip(other, 0, n - 1)
-    for plan, j0, j1 in ((plan0, 0, split), (plan1, split, by)):
-        plan[3, 0], _ = list_pairs(plan, flags, by, [(-side, there, j0, j1, 0, False)])
+    pairs = list_pairs(items, flags, by, [(0, None, 0, by, 0, True)])
+    for plan, a, j0, j1 in ((plan_near, side, 0, by), (plan0, -side, 0, split), (plan1, -side, split, by)):
+        there = (me + a >= 0) & (me + a < n)
+        slab = jnp.clip(me + a, 0, n - 1)
+        plan[3, 0] = list_pairs(plan, flags, by, [(a, there, j0, j1, 0, False)])
         for i in range(by):
             plan[3, 1 + i] = live[i, 0, me]
         for j in range(j0, j1):
-            plan[3, 1 + by + j - j0] = live[j, 0, beyond]
+            plan[3, 1 + by + j - j0] = live[j, 0, slab]
     zeros = jnp.zeros((hd, p), BF16)
     copies[2].wait()
-    mine, theirs = own[...].reshape(by * p, width), near[...].reshape(by * p, width)
+    mine = own[...].reshape(by * p, width)
     wide = min(256, width)
     for c in range(0, width, wide):
         q = (nn(mine, w_all[:, c : c + wide]).astype(BF16) * BF16(1.0 / hd**0.5)).astype(F32)
@@ -271,7 +264,6 @@
                 qt[i, g, hd:, :p] = zeros
                 qt[i, g, hd:, p:] = t[mid : mid + hd]
     put_blocks(0, mine, w_all, keys, vals, [place < live[i, 0, me] for i in range(by)])
-    put_blocks(by, theirs, w_all, keys, vals, [place < live[i, 0, slab] for i in range(by)])
     attend(items, pairs, keys, vals, qt, top, acc, scores, peaks)
     copies[3].wait()
 
@@ -283,6 +275,10 @@
     vals[blocks] = jnp.zeros(vals.shape[1:], BF16)
     put_blocks(0, rim[...].reshape(blocks * p, width), w_all, keys, vals, [place < plan[3, 1 + by + j] for j in range(blocks)])
     attend(plan, plan[3, 0], keys, vals, qt, top, acc, scores, peaks)
+
+
+def near_kernel(rim, w_all, qt, top_in, acc_in, plan, top, acc, keys, vals, scores, peaks):
+    far_work(rim, w_all, qt, plan, top, acc, keys, vals, scores, peaks)
 
 
 def far_kernel(
@@ -328,7 +324,7 @@
     _, by, bz, p, width = points.shape
     hd = width // HEADS
     groups, depth, lanes = HEADS // 2, 2 * hd, 2 * p
-    split = max(by // 2, 1)
+    split = max(by - 2, 1)
     early = max(split - 1, 1)
     whole = pl.BlockSpec(memory_space=pltpu.VMEM)
     apart = pl.BlockSpec(memory_space=pltpu.HBM)
@@ -397,23 +393,32 @@
         pltpu.VMEM((2 * p, groups * lanes), F32),
         pltpu.VMEM((1, groups * lanes), F32),
     ]
-    qt, top, acc, w_all, w_last, plan0, plan1 = pl.pallas_call(
-        functools.partial(main_kernel, n, split),
+    qt, top, acc, w_all, w_last, plan_near, plan0, plan1 = pl.pallas_call(
+        functools.partial(own_kernel, n, split),
         out_shape=(
             pltpu.VMEM((by, groups, depth, lanes), BF16),
             *state,
             pltpu.VMEM(w_qkv.shape, BF16),
             pltpu.VMEM(w_out.shape, BF16),
-            plan,
-            plan,
+            *(plan,) * 3,
         ),
-        in_specs=[whole, whole, apart, apart, apart, apart],
-        out_specs=(whole,) * 5 + (words,) * 2,
-        scratch_shapes=[*scratch(2 * by), plan, flags, live, *ahead, pltpu.SemaphoreType.DMA((4,))],
-        compiler_params=params,
-        name="main",
-    )(vmem(normed), vmem(near), masks, counts, w_qkv, w_out)
-
+        in_specs=[whole, apart, apart, apart, apart],
+        out_specs=(whole,) * 5 + (words,) * 3,
+        scratch_shapes=[*scratch(by), plan, flags, live, *ahead, pltpu.SemaphoreType.DMA((4,))],
+        compiler_params=params,
+        name="own",
+    )(vmem(normed), masks, counts, w_qkv, w_out)
+    near_work = pl.pallas_call(
+        near_kernel,
+        out_shape=state,
+        in_specs=[*(whole,) * 5, words],
+        out_specs=(whole,) * 2,
+        scratch_shapes=[*scratch(by), *ahead],
+        input_output_aliases={3: 0, 4: 1},
+        compiler_params=params,
+        name="near",
+    )
+    top, acc = near_work(*map(vmem, (near, w_all, qt, top, acc)), smem(plan_near))
     ins = [far0, norm, w_all, qt, top, acc, tiled, w_last]
     top, acc, held = pl.pallas_call(
         far_kernel,

time: 28.3 us -> 28.8 us (1.018)
  the two profiles are of different devices: /device:TPU:1 before, /device:TPU:27 now
where the time goes in v7:
time: 28.8 us; the launch traced here: 28.6 us
  Pallas kernels  18.4 us (64%)
  starting transfers between devices  6.29 us (22%)
  waiting for transfers between devices  3.85 us (13%)
    pallas_call x1, Pallas kernels, shards(): pl.pallas_call(functools.partial(own_kernel, n, split), out_shape=(pltpu....  6.42 us
    ppermute x3, starting transfers between devices, moved(): return lax.ppermute(value, 'gx', pairs)  6.29 us
    pallas_call x1, Pallas kernels, shards(): pl.pallas_call(far_kernel, out_shape=(*state, pltpu.VMEM((early, p, width...  4 us
    ppermute x3, waiting for transfers between devices, moved(): return lax.ppermute(value, 'gx', pairs)  3.85 us
    pallas_call x1, Pallas kernels, shards(): near_work(*map(vmem, (near, w_all, qt, top, acc)), smem(plan_near))  3.07 us
    pallas_call x1, Pallas kernels, shards(): pl.pallas_call(last_kernel, out_shape=(*state, pltpu.HBM((1, by, bz, p, w...  2.73 us
    pallas_call x1, Pallas kernels, shards(): pl.pallas_call(gather_kernel, out_shape=(pltpu.VMEM((split, p, width), BF...  1.53 us
    pallas_call x1, Pallas kernels, shards(): tile_rest(vmem(first), vmem(rest), vmem(places), vmem(norm))  0.65 us
  transfers between devices with their start and end apart: 3, of which 1 were waited for; matrix products, arithmetic and copies ran while one was open for 0% of the time, Pallas kernels for 47%

profile of v7, /device:TPU:27, one launch (start us, length us, event | category | flops | bytes accessed | tf_op | source)
XLA Modules:
  0.0 28.6 jit_solution(10323400782378812740)
XLA Ops:
  0.0 1.5 %gather.1 = (bf16[4,128,512]{2,1,0:T(8,128)(2,1)S(1)}, bf16[2,128,512]{2,1,0:T(8,128)(2,1)S(1)}, s32[2,1,128]{2,1,0:T(1,128)S(1)}, f32[2,512]{1,0:T(2,128)S(1)}) custom-call(bf16[1,6,1,128,512]{4,3,2,1,0:T(8,128)(2,1)} %points.1, s32[1,6,1,128]{3,2,1,0:T(1,128)} %order.1, s32[6,1,16]{2,1,0:T(1,128)} %bitcast.3, f32[1,512]{1,0:T(1,128)} %bitcast.5, ...), custom_call_target="tpu_custom_call" | custom-call | tf_op jit(solution)/shard_map/gather/pallas_call | solution.py:339
  1.5 0.7 %rest.1 = (bf16[6,128,512]{2,1,0:T(8,128)(2,1)S(1)}, bf16[6,128,512]{2,1,0:T(8,128)(2,1)S(1)}, bf16[2,128,512]{2,1,0:T(8,128)(2,1)S(1)}) custom-call(bf16[4,128,512]{2,1,0:T(8,128)(2,1)S(1)} %get-tuple-element.26.first, bf16[2,128,512]{2,1,0:T(8,128)(2,1)S(1)} %get-tuple-element.27.rest, s32[2,1,128]{2,1,0:T(1,128)S(1)} %get-tuple-element.28.places, ...), custom_call_target="tpu_custom_call" | custom-call | tf_op jit(solution)/shard_map/rest/pallas_call | solution.py:370
  2.2 0.7 %collective-permute-start.2 = (bf16[6,128,512]{2,1,0:T(8,128)(2,1)S(1)}, bf16[6,128,512]{2,1,0:T(8,128)(2,1)S(1)}, u32[]{:S(2)}, u32[]{:S(2)}) collective-permute-start(bf16[6,128,512]{2,1,0:T(8,128)(2,1)S(1)} %get-tuple-element.31.own), channel_id=1, source_target_pairs={{0,1},{1,0},{2,3},{3,2},{4,5},{5,4},{6,7},{7,6},{8,9},{9,8},{10,11... | collective-permute-start | bytes 2359304 | tf_op jit(solution)/shard_map/ppermute | solution.py:375
  2.9 3.0 %collective-permute-start.1 = (bf16[4,128,512]{2,1,0:T(8,128)(2,1)S(1)}, bf16[4,128,512]{2,1,0:T(8,128)(2,1)S(1)}, u32[]{:S(2)}, u32[]{:S(2)}) collective-permute-start(bf16[4,128,512]{2,1,0:T(8,128)(2,1)S(1)} %get-tuple-element.26.first), channel_id=1, source_target_pairs={{1,2},{3,4},{5,6},{7,8},{9,10},{11,12},{13,14},{2,1},{4,3},{6,5},{... | collective-permute-start | bytes 1572872 | tf_op jit(solution)/shard_map/ppermute | solution.py:375
  6.0 2.5 %collective-permute-start = (bf16[2,128,512]{2,1,0:T(8,128)(2,1)S(1)}, bf16[2,128,512]{2,1,0:T(8,128)(2,1)S(1)}, u32[]{:S(2)}, u32[]{:S(2)}) collective-permute-start(bf16[2,128,512]{2,1,0:T(8,128)(2,1)S(1)} %get-tuple-element.30), channel_id=1, source_target_pairs={{1,2},{3,4},{5,6},{7,8},{9,10},{11,12},{13,14},{2,1},{4,3},{6,5},{... | collective-permute-start | bytes 786440 | tf_op jit(solution)/shard_map/ppermute | solution.py:375
  8.5 6.4 %own.1 = (bf16[6,4,128,256]{3,2,1,0:T(8,128)(2,1)S(1)}, f32[6,1,1024]{2,1,0:T(1,128)S(1)}, f32[6,72,1024]{2,1,0:T(8,128)S(1)}, bf16[512,1536]{1,0:T(8,128)(2,1)S...) custom-call(bf16[6,128,512]{2,1,0:T(8,128)(2,1)S(1)} %get-tuple-element.31., ...), custom_call_target="tpu_custom_call" | custom-call | tf_op jit(solution)/shard_map/own/pallas_call | solution.py:396
  14.9 0.0 collective-permute-done.2.rim
  14.9 3.1 %near.1 = (f32[6,1,1024]{2,1,0:T(1,128)S(1)}, f32[6,72,1024]{2,1,0:T(8,128)S(1)}) custom-call(bf16[6,128,512]{2,1,0:T(8,128)(2,1)S(1)} %collective-permute-done.2.rim, bf16[512,1536]{1,0:T(8,128)(2,1)S(1)} %get-tuple-element.32.w_all, bf16[6,4,128,256]{3,2,1,0:T(8,128)(2,1)S(1)} %get-tuple-element.33.qt, ...), custom_call_target="tpu_custom_call", output_to_operand_aliasing={{0}: (3, {}), {1}: (4, {})} | custom-call | tf_op jit(solution)/shard_map/near/pallas_call | solution.py:421
  18.0 3.8 %collective-permute-done.1.rim = bf16[4,128,512]{2,1,0:T(8,128)(2,1)S(1)} collective-permute-done((bf16[4,128,512]{2,1,0:T(8,128)(2,1)S(1)}, bf16[4,128,512]{2,1,0:T(8,128)(2,1)S(1)}, u32[]{:S(2)}, u32[]{:S(2)}) %collective-permute-start.1) | collective-permute-done | bytes 524320 | tf_op jit(solution)/shard_map/ppermute | solution.py:375
  21.9 4.0 %far.1 = (f32[6,1,1024]{2,1,0:T(1,128)S(1)}, f32[6,72,1024]{2,1,0:T(8,128)S(1)}, bf16[3,128,512]{2,1,0:T(8,128)(2,1)S(1)}) custom-call(bf16[4,128,512]{2,1,0:T(8,128)(2,1)S(1)} %collective-permute-done.1.rim, f32[2,512]{1,0:T(2,128)S(1)} %get-tuple-element.29.norm, ...), custom_call_target="tpu_custom_call", output_to_operand_aliasing={{0}: (4, {}), {1}: (5, {})} | custom-call | tf_op jit(solution)/shard_map/far/pallas_call | solution.py:423
  25.9 0.0 collective-permute-done.rim
  25.9 2.7 %last.1 = (f32[6,1,1024]{2,1,0:T(1,128)S(1)}, f32[6,72,1024]{2,1,0:T(8,128)S(1)}, bf16[1,6,1,128,512]{4,3,2,1,0:T(8,128)(2,1)}) custom-call(bf16[2,128,512]{2,1,0:T(8,128)(2,1)S(1)} %collective-permute-done.rim, bf16[512,1536]{1,0:T(8,128)(2,1)S(1)} %get-tuple-element.32.w_all, ...), custom_call_target="tpu_custom_call", output_to_operand_aliasing={{0}: (3, {}), {1}: (4, {})} | custom-call | tf_op jit(solution)/shard_map/last/pallas_call | solution.py:434
Async XLA Ops:
  2.2 12.7 %collective-permute-start.2 = (bf16[6,128,512]{2,1,0:T(8,128)(2,1)S(1)}, bf16[6,128,512]{2,1,0:T(8,128)(2,1)S(1)}, u32[]{:S(2)}, u32[]{:S(2)}) collective-permute-start(bf16[6,128,512]{2,1,0:T(8,128)(2,1)S(1)} %get-tuple-element.31.own), channel_id=1, source_target_pairs={{0,1},{1,0},{2,3},{3,2},{4,5},{5,4},{6,7},{7,6},{8,9},{9,8},{10,11... | collective-permute-start | bytes 2359304 | tf_op jit(solution)/shard_map/ppermute | solution.py:375
  2.9 18.9 %collective-permute-start.1 = (bf16[4,128,512]{2,1,0:T(8,128)(2,1)S(1)}, bf16[4,128,512]{2,1,0:T(8,128)(2,1)S(1)}, u32[]{:S(2)}, u32[]{:S(2)}) collective-permute-start(bf16[4,128,512]{2,1,0:T(8,128)(2,1)S(1)} %get-tuple-element.26.first), channel_id=1, source_target_pairs={{1,2},{3,4},{5,6},{7,8},{9,10},{11,12},{13,14},{2,1},{4,3},{6,5},{... | collective-permute-start | bytes 1572872 | tf_op jit(solution)/shard_map/ppermute | solution.py:375
  6.0 19.9 %collective-permute-start = (bf16[2,128,512]{2,1,0:T(8,128)(2,1)S(1)}, bf16[2,128,512]{2,1,0:T(8,128)(2,1)S(1)}, u32[]{:S(2)}, u32[]{:S(2)}) collective-permute-start(bf16[2,128,512]{2,1,0:T(8,128)(2,1)S(1)} %get-tuple-element.30), channel_id=1, source_target_pairs={{1,2},{3,4},{5,6},{7,8},{9,10},{11,12},{13,14},{2,1},{4,3},{6,5},{... | collective-permute-start | bytes 786440 | tf_op jit(solution)/shard_map/ppermute | solution.py:375

commit v8 on v6

--- a/solution.py
+++ b/solution.py
@@ -90,6 +90,10 @@
     return 1 - 2 * (lax.axis_index("gx") & 1)
 
 
+def in_first_class(me):
+    return ((me + 1) >> 1) & 1 == 1
+
+
 def column(side, b):
     index = 9 * (side + 1) + 3 * (b + 1) + 1
     if isinstance(index, int):
@@ -296,13 +300,14 @@
 
 
 def last_kernel(
-    rim, w_all, qt, top_in, acc_in, tiled, w_out, held, plan, top, acc, result, keys, vals, scores, peaks, out,
-    sems
+    rim_a, rim_b, w_all, qt, top_in, acc_in, tiled, w_out, held, plan, top, acc, result, keys, vals, scores, peaks, out,
+    rim, sems
 ):
     by, early = tiled.shape[0], held.shape[0]
     copies = [pltpu.make_async_copy(held.at[i], result.at[0, i, 0], sems.at[i]) for i in range(early)]
     for copy in copies:
         copy.start()
+    rim[...] = jnp.where(in_first_class(lax.axis_index("gx")), rim_a[...], rim_b[...])
     far_work(rim, w_all, qt, plan, top, acc, keys, vals, scores, peaks)
     for i in range(early, by):
         out[i - early] = finish(i, tiled, acc, w_out, plan[3, 1 + i])
@@ -328,7 +333,7 @@
     _, by, bz, p, width = points.shape
     hd = width // HEADS
     groups, depth, lanes = HEADS // 2, 2 * hd, 2 * p
-    split = max(by // 2, 1)
+    split = max(by - 2, 1)
     early = max(split - 1, 1)
     whole = pl.BlockSpec(memory_space=pltpu.VMEM)
     apart = pl.BlockSpec(memory_space=pltpu.HBM)
@@ -380,7 +385,8 @@
 
     far0 = moved(first, far_pairs)
     near = moved(normed, near_pairs)
-    far1 = moved(second, far_pairs)
+    far_a = moved(second, [pair for pair in far_pairs if in_first_class(pair[0])])
+    far_b = moved(second, [pair for pair in far_pairs if not in_first_class(pair[0])])
 
     state = (
         pltpu.VMEM((by, 1, groups * lanes), F32),
@@ -397,7 +403,7 @@
         pltpu.VMEM((2 * p, groups * lanes), F32),
         pltpu.VMEM((1, groups * lanes), F32),
     ]
-    qt, top, acc, w_all, w_last, plan0, plan1 = pl.pallas_call(
+    main = pl.pallas_call(
         functools.partial(main_kernel, n, split),
         out_shape=(
             pltpu.VMEM((by, groups, depth, lanes), BF16),
@@ -412,7 +418,10 @@
         scratch_shapes=[*scratch(2 * by), plan, flags, live, *ahead, pltpu.SemaphoreType.DMA((4,))],
         compiler_params=params,
         name="main",
-    )(vmem(normed), vmem(near), masks, counts, w_qkv, w_out)
+    )
+    qt, top, acc, w_all, w_last, plan0, plan1 = main(
+        vmem(normed), vmem(near), masks, counts, w_qkv, w_out
+    )
 
     ins = [far0, norm, w_all, qt, top, acc, tiled, w_last]
     top, acc, held = pl.pallas_call(
@@ -425,7 +434,7 @@
         compiler_params=params,
         name="far",
     )(*map(vmem, ins), smem(plan0))
-    ins = [far1, w_all, qt, top, acc, tiled, w_last, held]
+    ins = [far_a, far_b, w_all, qt, top, acc, tiled, w_last, held]
     _, _, result = pl.pallas_call(
         last_kernel,
         out_shape=(*state, pltpu.HBM((1, by, bz, p, width), BF16)),
@@ -435,9 +444,10 @@
             *scratch(by - split),
             *ahead,
             pltpu.VMEM((by - early, p, width), BF16),
+            pltpu.VMEM((by - split, p, width), BF16),
             pltpu.SemaphoreType.DMA((by,)),
         ],
-        input_output_aliases={3: 0, 4: 1},
+        input_output_aliases={4: 0, 5: 1},
         compiler_params=params,
         name="last",
     )(*map(vmem, ins), smem(plan1))

time: 28.3 us -> 28.8 us (1.018)
  the two profiles are of different devices: /device:TPU:1 before, /device:TPU:27 now
where the time goes in v8:
time: 28.8 us; the launch traced here: 28.6 us
  Pallas kernels  17.5 us (61%)
  starting transfers between devices  6.97 us (24%)
  waiting for transfers between devices  4.01 us (14%)
    pallas_call x1, Pallas kernels, shards(): main(vmem(normed), vmem(near), masks, counts, w_qkv, w_out)  8.65 us
    ppermute x4, starting transfers between devices, moved(): return lax.ppermute(value, 'gx', pairs)  6.97 us
    ppermute x4, waiting for transfers between devices, moved(): return lax.ppermute(value, 'gx', pairs)  4.01 us
    pallas_call x1, Pallas kernels, shards(): pl.pallas_call(far_kernel, out_shape=(*state, pltpu.VMEM((early, p, width...  3.98 us
    pallas_call x1, Pallas kernels, shards(): pl.pallas_call(last_kernel, out_shape=(*state, pltpu.HBM((1, by, bz, p, w...  2.75 us
    pallas_call x1, Pallas kernels, shards(): pl.pallas_call(gather_kernel, out_shape=(pltpu.VMEM((split, p, width), BF...  1.53 us
    pallas_call x1, Pallas kernels, shards(): tile_rest(vmem(first), vmem(rest), vmem(places), vmem(norm))  0.65 us
  transfers between devices with their start and end apart: 4, of which 1 were waited for; matrix products, arithmetic and copies ran while one was open for 0% of the time, Pallas kernels for 44%

profile of v8, /device:TPU:27, one launch (start us, length us, event | category | flops | bytes accessed | tf_op | source)
XLA Modules:
  0.0 28.6 jit_solution(3718704740444001116)
XLA Ops:
  0.0 1.5 %gather.1 = (bf16[4,128,512]{2,1,0:T(8,128)(2,1)S(1)}, bf16[2,128,512]{2,1,0:T(8,128)(2,1)S(1)}, s32[2,1,128]{2,1,0:T(1,128)S(1)}, f32[2,512]{1,0:T(2,128)S(1)}) custom-call(bf16[1,6,1,128,512]{4,3,2,1,0:T(8,128)(2,1)} %points.1, s32[1,6,1,128]{3,2,1,0:T(1,128)} %order.1, s32[6,1,16]{2,1,0:T(1,128)} %bitcast.3, f32[1,512]{1,0:T(1,128)} %bitcast.5, ...), custom_call_target="tpu_custom_call" | custom-call | tf_op jit(solution)/shard_map/gather/pallas_call | solution.py:348
  1.5 0.6 %rest.1 = (bf16[6,128,512]{2,1,0:T(8,128)(2,1)S(1)}, bf16[6,128,512]{2,1,0:T(8,128)(2,1)S(1)}, bf16[2,128,512]{2,1,0:T(8,128)(2,1)S(1)}) custom-call(bf16[4,128,512]{2,1,0:T(8,128)(2,1)S(1)} %get-tuple-element.23.first, bf16[2,128,512]{2,1,0:T(8,128)(2,1)S(1)} %get-tuple-element.24.rest, s32[2,1,128]{2,1,0:T(1,128)S(1)} %get-tuple-element.25.places, ...), custom_call_target="tpu_custom_call" | custom-call | tf_op jit(solution)/shard_map/rest/pallas_call | solution.py:379
  2.2 0.7 %collective-permute-start.2 = (bf16[6,128,512]{2,1,0:T(8,128)(2,1)S(1)}, bf16[6,128,512]{2,1,0:T(8,128)(2,1)S(1)}, u32[]{:S(2)}, u32[]{:S(2)}) collective-permute-start(bf16[6,128,512]{2,1,0:T(8,128)(2,1)S(1)} %get-tuple-element.28.own), channel_id=1, source_target_pairs={{0,1},{1,0},{2,3},{3,2},{4,5},{5,4},{6,7},{7,6},{8,9},{9,8},{10,11... | collective-permute-start | bytes 2359304 | tf_op jit(solution)/shard_map/ppermute | solution.py:384
  2.9 3.0 %collective-permute-start.3 = (bf16[4,128,512]{2,1,0:T(8,128)(2,1)S(1)}, bf16[4,128,512]{2,1,0:T(8,128)(2,1)S(1)}, u32[]{:S(2)}, u32[]{:S(2)}) collective-permute-start(bf16[4,128,512]{2,1,0:T(8,128)(2,1)S(1)} %get-tuple-element.23.first), channel_id=1, source_target_pairs={{1,2},{3,4},{5,6},{7,8},{9,10},{11,12},{13,14},{2,1},{4,3},{6,5},{... | collective-permute-start | bytes 1572872 | tf_op jit(solution)/shard_map/ppermute | solution.py:384
  6.0 0.7 %collective-permute-start.1 = (bf16[2,128,512]{2,1,0:T(8,128)(2,1)S(1)}, bf16[2,128,512]{2,1,0:T(8,128)(2,1)S(1)}, u32[]{:S(2)}, u32[]{:S(2)}) collective-permute-start(bf16[2,128,512]{2,1,0:T(8,128)(2,1)S(1)} %get-tuple-element.27), channel_id=1, source_target_pairs={{3,4},{7,8},{11,12},{4,3},{8,7},{12,11},{19,20},{23,24},{27,28},{2... | collective-permute-start | bytes 786440 | tf_op jit(solution)/shard_map/ppermute | solution.py:384
  6.7 2.5 %collective-permute-start = (bf16[2,128,512]{2,1,0:T(8,128)(2,1)S(1)}, bf16[2,128,512]{2,1,0:T(8,128)(2,1)S(1)}, u32[]{:S(2)}, u32[]{:S(2)}) collective-permute-start(bf16[2,128,512]{2,1,0:T(8,128)(2,1)S(1)} %get-tuple-element.27), channel_id=1, source_target_pairs={{1,2},{5,6},{9,10},{13,14},{2,1},{6,5},{10,9},{14,13},{17,18},{21,... | collective-permute-start | bytes 786440 | tf_op jit(solution)/shard_map/ppermute | solution.py:384
  9.2 0.0 collective-permute-done.2.near
  9.2 8.6 %main.1 = (bf16[6,4,128,256]{3,2,1,0:T(8,128)(2,1)S(1)}, f32[6,1,1024]{2,1,0:T(1,128)S(1)}, f32[6,72,1024]{2,1,0:T(8,128)S(1)}, bf16[512,1536]{1,0:T(8,128)(2,1)...) custom-call(bf16[6,128,512]{2,1,0:T(8,128)(2,1)S(1)} %get-tuple-element.28.own, ...), custom_call_target="tpu_custom_call" | custom-call | tf_op jit(solution)/shard_map/main/pallas_call | solution.py:422
  17.8 4.0 %collective-permute-done.3.rim = bf16[4,128,512]{2,1,0:T(8,128)(2,1)S(1)} collective-permute-done((bf16[4,128,512]{2,1,0:T(8,128)(2,1)S(1)}, bf16[4,128,512]{2,1,0:T(8,128)(2,1)S(1)}, u32[]{:S(2)}, u32[]{:S(2)}) %collective-permute-start.3) | collective-permute-done | bytes 524320 | tf_op jit(solution)/shard_map/ppermute | solution.py:384
  21.8 4.0 %far.1 = (f32[6,1,1024]{2,1,0:T(1,128)S(1)}, f32[6,72,1024]{2,1,0:T(8,128)S(1)}, bf16[3,128,512]{2,1,0:T(8,128)(2,1)S(1)}) custom-call(bf16[4,128,512]{2,1,0:T(8,128)(2,1)S(1)} %collective-permute-done.3.rim, f32[2,512]{1,0:T(2,128)S(1)} %get-tuple-element.26.norm, ...), custom_call_target="tpu_custom_call", output_to_operand_aliasing={{0}: (4, {}), {1}: (5, {})} | custom-call | tf_op jit(solution)/shard_map/far/pallas_call | solution.py:427
  25.8 0.0 collective-permute-done.1.rim_b
  25.8 0.0 collective-permute-done.rim_a
  25.9 2.7 %last.1 = (f32[6,1,1024]{2,1,0:T(1,128)S(1)}, f32[6,72,1024]{2,1,0:T(8,128)S(1)}, bf16[1,6,1,128,512]{4,3,2,1,0:T(8,128)(2,1)}) custom-call(bf16[2,128,512]{2,1,0:T(8,128)(2,1)S(1)} %collective-permute-done.rim_a, bf16[2,128,512]{2,1,0:T(8,128)(2,1)S(1)} %collective-permute-done.1.rim_b, ...), custom_call_target="tpu_custom_call", output_to_operand_aliasing={{0}: (4, {}), {1}: (5, {})} | custom-call | tf_op jit(solution)/shard_map/last/pallas_call | solution.py:438
Async XLA Ops:
  2.2 7.0 %collective-permute-start.2 = (bf16[6,128,512]{2,1,0:T(8,128)(2,1)S(1)}, bf16[6,128,512]{2,1,0:T(8,128)(2,1)S(1)}, u32[]{:S(2)}, u32[]{:S(2)}) collective-permute-start(bf16[6,128,512]{2,1,0:T(8,128)(2,1)S(1)} %get-tuple-element.28.own), channel_id=1, source_target_pairs={{0,1},{1,0},{2,3},{3,2},{4,5},{5,4},{6,7},{7,6},{8,9},{9,8},{10,11... | collective-permute-start | bytes 2359304 | tf_op jit(solution)/shard_map/ppermute | solution.py:384
  2.9 18.9 %collective-permute-start.3 = (bf16[4,128,512]{2,1,0:T(8,128)(2,1)S(1)}, bf16[4,128,512]{2,1,0:T(8,128)(2,1)S(1)}, u32[]{:S(2)}, u32[]{:S(2)}) collective-permute-start(bf16[4,128,512]{2,1,0:T(8,128)(2,1)S(1)} %get-tuple-element.23.first), channel_id=1, source_target_pairs={{1,2},{3,4},{5,6},{7,8},{9,10},{11,12},{13,14},{2,1},{4,3},{6,5},{... | collective-permute-start | bytes 1572872 | tf_op jit(solution)/shard_map/ppermute | solution.py:384
  6.0 19.9 %collective-permute-start.1 = (bf16[2,128,512]{2,1,0:T(8,128)(2,1)S(1)}, bf16[2,128,512]{2,1,0:T(8,128)(2,1)S(1)}, u32[]{:S(2)}, u32[]{:S(2)}) collective-permute-start(bf16[2,128,512]{2,1,0:T(8,128)(2,1)S(1)} %get-tuple-element.27), channel_id=1, source_target_pairs={{3,4},{7,8},{11,12},{4,3},{8,7},{12,11},{19,20},{23,24},{27,28},{2... | collective-permute-start | bytes 786440 | tf_op jit(solution)/shard_map/ppermute | solution.py:384
  6.7 19.2 %collective-permute-start = (bf16[2,128,512]{2,1,0:T(8,128)(2,1)S(1)}, bf16[2,128,512]{2,1,0:T(8,128)(2,1)S(1)}, u32[]{:S(2)}, u32[]{:S(2)}) collective-permute-start(bf16[2,128,512]{2,1,0:T(8,128)(2,1)S(1)} %get-tuple-element.27), channel_id=1, source_target_pairs={{1,2},{5,6},{9,10},{13,14},{2,1},{6,5},{10,9},{14,13},{17,18},{21,... | collective-permute-start | bytes 786440 | tf_op jit(solution)/shard_map/ppermute | solution.py:384

commit v9 on v8

--- a/solution.py
+++ b/solution.py
@@ -136,7 +136,7 @@
     return pairs, ends
 
 
-def attend(items, high, keys, vals, qt, top, acc, scores, peaks):
+def attend(items, low, high, keys, vals, qt, top, acc, scores, peaks):
     groups, depth, lanes = qt.shape[1:]
     hd, p = depth // 2, lanes // 2
 
@@ -183,8 +183,8 @@
         return carry
 
     for g in range(lead):
-        score(0, g)
-    lax.fori_loop(0, high, step, 0)
+        score(low, g)
+    lax.fori_loop(low, high, step, 0)
 
 
 def put_values(vals, tile, g0, v, live):
@@ -223,8 +223,8 @@
 
 
 def main_kernel(
-    n, split, own, near, masks, counts, w_qkv, w_out, qt, top, acc, w_all, w_last, plan0, plan1, keys, vals,
-    items, flags, live, scores, peaks, sems
+    n, split, own, near, masks, counts, w_qkv, w_out, qt, top, acc, w_all, w_last, plan0, plan1, keys, vals, items,
+    flags, live, scores, peaks, sems
 ):
     by, p, width = own.shape
     _, depth = qt.shape[1:3]
@@ -276,8 +276,14 @@
                 qt[i, g, hd:, p:] = t[mid : mid + hd]
     put_blocks(0, mine, w_all, keys, vals, [place < live[i, 0, me] for i in range(by)])
     put_blocks(by, theirs, w_all, keys, vals, [place < live[i, 0, slab] for i in range(by)])
-    attend(items, pairs, keys, vals, qt, top, acc, scores, peaks)
+    items[3, 0] = (pairs * 11) >> 4
+    items[3, 1] = pairs
+    attend(items, 0, items[3, 0], keys, vals, qt, top, acc, scores, peaks)
     copies[3].wait()
+
+
+def more_kernel(qt, keys, vals, top_in, acc_in, items, top, acc, scores, peaks):
+    attend(items, items[3, 0], items[3, 1], keys, vals, qt, top, acc, scores, peaks)
 
 
 def far_work(rim, w_all, qt, plan, top, acc, keys, vals, scores, peaks):
@@ -286,7 +292,7 @@
     place = lax.broadcasted_iota(jnp.int32, (1, p), 1)
     vals[blocks] = jnp.zeros(vals.shape[1:], BF16)
     put_blocks(0, rim[...].reshape(blocks * p, width), w_all, keys, vals, [place < plan[3, 1 + by + j] for j in range(blocks)])
-    attend(plan, plan[3, 0], keys, vals, qt, top, acc, scores, peaks)
+    attend(plan, 0, plan[3, 0], keys, vals, qt, top, acc, scores, peaks)
 
 
 def far_kernel(
@@ -412,17 +418,29 @@
             pltpu.VMEM(w_out.shape, BF16),
             plan,
             plan,
+            *scratch(2 * by),
+            plan,
         ),
         in_specs=[whole, whole, apart, apart, apart, apart],
-        out_specs=(whole,) * 5 + (words,) * 2,
-        scratch_shapes=[*scratch(2 * by), plan, flags, live, *ahead, pltpu.SemaphoreType.DMA((4,))],
+        out_specs=(*(whole,) * 5, words, words, whole, whole, words),
+        scratch_shapes=[flags, live, *ahead, pltpu.SemaphoreType.DMA((4,))],
         compiler_params=params,
         name="main",
     )
-    qt, top, acc, w_all, w_last, plan0, plan1 = main(
+    more = pl.pallas_call(
+        more_kernel,
+        out_shape=state,
+        in_specs=[*(whole,) * 5, words],
+        out_specs=(whole,) * 2,
+        scratch_shapes=ahead,
+        input_output_aliases={3: 0, 4: 1},
+        compiler_params=params,
+        name="more",
+    )
+    qt, top, acc, w_all, w_last, plan0, plan1, keys, vals, items = main(
         vmem(normed), vmem(near), masks, counts, w_qkv, w_out
     )
-
+    top, acc = more(*map(vmem, (qt, keys, vals, top, acc)), smem(items))
     ins = [far0, norm, w_all, qt, top, acc, tiled, w_last]
     top, acc, held = pl.pallas_call(
         far_kernel,

time: 28.8 us -> 28.9 us (level)
  Pallas kernels: 17.5 us -> 17.9 us
  waiting for transfers between devices: 4.01 us -> 3.66 us
    pallas_call x0 -> x1, Pallas kernels: none -> 2.14 us  [shards(): top, acc = more(*map(vmem, (qt, keys, vals, top, acc)), smem(items))]
    pallas_call x1, Pallas kernels: 8.65 us -> 6.85 us  [shards(): main(vmem(normed), vmem(near), masks, counts, w_qkv, w_out)]
    ppermute x4, waiting for transfers between devices: 4.01 us -> 3.66 us  [moved(): return lax.ppermute(value, 'gx', pairs)]
  transfers between devices with their start and end apart: 4 -> 4, of which waited for: 1 -> 1; matrix products, arithmetic and copies ran while one was open for 0% -> 0% of each run, Pallas kernels for 44% -> 45%
where the time goes in v9:
time: 28.9 us; the launch traced here: 28.7 us
  Pallas kernels  17.9 us (62%)
  starting transfers between devices  6.97 us (24%)
  waiting for transfers between devices  3.66 us (13%)
    ppermute x4, starting transfers between devices, moved(): return lax.ppermute(value, 'gx', pairs)  6.97 us
    pallas_call x1, Pallas kernels, shards(): main(vmem(normed), vmem(near), masks, counts, w_qkv, w_out)  6.85 us
    pallas_call x1, Pallas kernels, shards(): pl.pallas_call(far_kernel, out_shape=(*state, pltpu.VMEM((early, p, width...  4.02 us
    ppermute x4, waiting for transfers between devices, moved(): return lax.ppermute(value, 'gx', pairs)  3.66 us
    pallas_call x1, Pallas kernels, shards(): pl.pallas_call(last_kernel, out_shape=(*state, pltpu.HBM((1, by, bz, p, w...  2.76 us
    pallas_call x1, Pallas kernels, shards(): top, acc = more(*map(vmem, (qt, keys, vals, top, acc)), smem(items))  2.14 us
    pallas_call x1, Pallas kernels, shards(): pl.pallas_call(gather_kernel, out_shape=(pltpu.VMEM((split, p, width), BF...  1.53 us
    pallas_call x1, Pallas kernels, shards(): tile_rest(vmem(first), vmem(rest), vmem(places), vmem(norm))  0.65 us
  transfers between devices with their start and end apart: 4, of which 1 were waited for; matrix products, arithmetic and copies ran while one was open for 0% of the time, Pallas kernels for 45%

profile of v9, /device:TPU:27, one launch (start us, length us, event | category | flops | bytes accessed | tf_op | source)
XLA Modules:
  0.0 28.7 jit_solution(15643644604612299729)
XLA Ops:
  0.0 1.5 %gather.1 = (bf16[4,128,512]{2,1,0:T(8,128)(2,1)S(1)}, bf16[2,128,512]{2,1,0:T(8,128)(2,1)S(1)}, s32[2,1,128]{2,1,0:T(1,128)S(1)}, f32[2,512]{1,0:T(2,128)S(1)}) custom-call(bf16[1,6,1,128,512]{4,3,2,1,0:T(8,128)(2,1)} %points.1, s32[1,6,1,128]{3,2,1,0:T(1,128)} %order.1, s32[6,1,16]{2,1,0:T(1,128)} %bitcast.3, f32[1,512]{1,0:T(1,128)} %bitcast.5, ...), custom_call_target="tpu_custom_call" | custom-call | tf_op jit(solution)/shard_map/gather/pallas_call | solution.py:354
  1.5 0.6 %rest.1 = (bf16[6,128,512]{2,1,0:T(8,128)(2,1)S(1)}, bf16[6,128,512]{2,1,0:T(8,128)(2,1)S(1)}, bf16[2,128,512]{2,1,0:T(8,128)(2,1)S(1)}) custom-call(bf16[4,128,512]{2,1,0:T(8,128)(2,1)S(1)} %get-tuple-element.28.first, bf16[2,128,512]{2,1,0:T(8,128)(2,1)S(1)} %get-tuple-element.29.rest, s32[2,1,128]{2,1,0:T(1,128)S(1)} %get-tuple-element.30.places, ...), custom_call_target="tpu_custom_call" | custom-call | tf_op jit(solution)/shard_map/rest/pallas_call | solution.py:385
  2.2 0.7 %collective-permute-start.2 = (bf16[6,128,512]{2,1,0:T(8,128)(2,1)S(1)}, bf16[6,128,512]{2,1,0:T(8,128)(2,1)S(1)}, u32[]{:S(2)}, u32[]{:S(2)}) collective-permute-start(bf16[6,128,512]{2,1,0:T(8,128)(2,1)S(1)} %get-tuple-element.33.own), channel_id=1, source_target_pairs={{0,1},{1,0},{2,3},{3,2},{4,5},{5,4},{6,7},{7,6},{8,9},{9,8},{10,11... | collective-permute-start | bytes 2359304 | tf_op jit(solution)/shard_map/ppermute | solution.py:390
  2.9 3.0 %collective-permute-start.3 = (bf16[4,128,512]{2,1,0:T(8,128)(2,1)S(1)}, bf16[4,128,512]{2,1,0:T(8,128)(2,1)S(1)}, u32[]{:S(2)}, u32[]{:S(2)}) collective-permute-start(bf16[4,128,512]{2,1,0:T(8,128)(2,1)S(1)} %get-tuple-element.28.first), channel_id=1, source_target_pairs={{1,2},{3,4},{5,6},{7,8},{9,10},{11,12},{13,14},{2,1},{4,3},{6,5},{... | collective-permute-start | bytes 1572872 | tf_op jit(solution)/shard_map/ppermute | solution.py:390
  6.0 2.5 %collective-permute-start = (bf16[2,128,512]{2,1,0:T(8,128)(2,1)S(1)}, bf16[2,128,512]{2,1,0:T(8,128)(2,1)S(1)}, u32[]{:S(2)}, u32[]{:S(2)}) collective-permute-start(bf16[2,128,512]{2,1,0:T(8,128)(2,1)S(1)} %get-tuple-element.32), channel_id=1, source_target_pairs={{1,2},{5,6},{9,10},{13,14},{2,1},{6,5},{10,9},{14,13},{17,18},{21,... | collective-permute-start | bytes 786440 | tf_op jit(solution)/shard_map/ppermute | solution.py:390
  8.5 0.7 %collective-permute-start.1 = (bf16[2,128,512]{2,1,0:T(8,128)(2,1)S(1)}, bf16[2,128,512]{2,1,0:T(8,128)(2,1)S(1)}, u32[]{:S(2)}, u32[]{:S(2)}) collective-permute-start(bf16[2,128,512]{2,1,0:T(8,128)(2,1)S(1)} %get-tuple-element.32), channel_id=1, source_target_pairs={{3,4},{7,8},{11,12},{4,3},{8,7},{12,11},{19,20},{23,24},{27,28},{2... | collective-permute-start | bytes 786440 | tf_op jit(solution)/shard_map/ppermute | solution.py:390
  9.2 0.0 collective-permute-done.2.near
  9.2 6.8 %main.1 = (bf16[6,4,128,256]{3,2,1,0:T(8,128)(2,1)S(1)}, f32[6,1,1024]{2,1,0:T(1,128)S(1)}, f32[6,72,1024]{2,1,0:T(8,128)S(1)}, bf16[512,1536]{1,0:T(8,128)(2,1)...) custom-call(bf16[6,128,512]{2,1,0:T(8,128)(2,1)S(1)} %get-tuple-elem, ...), custom_call_target="tpu_custom_call" | custom-call | tf_op jit(solution)/shard_map/main/pallas_call | solution.py:440
  16.0 2.1 %more.1 = (f32[6,1,1024]{2,1,0:T(1,128)S(1)}, f32[6,72,1024]{2,1,0:T(8,128)S(1)}) custom-call(bf16[6,4,128,256]{3,2,1,0:T(8,128)(2,1)S(1)} %get-tuple-element.35.qt, bf16[12,128,512]{2,1,0:T(8,128)(2,1)S(1)} %get-tuple-element.36.keys, bf16[13,4,160,128]{3,2,1,0:T(8,128)(2,1)S(1)} %get-tuple-element.37.vals, ...), custom_call_target="tpu_custom_call", output_to_operand_aliasing={{0}: (3, {}), {1}: (4, {})} | custom-call | tf_op jit(solution)/shard_map/more/pallas_call | solution.py:443
  18.2 3.7 %collective-permute-done.3.rim = bf16[4,128,512]{2,1,0:T(8,128)(2,1)S(1)} collective-permute-done((bf16[4,128,512]{2,1,0:T(8,128)(2,1)S(1)}, bf16[4,128,512]{2,1,0:T(8,128)(2,1)S(1)}, u32[]{:S(2)}, u32[]{:S(2)}) %collective-permute-start.3) | collective-permute-done | bytes 524320 | tf_op jit(solution)/shard_map/ppermute | solution.py:390
  21.8 4.0 %far.1 = (f32[6,1,1024]{2,1,0:T(1,128)S(1)}, f32[6,72,1024]{2,1,0:T(8,128)S(1)}, bf16[3,128,512]{2,1,0:T(8,128)(2,1)S(1)}) custom-call(bf16[4,128,512]{2,1,0:T(8,128)(2,1)S(1)} %collective-permute-done.3.rim, f32[2,512]{1,0:T(2,128)S(1)} %get-tuple-element.31.norm, ...), custom_call_target="tpu_custom_call", output_to_operand_aliasing={{0}: (4, {}), {1}: (5, {})} | custom-call | tf_op jit(solution)/shard_map/far/pallas_call | solution.py:445
  25.9 0.0 collective-permute-done.rim_a
  25.9 0.0 collective-permute-done.1.rim_b
  25.9 2.8 %last.1 = (f32[6,1,1024]{2,1,0:T(1,128)S(1)}, f32[6,72,1024]{2,1,0:T(8,128)S(1)}, bf16[1,6,1,128,512]{4,3,2,1,0:T(8,128)(2,1)}) custom-call(bf16[2,128,512]{2,1,0:T(8,128)(2,1)S(1)} %collective-permute-done.rim_a, bf16[2,128,512]{2,1,0:T(8,128)(2,1)S(1)} %collective-permute-done.1.rim_b, ...), custom_call_target="tpu_custom_call", output_to_operand_aliasing={{0}: (4, {}), {1}: (5, {})} | custom-call | tf_op jit(solution)/shard_map/last/pallas_call | solution.py:456
Async XLA Ops:
  2.2 7.0 %collective-permute-start.2 = (bf16[6,128,512]{2,1,0:T(8,128)(2,1)S(1)}, bf16[6,128,512]{2,1,0:T(8,128)(2,1)S(1)}, u32[]{:S(2)}, u32[]{:S(2)}) collective-permute-start(bf16[6,128,512]{2,1,0:T(8,128)(2,1)S(1)} %get-tuple-element.33.own), channel_id=1, source_target_pairs={{0,1},{1,0},{2,3},{3,2},{4,5},{5,4},{6,7},{7,6},{8,9},{9,8},{10,11... | collective-permute-start | bytes 2359304 | tf_op jit(solution)/shard_map/ppermute | solution.py:390
  2.9 18.9 %collective-permute-start.3 = (bf16[4,128,512]{2,1,0:T(8,128)(2,1)S(1)}, bf16[4,128,512]{2,1,0:T(8,128)(2,1)S(1)}, u32[]{:S(2)}, u32[]{:S(2)}) collective-permute-start(bf16[4,128,512]{2,1,0:T(8,128)(2,1)S(1)} %get-tuple-element.28.first), channel_id=1, source_target_pairs={{1,2},{3,4},{5,6},{7,8},{9,10},{11,12},{13,14},{2,1},{4,3},{6,5},{... | collective-permute-start | bytes 1572872 | tf_op jit(solution)/shard_map/ppermute | solution.py:390
  6.0 19.9 %collective-permute-start = (bf16[2,128,512]{2,1,0:T(8,128)(2,1)S(1)}, bf16[2,128,512]{2,1,0:T(8,128)(2,1)S(1)}, u32[]{:S(2)}, u32[]{:S(2)}) collective-permute-start(bf16[2,128,512]{2,1,0:T(8,128)(2,1)S(1)} %get-tuple-element.32), channel_id=1, source_target_pairs={{1,2},{5,6},{9,10},{13,14},{2,1},{6,5},{10,9},{14,13},{17,18},{21,... | collective-permute-start | bytes 786440 | tf_op jit(solution)/shard_map/ppermute | solution.py:390
  8.5 17.4 %collective-permute-start.1 = (bf16[2,128,512]{2,1,0:T(8,128)(2,1)S(1)}, bf16[2,128,512]{2,1,0:T(8,128)(2,1)S(1)}, u32[]{:S(2)}, u32[]{:S(2)}) collective-permute-start(bf16[2,128,512]{2,1,0:T(8,128)(2,1)S(1)} %get-tuple-element.32), channel_id=1, source_target_pairs={{3,4},{7,8},{11,12},{4,3},{8,7},{12,11},{19,20},{23,24},{27,28},{2... | collective-permute-start | bytes 786440 | tf_op jit(solution)/shard_map/ppermute | solution.py:390

commit v10 on v7

--- a/solution.py
+++ b/solution.py
@@ -393,7 +393,7 @@
         pltpu.VMEM((2 * p, groups * lanes), F32),
         pltpu.VMEM((1, groups * lanes), F32),
     ]
-    qt, top, acc, w_all, w_last, plan_near, plan0, plan1 = pl.pallas_call(
+    own_work = pl.pallas_call(
         functools.partial(own_kernel, n, split),
         out_shape=(
             pltpu.VMEM((by, groups, depth, lanes), BF16),
@@ -407,7 +407,7 @@
         scratch_shapes=[*scratch(by), plan, flags, live, *ahead, pltpu.SemaphoreType.DMA((4,))],
         compiler_params=params,
         name="own",
-    )(vmem(normed), masks, counts, w_qkv, w_out)
+    )
     near_work = pl.pallas_call(
         near_kernel,
         out_shape=state,
@@ -417,6 +417,9 @@
         input_output_aliases={3: 0, 4: 1},
         compiler_params=params,
         name="near",
+    )
+    qt, top, acc, w_all, w_last, plan_near, plan0, plan1 = own_work(
+        vmem(normed), masks, counts, w_qkv, w_out
     )
     top, acc = near_work(*map(vmem, (near, w_all, qt, top, acc)), smem(plan_near))
     ins = [far0, norm, w_all, qt, top, acc, tiled, w_last]

time: 28.8 us -> 28.8 us (level)
  no operation moved by 1% of the time
where the time goes in v10:
time: 28.8 us; the launch traced here: 28.6 us
  Pallas kernels  18.4 us (64%)
  starting transfers between devices  6.29 us (22%)
  waiting for transfers between devices  3.85 us (13%)
    pallas_call x1, Pallas kernels, shards(): own_work(vmem(normed), masks, counts, w_qkv, w_out)  6.42 us
    ppermute x3, starting transfers between devices, moved(): return lax.ppermute(value, 'gx', pairs)  6.29 us
    pallas_call x1, Pallas kernels, shards(): pl.pallas_call(far_kernel, out_shape=(*state, pltpu.VMEM((early, p, width...  4 us
    ppermute x3, waiting for transfers between devices, moved(): return lax.ppermute(value, 'gx', pairs)  3.85 us
    pallas_call x1, Pallas kernels, shards(): near_work(*map(vmem, (near, w_all, qt, top, acc)), smem(plan_near))  3.07 us
    pallas_call x1, Pallas kernels, shards(): pl.pallas_call(last_kernel, out_shape=(*state, pltpu.HBM((1, by, bz, p, w...  2.73 us
    pallas_call x1, Pallas kernels, shards(): pl.pallas_call(gather_kernel, out_shape=(pltpu.VMEM((split, p, width), BF...  1.53 us
    pallas_call x1, Pallas kernels, shards(): tile_rest(vmem(first), vmem(rest), vmem(places), vmem(norm))  0.65 us
  transfers between devices with their start and end apart: 3, of which 1 were waited for; matrix products, arithmetic and copies ran while one was open for 0% of the time, Pallas kernels for 47%

profile of v10, /device:TPU:27, one launch (start us, length us, event | category | flops | bytes accessed | tf_op | source)
XLA Modules:
  0.0 28.6 jit_solution(10323400782378812740)
XLA Ops:
  0.0 1.5 %gather.1 = (bf16[4,128,512]{2,1,0:T(8,128)(2,1)S(1)}, bf16[2,128,512]{2,1,0:T(8,128)(2,1)S(1)}, s32[2,1,128]{2,1,0:T(1,128)S(1)}, f32[2,512]{1,0:T(2,128)S(1)}) custom-call(bf16[1,6,1,128,512]{4,3,2,1,0:T(8,128)(2,1)} %points.1, s32[1,6,1,128]{3,2,1,0:T(1,128)} %order.1, s32[6,1,16]{2,1,0:T(1,128)} %bitcast.3, f32[1,512]{1,0:T(1,128)} %bitcast.5, ...), custom_call_target="tpu_custom_call" | custom-call | tf_op jit(solution)/shard_map/gather/pallas_call | solution.py:339
  1.5 0.7 %rest.1 = (bf16[6,128,512]{2,1,0:T(8,128)(2,1)S(1)}, bf16[6,128,512]{2,1,0:T(8,128)(2,1)S(1)}, bf16[2,128,512]{2,1,0:T(8,128)(2,1)S(1)}) custom-call(bf16[4,128,512]{2,1,0:T(8,128)(2,1)S(1)} %get-tuple-element.26.first, bf16[2,128,512]{2,1,0:T(8,128)(2,1)S(1)} %get-tuple-element.27.rest, s32[2,1,128]{2,1,0:T(1,128)S(1)} %get-tuple-element.28.places, ...), custom_call_target="tpu_custom_call" | custom-call | tf_op jit(solution)/shard_map/rest/pallas_call | solution.py:370
  2.2 0.7 %collective-permute-start.2 = (bf16[6,128,512]{2,1,0:T(8,128)(2,1)S(1)}, bf16[6,128,512]{2,1,0:T(8,128)(2,1)S(1)}, u32[]{:S(2)}, u32[]{:S(2)}) collective-permute-start(bf16[6,128,512]{2,1,0:T(8,128)(2,1)S(1)} %get-tuple-element.31.own), channel_id=1, source_target_pairs={{0,1},{1,0},{2,3},{3,2},{4,5},{5,4},{6,7},{7,6},{8,9},{9,8},{10,11... | collective-permute-start | bytes 2359304 | tf_op jit(solution)/shard_map/ppermute | solution.py:375
  2.9 3.0 %collective-permute-start.1 = (bf16[4,128,512]{2,1,0:T(8,128)(2,1)S(1)}, bf16[4,128,512]{2,1,0:T(8,128)(2,1)S(1)}, u32[]{:S(2)}, u32[]{:S(2)}) collective-permute-start(bf16[4,128,512]{2,1,0:T(8,128)(2,1)S(1)} %get-tuple-element.26.first), channel_id=1, source_target_pairs={{1,2},{3,4},{5,6},{7,8},{9,10},{11,12},{13,14},{2,1},{4,3},{6,5},{... | collective-permute-start | bytes 1572872 | tf_op jit(solution)/shard_map/ppermute | solution.py:375
  6.0 2.5 %collective-permute-start = (bf16[2,128,512]{2,1,0:T(8,128)(2,1)S(1)}, bf16[2,128,512]{2,1,0:T(8,128)(2,1)S(1)}, u32[]{:S(2)}, u32[]{:S(2)}) collective-permute-start(bf16[2,128,512]{2,1,0:T(8,128)(2,1)S(1)} %get-tuple-element.30), channel_id=1, source_target_pairs={{1,2},{3,4},{5,6},{7,8},{9,10},{11,12},{13,14},{2,1},{4,3},{6,5},{... | collective-permute-start | bytes 786440 | tf_op jit(solution)/shard_map/ppermute | solution.py:375
  8.5 6.4 %own.1 = (bf16[6,4,128,256]{3,2,1,0:T(8,128)(2,1)S(1)}, f32[6,1,1024]{2,1,0:T(1,128)S(1)}, f32[6,72,1024]{2,1,0:T(8,128)S(1)}, bf16[512,1536]{1,0:T(8,128)(2,1)S...) custom-call(bf16[6,128,512]{2,1,0:T(8,128)(2,1)S(1)} %get-tuple-element.31., ...), custom_call_target="tpu_custom_call" | custom-call | tf_op jit(solution)/shard_map/own/pallas_call | solution.py:421
  14.9 0.0 collective-permute-done.2.rim
  14.9 3.1 %near.1 = (f32[6,1,1024]{2,1,0:T(1,128)S(1)}, f32[6,72,1024]{2,1,0:T(8,128)S(1)}) custom-call(bf16[6,128,512]{2,1,0:T(8,128)(2,1)S(1)} %collective-permute-done.2.rim, bf16[512,1536]{1,0:T(8,128)(2,1)S(1)} %get-tuple-element.32.w_all, bf16[6,4,128,256]{3,2,1,0:T(8,128)(2,1)S(1)} %get-tuple-element.33.qt, ...), custom_call_target="tpu_custom_call", output_to_operand_aliasing={{0}: (3, {}), {1}: (4, {})} | custom-call | tf_op jit(solution)/shard_map/near/pallas_call | solution.py:424
  18.0 3.8 %collective-permute-done.1.rim = bf16[4,128,512]{2,1,0:T(8,128)(2,1)S(1)} collective-permute-done((bf16[4,128,512]{2,1,0:T(8,128)(2,1)S(1)}, bf16[4,128,512]{2,1,0:T(8,128)(2,1)S(1)}, u32[]{:S(2)}, u32[]{:S(2)}) %collective-permute-start.1) | collective-permute-done | bytes 524320 | tf_op jit(solution)/shard_map/ppermute | solution.py:375
  21.9 4.0 %far.1 = (f32[6,1,1024]{2,1,0:T(1,128)S(1)}, f32[6,72,1024]{2,1,0:T(8,128)S(1)}, bf16[3,128,512]{2,1,0:T(8,128)(2,1)S(1)}) custom-call(bf16[4,128,512]{2,1,0:T(8,128)(2,1)S(1)} %collective-permute-done.1.rim, f32[2,512]{1,0:T(2,128)S(1)} %get-tuple-element.29.norm, ...), custom_call_target="tpu_custom_call", output_to_operand_aliasing={{0}: (4, {}), {1}: (5, {})} | custom-call | tf_op jit(solution)/shard_map/far/pallas_call | solution.py:426
  25.9 0.0 collective-permute-done.rim
  25.9 2.7 %last.1 = (f32[6,1,1024]{2,1,0:T(1,128)S(1)}, f32[6,72,1024]{2,1,0:T(8,128)S(1)}, bf16[1,6,1,128,512]{4,3,2,1,0:T(8,128)(2,1)}) custom-call(bf16[2,128,512]{2,1,0:T(8,128)(2,1)S(1)} %collective-permute-done.rim, bf16[512,1536]{1,0:T(8,128)(2,1)S(1)} %get-tuple-element.32.w_all, ...), custom_call_target="tpu_custom_call", output_to_operand_aliasing={{0}: (3, {}), {1}: (4, {})} | custom-call | tf_op jit(solution)/shard_map/last/pallas_call | solution.py:437
Async XLA Ops:
  2.2 12.7 %collective-permute-start.2 = (bf16[6,128,512]{2,1,0:T(8,128)(2,1)S(1)}, bf16[6,128,512]{2,1,0:T(8,128)(2,1)S(1)}, u32[]{:S(2)}, u32[]{:S(2)}) collective-permute-start(bf16[6,128,512]{2,1,0:T(8,128)(2,1)S(1)} %get-tuple-element.31.own), channel_id=1, source_target_pairs={{0,1},{1,0},{2,3},{3,2},{4,5},{5,4},{6,7},{7,6},{8,9},{9,8},{10,11... | collective-permute-start | bytes 2359304 | tf_op jit(solution)/shard_map/ppermute | solution.py:375
  2.9 18.9 %collective-permute-start.1 = (bf16[4,128,512]{2,1,0:T(8,128)(2,1)S(1)}, bf16[4,128,512]{2,1,0:T(8,128)(2,1)S(1)}, u32[]{:S(2)}, u32[]{:S(2)}) collective-permute-start(bf16[4,128,512]{2,1,0:T(8,128)(2,1)S(1)} %get-tuple-element.26.first), channel_id=1, source_target_pairs={{1,2},{3,4},{5,6},{7,8},{9,10},{11,12},{13,14},{2,1},{4,3},{6,5},{... | collective-permute-start | bytes 1572872 | tf_op jit(solution)/shard_map/ppermute | solution.py:375
  6.0 19.9 %collective-permute-start = (bf16[2,128,512]{2,1,0:T(8,128)(2,1)S(1)}, bf16[2,128,512]{2,1,0:T(8,128)(2,1)S(1)}, u32[]{:S(2)}, u32[]{:S(2)}) collective-permute-start(bf16[2,128,512]{2,1,0:T(8,128)(2,1)S(1)} %get-tuple-element.30), channel_id=1, source_target_pairs={{1,2},{3,4},{5,6},{7,8},{9,10},{11,12},{13,14},{2,1},{4,3},{6,5},{... | collective-permute-start | bytes 786440 | tf_op jit(solution)/shard_map/ppermute | solution.py:375

commit v11 on v10

--- a/solution.py
+++ b/solution.py
@@ -98,19 +98,16 @@
 
 
 def list_pairs(items, masks, by, sides):
-    spare = sum(j1 - j0 for _, _, j0, j1, _, _ in sides)
-    pairs = jnp.int32(0)
+    pairs, singles = jnp.int32(0), jnp.int32(0)
     for i in range(by):
-        start, found, last = pairs, jnp.int32(0), jnp.int32(0)
-        most = 0
+        found, last, most = jnp.int32(0), jnp.int32(0), 0
         for side, exists, j0, j1, tile0, own in sides:
             for b in (0, -1, 1):
                 j = i + b
                 if not j0 <= j < j1:
                     continue
                 tile = tile0 + j - j0
-                items[1, 2 * start + found] = tile
-                items[2, 2 * start + found] = tile
+                items[1, 2 * pairs + found] = tile
                 most += 1
                 if own and b == 0:
                     found = found + 1
@@ -120,66 +117,72 @@
                 on = on if exists is None else on & exists
                 found = found + on.astype(jnp.int32)
                 last = jnp.where(on, tile, last)
-        items[1, 2 * start + found] = last
-        items[2, 2 * start + found] = spare
-        for u in range((most + 1) // 2):
-            items[0, start + u] = i
-        pairs = start + ((found + 1) >> 1)
+        items[2, 2 * singles] = i
+        items[2, 2 * singles + 1] = last
+        for u in range(most // 2):
+            items[0, pairs + u] = i
+        pairs = pairs + (found >> 1)
+        singles = singles + (found & 1)
     items[0, pairs] = 0
     for u in range(2):
         items[1, 2 * pairs + u] = 0
-    return pairs
-
-
-def attend(items, high, keys, vals, qt, top, acc, scores, peaks):
+        items[2, 2 * singles + u] = 0
+    return pairs, singles
+
+
+def attend(items, pairs, singles, keys, vals, qt, top, acc, scores, peaks):
     groups, depth, lanes = qt.shape[1:]
     hd, p = depth // 2, lanes // 2
-
-    def score(t, g):
-        i, k0, k1 = items[0, t], items[1, 2 * t], items[1, 2 * t + 1]
-        rows = slice(g * depth, (g + 1) * depth)
-        cols = slice(g * lanes, (g + 1) * lanes)
-        s0 = nn(keys[k0, :, rows], qt[i, g])
-        s1 = nn(keys[k1, :, rows], qt[i, g])
-        scores[:p, cols] = s0
-        scores[p:, cols] = s1
-        peaks[:, cols] = jnp.max(jnp.maximum(s0, s1), axis=0, keepdims=True)
-
-    def weigh(t, g):
-        i, v0, v1 = items[0, t], items[2, 2 * t], items[2, 2 * t + 1]
-        cols = slice(g * lanes, (g + 1) * lanes)
-        old = top[i, :, cols]
-        new = jnp.maximum(old, peaks[:, cols])
-        probs = jnp.exp(scores[:, cols] - new).astype(BF16)
-        fade = jnp.exp(old - new)
-        both, sums = [], []
-        for h in range(2):
-            rows = slice(h * (hd + ONES), (h + 1) * (hd + ONES))
-            val = jnp.concatenate([vals[v0, g, rows], vals[v1, g, rows]], axis=1)
-            out = nn(val, probs[:, h * p : (h + 1) * p])
-            both.append(out[:hd])
-            sums.append(out[hd : hd + 8])
-        return cols, new, fade, jnp.concatenate(both, axis=1), jnp.concatenate(sums, axis=1)
-
     lead = groups // 2
 
-    def step(t, carry):
-        made = []
-        for g in range(0, groups, lead):
-            for u in range(g, g + lead):
-                score(t + (u + lead) // groups, (u + lead) % groups)
-            for u in range(g, g + lead):
-                made.append(weigh(t, u))
-        i = items[0, t]
-        for cols, new, fade, both, sums in made:
-            top[i, :, cols] = new
-            acc[i, :hd, cols] = acc[i, :hd, cols] * fade + both
-            acc[i, hd:, cols] = acc[i, hd:, cols] * fade + sums
-        return carry
-
-    for g in range(lead):
-        score(0, g)
-    lax.fori_loop(0, high, step, 0)
+    def run(count, tiles, entry):
+        def score(t, g):
+            i, picked = entry(t)
+            rows = slice(g * depth, (g + 1) * depth)
+            cols = slice(g * lanes, (g + 1) * lanes)
+            peak = None
+            for u, k in enumerate(picked):
+                made = nn(keys[k, :, rows], qt[i, g])
+                scores[u * p : (u + 1) * p, cols] = made
+                peak = made if peak is None else jnp.maximum(peak, made)
+            peaks[:, cols] = jnp.max(peak, axis=0, keepdims=True)
+
+        def weigh(t, g):
+            i, picked = entry(t)
+            cols = slice(g * lanes, (g + 1) * lanes)
+            old = top[i, :, cols]
+            new = jnp.maximum(old, peaks[:, cols])
+            probs = jnp.exp(scores[: tiles * p, cols] - new).astype(BF16)
+            fade = jnp.exp(old - new)
+            both, sums = [], []
+            for h in range(2):
+                rows = slice(h * (hd + ONES), (h + 1) * (hd + ONES))
+                val = jnp.concatenate([vals[k, g, rows] for k in picked], axis=1)
+                out = nn(val, probs[:, h * p : (h + 1) * p])
+                both.append(out[:hd])
+                sums.append(out[hd : hd + 8])
+            return cols, new, fade, jnp.concatenate(both, axis=1), jnp.concatenate(sums, axis=1)
+
+        def step(t, carry):
+            made = []
+            for g in range(0, groups, lead):
+                for u in range(g, g + lead):
+                    score(t + (u + lead) // groups, (u + lead) % groups)
+                for u in range(g, g + lead):
+                    made.append(weigh(t, u))
+            i, _ = entry(t)
+            for cols, new, fade, both, sums in made:
+                top[i, :, cols] = new
+                acc[i, :hd, cols] = acc[i, :hd, cols] * fade + both
+                acc[i, hd:, cols] = acc[i, hd:, cols] * fade + sums
+            return carry
+
+        for g in range(lead):
+            score(0, g)
+        lax.fori_loop(0, count, step, 0)
+
+    run(pairs, 2, lambda t: (items[0, t], (items[1, 2 * t], items[1, 2 * t + 1])))
+    run(singles, 1, lambda t: (items[2, 2 * t], (items[2, 2 * t + 1],)))
 
 
 def put_values(vals, tile, g0, v, live):
@@ -237,14 +240,13 @@
     place = lax.broadcasted_iota(jnp.int32, (1, p), 1)
     top[...] = jnp.full_like(top, NEG)
     acc[...] = jnp.zeros_like(acc)
-    vals[by] = jnp.zeros(vals.shape[1:], BF16)
     copies[0].wait()
     copies[1].wait()
-    pairs = list_pairs(items, flags, by, [(0, None, 0, by, 0, True)])
+    pairs, singles = list_pairs(items, flags, by, [(0, None, 0, by, 0, True)])
     for plan, a, j0, j1 in ((plan_near, side, 0, by), (plan0, -side, 0, split), (plan1, -side, split, by)):
         there = (me + a >= 0) & (me + a < n)
         slab = jnp.clip(me + a, 0, n - 1)
-        plan[3, 0] = list_pairs(plan, flags, by, [(a, there, j0, j1, 0, False)])
+        plan[3, 0], plan[3, 1 + 2 * by] = list_pairs(plan, flags, by, [(a, there, j0, j1, 0, False)])
         for i in range(by):
             plan[3, 1 + i] = live[i, 0, me]
         for j in range(j0, j1):
@@ -264,7 +266,7 @@
                 qt[i, g, hd:, :p] = zeros
                 qt[i, g, hd:, p:] = t[mid : mid + hd]
     put_blocks(0, mine, w_all, keys, vals, [place < live[i, 0, me] for i in range(by)])
-    attend(items, pairs, keys, vals, qt, top, acc, scores, peaks)
+    attend(items, pairs, singles, keys, vals, qt, top, acc, scores, peaks)
     copies[3].wait()
 
 
@@ -272,9 +274,8 @@
     by = qt.shape[0]
     blocks, p, width = rim.shape
     place = lax.broadcasted_iota(jnp.int32, (1, p), 1)
-    vals[blocks] = jnp.zeros(vals.shape[1:], BF16)
     put_blocks(0, rim[...].reshape(blocks * p, width), w_all, keys, vals, [place < plan[3, 1 + by + j] for j in range(blocks)])
-    attend(plan, plan[3, 0], keys, vals, qt, top, acc, scores, peaks)
+    attend(plan, plan[3, 0], plan[3, 1 + 2 * by], keys, vals, qt, top, acc, scores, peaks)
 
 
 def near_kernel(rim, w_all, qt, top_in, acc_in, plan, top, acc, keys, vals, scores, peaks):
@@ -386,7 +387,7 @@
     def scratch(tiles):
         return [
             pltpu.VMEM((tiles, p, width), BF16),
-            pltpu.VMEM((tiles + 1, groups, depth + 2 * ONES, p), BF16),
+            pltpu.VMEM((tiles, groups, depth + 2 * ONES, p), BF16),
         ]
 
     ahead = [

time: 28.8 us -> 28.8 us (level)
  the two profiles are of different devices: /device:TPU:27 before, /device:TPU:6 now
where the time goes in v11:
time: 28.8 us; the launch traced here: 28.6 us
  Pallas kernels  18.7 us (65%)
  starting transfers between devices  5.63 us (20%)
  waiting for transfers between devices  4.22 us (15%)
    pallas_call x1, Pallas kernels, shards(): own_work(vmem(normed), masks, counts, w_qkv, w_out)  6.5 us
    ppermute x3, starting transfers between devices, moved(): return lax.ppermute(value, 'gx', pairs)  5.63 us
    ppermute x3, waiting for transfers between devices, moved(): return lax.ppermute(value, 'gx', pairs)  4.22 us
    pallas_call x1, Pallas kernels, shards(): pl.pallas_call(far_kernel, out_shape=(*state, pltpu.VMEM((early, p, width...  4.12 us
    pallas_call x1, Pallas kernels, shards(): pl.pallas_call(last_kernel, out_shape=(*state, pltpu.HBM((1, by, bz, p, w...  3.27 us
    pallas_call x1, Pallas kernels, shards(): near_work(*map(vmem, (near, w_all, qt, top, acc)), smem(plan_near))  2.61 us
    pallas_call x1, Pallas kernels, shards(): pl.pallas_call(gather_kernel, out_shape=(pltpu.VMEM((split, p, width), BF...  1.52 us
    pallas_call x1, Pallas kernels, shards(): tile_rest(vmem(first), vmem(rest), vmem(places), vmem(norm))  0.65 us
  transfers between devices with their start and end apart: 3, of which 1 were waited for; matrix products, arithmetic and copies ran while one was open for 0% of the time, Pallas kernels for 46%

profile of v11, /device:TPU:6, one launch (start us, length us, event | category | flops | bytes accessed | tf_op | source)
XLA Modules:
  0.0 28.6 jit_solution(5356785256445741986)
XLA Ops:
  0.0 1.5 %gather.1 = (bf16[4,128,512]{2,1,0:T(8,128)(2,1)S(1)}, bf16[2,128,512]{2,1,0:T(8,128)(2,1)S(1)}, s32[2,1,128]{2,1,0:T(1,128)S(1)}, f32[2,512]{1,0:T(2,128)S(1)}) custom-call(bf16[1,6,1,128,512]{4,3,2,1,0:T(8,128)(2,1)} %points.1, s32[1,6,1,128]{3,2,1,0:T(1,128)} %order.1, s32[6,1,16]{2,1,0:T(1,128)} %bitcast.3, f32[1,512]{1,0:T(1,128)} %bitcast.5, ...), custom_call_target="tpu_custom_call" | custom-call | tf_op jit(solution)/shard_map/gather/pallas_call | solution.py:340
  1.5 0.6 %rest.1 = (bf16[6,128,512]{2,1,0:T(8,128)(2,1)S(1)}, bf16[6,128,512]{2,1,0:T(8,128)(2,1)S(1)}, bf16[2,128,512]{2,1,0:T(8,128)(2,1)S(1)}) custom-call(bf16[4,128,512]{2,1,0:T(8,128)(2,1)S(1)} %get-tuple-element.26.first, bf16[2,128,512]{2,1,0:T(8,128)(2,1)S(1)} %get-tuple-element.27.rest, s32[2,1,128]{2,1,0:T(1,128)S(1)} %get-tuple-element.28.places, ...), custom_call_target="tpu_custom_call" | custom-call | tf_op jit(solution)/shard_map/rest/pallas_call | solution.py:371
  2.2 0.1 collective-permute-start.2
  2.3 2.5 %collective-permute-start.1 = (bf16[4,128,512]{2,1,0:T(8,128)(2,1)S(1)}, bf16[4,128,512]{2,1,0:T(8,128)(2,1)S(1)}, u32[]{:S(2)}, u32[]{:S(2)}) collective-permute-start(bf16[4,128,512]{2,1,0:T(8,128)(2,1)S(1)} %get-tuple-element.26.first), channel_id=1, source_target_pairs={{1,2},{3,4},{5,6},{7,8},{9,10},{11,12},{13,14},{2,1},{4,3},{6,5},{... | collective-permute-start | bytes 1572872 | tf_op jit(solution)/shard_map/ppermute | solution.py:376
  4.8 3.1 %collective-permute-start = (bf16[2,128,512]{2,1,0:T(8,128)(2,1)S(1)}, bf16[2,128,512]{2,1,0:T(8,128)(2,1)S(1)}, u32[]{:S(2)}, u32[]{:S(2)}) collective-permute-start(bf16[2,128,512]{2,1,0:T(8,128)(2,1)S(1)} %get-tuple-element.30), channel_id=1, source_target_pairs={{1,2},{3,4},{5,6},{7,8},{9,10},{11,12},{13,14},{2,1},{4,3},{6,5},{... | collective-permute-start | bytes 786440 | tf_op jit(solution)/shard_map/ppermute | solution.py:376
  7.8 6.5 %own.1 = (bf16[6,4,128,256]{3,2,1,0:T(8,128)(2,1)S(1)}, f32[6,1,1024]{2,1,0:T(1,128)S(1)}, f32[6,72,1024]{2,1,0:T(8,128)S(1)}, bf16[512,1536]{1,0:T(8,128)(2,1)S...) custom-call(bf16[6,128,512]{2,1,0:T(8,128)(2,1)S(1)} %get-tuple-element.31., ...), custom_call_target="tpu_custom_call" | custom-call | tf_op jit(solution)/shard_map/own/pallas_call | solution.py:422
  14.4 0.0 collective-permute-done.2.rim
  14.4 2.6 %near.1 = (f32[6,1,1024]{2,1,0:T(1,128)S(1)}, f32[6,72,1024]{2,1,0:T(8,128)S(1)}) custom-call(bf16[6,128,512]{2,1,0:T(8,128)(2,1)S(1)} %collective-permute-done.2.rim, bf16[512,1536]{1,0:T(8,128)(2,1)S(1)} %get-tuple-element.32.w_all, bf16[6,4,128,256]{3,2,1,0:T(8,128)(2,1)S(1)} %get-tuple-element.33.qt, ...), custom_call_target="tpu_custom_call", output_to_operand_aliasing={{0}: (3, {}), {1}: (4, {})} | custom-call | tf_op jit(solution)/shard_map/near/pallas_call | solution.py:425
  17.0 4.2 %collective-permute-done.1.rim = bf16[4,128,512]{2,1,0:T(8,128)(2,1)S(1)} collective-permute-done((bf16[4,128,512]{2,1,0:T(8,128)(2,1)S(1)}, bf16[4,128,512]{2,1,0:T(8,128)(2,1)S(1)}, u32[]{:S(2)}, u32[]{:S(2)}) %collective-permute-start.1) | collective-permute-done | bytes 524320 | tf_op jit(solution)/shard_map/ppermute | solution.py:376
  21.2 4.1 %far.1 = (f32[6,1,1024]{2,1,0:T(1,128)S(1)}, f32[6,72,1024]{2,1,0:T(8,128)S(1)}, bf16[3,128,512]{2,1,0:T(8,128)(2,1)S(1)}) custom-call(bf16[4,128,512]{2,1,0:T(8,128)(2,1)S(1)} %collective-permute-done.1.rim, f32[2,512]{1,0:T(2,128)S(1)} %get-tuple-element.29.norm, ...), custom_call_target="tpu_custom_call", output_to_operand_aliasing={{0}: (4, {}), {1}: (5, {})} | custom-call | tf_op jit(solution)/shard_map/far/pallas_call | solution.py:427
  25.3 0.0 collective-permute-done.rim
  25.3 3.3 %last.1 = (f32[6,1,1024]{2,1,0:T(1,128)S(1)}, f32[6,72,1024]{2,1,0:T(8,128)S(1)}, bf16[1,6,1,128,512]{4,3,2,1,0:T(8,128)(2,1)}) custom-call(bf16[2,128,512]{2,1,0:T(8,128)(2,1)S(1)} %collective-permute-done.rim, bf16[512,1536]{1,0:T(8,128)(2,1)S(1)} %get-tuple-element.32.w_all, ...), custom_call_target="tpu_custom_call", output_to_operand_aliasing={{0}: (3, {}), {1}: (4, {})} | custom-call | tf_op jit(solution)/shard_map/last/pallas_call | solution.py:438
Async XLA Ops:
  2.2 12.2 %collective-permute-start.2 = (bf16[6,128,512]{2,1,0:T(8,128)(2,1)S(1)}, bf16[6,128,512]{2,1,0:T(8,128)(2,1)S(1)}, u32[]{:S(2)}, u32[]{:S(2)}) collective-permute-start(bf16[6,128,512]{2,1,0:T(8,128)(2,1)S(1)} %get-tuple-element.31.own), channel_id=1, source_target_pairs={{0,1},{1,0},{2,3},{3,2},{4,5},{5,4},{6,7},{7,6},{8,9},{9,8},{10,11... | collective-permute-start | bytes 2359304 | tf_op jit(solution)/shard_map/ppermute | solution.py:376
  2.3 18.9 %collective-permute-start.1 = (bf16[4,128,512]{2,1,0:T(8,128)(2,1)S(1)}, bf16[4,128,512]{2,1,0:T(8,128)(2,1)S(1)}, u32[]{:S(2)}, u32[]{:S(2)}) collective-permute-start(bf16[4,128,512]{2,1,0:T(8,128)(2,1)S(1)} %get-tuple-element.26.first), channel_id=1, source_target_pairs={{1,2},{3,4},{5,6},{7,8},{9,10},{11,12},{13,14},{2,1},{4,3},{6,5},{... | collective-permute-start | bytes 1572872 | tf_op jit(solution)/shard_map/ppermute | solution.py:376
  4.8 20.5 %collective-permute-start = (bf16[2,128,512]{2,1,0:T(8,128)(2,1)S(1)}, bf16[2,128,512]{2,1,0:T(8,128)(2,1)S(1)}, u32[]{:S(2)}, u32[]{:S(2)}) collective-permute-start(bf16[2,128,512]{2,1,0:T(8,128)(2,1)S(1)} %get-tuple-element.30), channel_id=1, source_target_pairs={{1,2},{3,4},{5,6},{7,8},{9,10},{11,12},{13,14},{2,1},{4,3},{6,5},{... | collective-permute-start | bytes 786440 | tf_op jit(solution)/shard_map/ppermute | solution.py:376

commit v12 on v11

--- a/solution.py
+++ b/solution.py
@@ -198,7 +198,7 @@
 
 def put_blocks(tile0, x, w_all, keys, vals, lives):
     p, width = keys.shape[1:]
-    wide = min(256, width)
+    wide = min(512, width)
     groups = vals.shape[1]
     for c in range(0, width, wide):
         k = nn(x, w_all[:, width + c : width + c + wide]).astype(BF16)
@@ -209,15 +209,22 @@
             put_values(vals, tile0 + u, c * groups // width, v[rows], live)
 
 
-def finish(i, tiled, acc, w_out, alive):
+def finish(blocks, tiled, acc, w_out, plan):
     hd = acc.shape[1] - 8
     p = tiled.shape[1]
     heads = acc.shape[2] // p
-    attn = acc[i, :hd] * (1.0 / acc[i, hd : hd + 1])
-    attn = jnp.concatenate([attn[:, h * p : (h + 1) * p] for h in range(heads)], axis=0).astype(BF16)
-    mixed = tiled[i].astype(F32) + tn(attn, w_out[...])
+    columns = []
+    for i in blocks:
+        attn = acc[i, :hd] * (1.0 / acc[i, hd : hd + 1])
+        attn = [attn[:, h * p : (h + 1) * p] for h in range(heads)]
+        columns.append(jnp.concatenate(attn, axis=0).astype(BF16))
+    mixed = tn(jnp.concatenate(columns, axis=1), w_out[...])
     place = lax.broadcasted_iota(jnp.int32, (p, 1), 0)
-    return jnp.where(place < alive, mixed, 0.0).astype(BF16)
+    made = []
+    for u, i in enumerate(blocks):
+        value = tiled[i].astype(F32) + mixed[u * p : (u + 1) * p]
+        made.append(jnp.where(place < plan[3, 1 + i], value, 0.0).astype(BF16))
+    return made
 
 
 def own_kernel(
@@ -254,7 +261,7 @@
     zeros = jnp.zeros((hd, p), BF16)
     copies[2].wait()
     mine = own[...].reshape(by * p, width)
-    wide = min(256, width)
+    wide = min(512, width)
     for c in range(0, width, wide):
         q = (nn(mine, w_all[:, c : c + wide]).astype(BF16) * BF16(1.0 / hd**0.5)).astype(F32)
         for i in range(by):
@@ -288,8 +295,8 @@
     for j in range(rim.shape[0]):
         nrm[j] = normalise(rim[j], norm[0:1], norm[1:2])
     far_work(nrm, w_all, qt, plan, top, acc, keys, vals, scores, peaks)
-    for i in range(held.shape[0]):
-        held[i] = finish(i, tiled, acc, w_out, plan[3, 1 + i])
+    for i, value in enumerate(finish(range(held.shape[0]), tiled, acc, w_out, plan)):
+        held[i] = value
 
 
 def last_kernel(
@@ -301,8 +308,8 @@
     for copy in copies:
         copy.start()
     far_work(rim, w_all, qt, plan, top, acc, keys, vals, scores, peaks)
-    for i in range(early, by):
-        out[i - early] = finish(i, tiled, acc, w_out, plan[3, 1 + i])
+    for i, value in enumerate(finish(range(early, by), tiled, acc, w_out, plan), early):
+        out[i - early] = value
         copies.append(pltpu.make_async_copy(out.at[i - early], result.at[0, i, 0], sems.at[i]))
         copies[-1].start()
     for copy in copies:

time: 28.8 us -> 28.6 us (level)
  Pallas kernels: 18.7 us -> 18.2 us
  transfers between devices with their start and end apart: 3 -> 3, of which waited for: 1 -> 1; matrix products, arithmetic and copies ran while one was open for 0% -> 0% of each run, Pallas kernels for 46% -> 45%
where the time goes in v12:
time: 28.6 us; the launch traced here: 28.3 us
  Pallas kernels  18.2 us (64%)
  starting transfers between devices  5.63 us (20%)
  waiting for transfers between devices  4.47 us (16%)
    pallas_call x1, Pallas kernels, shards(): own_work(vmem(normed), masks, counts, w_qkv, w_out)  6.39 us
    ppermute x3, starting transfers between devices, moved(): return lax.ppermute(value, 'gx', pairs)  5.63 us
    ppermute x3, waiting for transfers between devices, moved(): return lax.ppermute(value, 'gx', pairs)  4.47 us
    pallas_call x1, Pallas kernels, shards(): pl.pallas_call(far_kernel, out_shape=(*state, pltpu.VMEM((early, p, width...  3.97 us
    pallas_call x1, Pallas kernels, shards(): pl.pallas_call(last_kernel, out_shape=(*state, pltpu.HBM((1, by, bz, p, w...  3.16 us
    pallas_call x1, Pallas kernels, shards(): near_work(*map(vmem, (near, w_all, qt, top, acc)), smem(plan_near))  2.48 us
    pallas_call x1, Pallas kernels, shards(): pl.pallas_call(gather_kernel, out_shape=(pltpu.VMEM((split, p, width), BF...  1.52 us
    pallas_call x1, Pallas kernels, shards(): tile_rest(vmem(first), vmem(rest), vmem(places), vmem(norm))  0.65 us
  transfers between devices with their start and end apart: 3, of which 1 were waited for; matrix products, arithmetic and copies ran while one was open for 0% of the time, Pallas kernels for 45%

profile of v12, /device:TPU:6, one launch (start us, length us, event | category | flops | bytes accessed | tf_op | source)
XLA Modules:
  0.0 28.3 jit_solution(4563326659655065151)
XLA Ops:
  0.0 1.5 %gather.1 = (bf16[4,128,512]{2,1,0:T(8,128)(2,1)S(1)}, bf16[2,128,512]{2,1,0:T(8,128)(2,1)S(1)}, s32[2,1,128]{2,1,0:T(1,128)S(1)}, f32[2,512]{1,0:T(2,128)S(1)}) custom-call(bf16[1,6,1,128,512]{4,3,2,1,0:T(8,128)(2,1)} %points.1, s32[1,6,1,128]{3,2,1,0:T(1,128)} %order.1, s32[6,1,16]{2,1,0:T(1,128)} %bitcast.3, f32[1,512]{1,0:T(1,128)} %bitcast.5, ...), custom_call_target="tpu_custom_call" | custom-call | tf_op jit(solution)/shard_map/gather/pallas_call | solution.py:347
  1.5 0.6 %rest.1 = (bf16[6,128,512]{2,1,0:T(8,128)(2,1)S(1)}, bf16[6,128,512]{2,1,0:T(8,128)(2,1)S(1)}, bf16[2,128,512]{2,1,0:T(8,128)(2,1)S(1)}) custom-call(bf16[4,128,512]{2,1,0:T(8,128)(2,1)S(1)} %get-tuple-element.26.first, bf16[2,128,512]{2,1,0:T(8,128)(2,1)S(1)} %get-tuple-element.27.rest, s32[2,1,128]{2,1,0:T(1,128)S(1)} %get-tuple-element.28.places, ...), custom_call_target="tpu_custom_call" | custom-call | tf_op jit(solution)/shard_map/rest/pallas_call | solution.py:378
  2.2 0.1 collective-permute-start.2
  2.3 2.5 %collective-permute-start.1 = (bf16[4,128,512]{2,1,0:T(8,128)(2,1)S(1)}, bf16[4,128,512]{2,1,0:T(8,128)(2,1)S(1)}, u32[]{:S(2)}, u32[]{:S(2)}) collective-permute-start(bf16[4,128,512]{2,1,0:T(8,128)(2,1)S(1)} %get-tuple-element.26.first), channel_id=1, source_target_pairs={{1,2},{3,4},{5,6},{7,8},{9,10},{11,12},{13,14},{2,1},{4,3},{6,5},{... | collective-permute-start | bytes 1572872 | tf_op jit(solution)/shard_map/ppermute | solution.py:383
  4.8 3.1 %collective-permute-start = (bf16[2,128,512]{2,1,0:T(8,128)(2,1)S(1)}, bf16[2,128,512]{2,1,0:T(8,128)(2,1)S(1)}, u32[]{:S(2)}, u32[]{:S(2)}) collective-permute-start(bf16[2,128,512]{2,1,0:T(8,128)(2,1)S(1)} %get-tuple-element.30), channel_id=1, source_target_pairs={{1,2},{3,4},{5,6},{7,8},{9,10},{11,12},{13,14},{2,1},{4,3},{6,5},{... | collective-permute-start | bytes 786440 | tf_op jit(solution)/shard_map/ppermute | solution.py:383
  7.8 6.4 %own.1 = (bf16[6,4,128,256]{3,2,1,0:T(8,128)(2,1)S(1)}, f32[6,1,1024]{2,1,0:T(1,128)S(1)}, f32[6,72,1024]{2,1,0:T(8,128)S(1)}, bf16[512,1536]{1,0:T(8,128)(2,1)S...) custom-call(bf16[6,128,512]{2,1,0:T(8,128)(2,1)S(1)} %get-tuple-element.31., ...), custom_call_target="tpu_custom_call" | custom-call | tf_op jit(solution)/shard_map/own/pallas_call | solution.py:429
  14.2 0.0 collective-permute-done.2.rim
  14.3 2.5 %near.1 = (f32[6,1,1024]{2,1,0:T(1,128)S(1)}, f32[6,72,1024]{2,1,0:T(8,128)S(1)}) custom-call(bf16[6,128,512]{2,1,0:T(8,128)(2,1)S(1)} %collective-permute-done.2.rim, bf16[512,1536]{1,0:T(8,128)(2,1)S(1)} %get-tuple-element.32.w_all, bf16[6,4,128,256]{3,2,1,0:T(8,128)(2,1)S(1)} %get-tuple-element.33.qt, ...), custom_call_target="tpu_custom_call", output_to_operand_aliasing={{0}: (3, {}), {1}: (4, {})} | custom-call | tf_op jit(solution)/shard_map/near/pallas_call | solution.py:432
  16.7 4.5 %collective-permute-done.1.rim = bf16[4,128,512]{2,1,0:T(8,128)(2,1)S(1)} collective-permute-done((bf16[4,128,512]{2,1,0:T(8,128)(2,1)S(1)}, bf16[4,128,512]{2,1,0:T(8,128)(2,1)S(1)}, u32[]{:S(2)}, u32[]{:S(2)}) %collective-permute-start.1) | collective-permute-done | bytes 524320 | tf_op jit(solution)/shard_map/ppermute | solution.py:383
  21.2 4.0 %far.1 = (f32[6,1,1024]{2,1,0:T(1,128)S(1)}, f32[6,72,1024]{2,1,0:T(8,128)S(1)}, bf16[3,128,512]{2,1,0:T(8,128)(2,1)S(1)}) custom-call(bf16[4,128,512]{2,1,0:T(8,128)(2,1)S(1)} %collective-permute-done.1.rim, f32[2,512]{1,0:T(2,128)S(1)} %get-tuple-element.29.norm, ...), custom_call_target="tpu_custom_call", output_to_operand_aliasing={{0}: (4, {}), {1}: (5, {})} | custom-call | tf_op jit(solution)/shard_map/far/pallas_call | solution.py:434
  25.2 0.0 collective-permute-done.rim
  25.2 3.2 %last.1 = (f32[6,1,1024]{2,1,0:T(1,128)S(1)}, f32[6,72,1024]{2,1,0:T(8,128)S(1)}, bf16[1,6,1,128,512]{4,3,2,1,0:T(8,128)(2,1)}) custom-call(bf16[2,128,512]{2,1,0:T(8,128)(2,1)S(1)} %collective-permute-done.rim, bf16[512,1536]{1,0:T(8,128)(2,1)S(1)} %get-tuple-element.32.w_all, ...), custom_call_target="tpu_custom_call", output_to_operand_aliasing={{0}: (3, {}), {1}: (4, {})} | custom-call | tf_op jit(solution)/shard_map/last/pallas_call | solution.py:445
Async XLA Ops:
  2.2 12.1 %collective-permute-start.2 = (bf16[6,128,512]{2,1,0:T(8,128)(2,1)S(1)}, bf16[6,128,512]{2,1,0:T(8,128)(2,1)S(1)}, u32[]{:S(2)}, u32[]{:S(2)}) collective-permute-start(bf16[6,128,512]{2,1,0:T(8,128)(2,1)S(1)} %get-tuple-element.31.own), channel_id=1, source_target_pairs={{0,1},{1,0},{2,3},{3,2},{4,5},{5,4},{6,7},{7,6},{8,9},{9,8},{10,11... | collective-permute-start | bytes 2359304 | tf_op jit(solution)/shard_map/ppermute | solution.py:383
  2.3 18.9 %collective-permute-start.1 = (bf16[4,128,512]{2,1,0:T(8,128)(2,1)S(1)}, bf16[4,128,512]{2,1,0:T(8,128)(2,1)S(1)}, u32[]{:S(2)}, u32[]{:S(2)}) collective-permute-start(bf16[4,128,512]{2,1,0:T(8,128)(2,1)S(1)} %get-tuple-element.26.first), channel_id=1, source_target_pairs={{1,2},{3,4},{5,6},{7,8},{9,10},{11,12},{13,14},{2,1},{4,3},{6,5},{... | collective-permute-start | bytes 1572872 | tf_op jit(solution)/shard_map/ppermute | solution.py:383
  4.8 20.4 %collective-permute-start = (bf16[2,128,512]{2,1,0:T(8,128)(2,1)S(1)}, bf16[2,128,512]{2,1,0:T(8,128)(2,1)S(1)}, u32[]{:S(2)}, u32[]{:S(2)}) collective-permute-start(bf16[2,128,512]{2,1,0:T(8,128)(2,1)S(1)} %get-tuple-element.30), channel_id=1, source_target_pairs={{1,2},{3,4},{5,6},{7,8},{9,10},{11,12},{13,14},{2,1},{4,3},{6,5},{... | collective-permute-start | bytes 786440 | tf_op jit(solution)/shard_map/ppermute | solution.py:383

commit v13 on v12

--- a/solution.py
+++ b/solution.py
@@ -308,8 +308,8 @@
     for copy in copies:
         copy.start()
     far_work(rim, w_all, qt, plan, top, acc, keys, vals, scores, peaks)
-    for i, value in enumerate(finish(range(early, by), tiled, acc, w_out, plan), early):
-        out[i - early] = value
+    for i in range(early, by):
+        (out[i - early],) = finish([i], tiled, acc, w_out, plan)
         copies.append(pltpu.make_async_copy(out.at[i - early], result.at[0, i, 0], sems.at[i]))
         copies[-1].start()
     for copy in copies:
@@ -332,7 +332,7 @@
     _, by, bz, p, width = points.shape
     hd = width // HEADS
     groups, depth, lanes = HEADS // 2, 2 * hd, 2 * p
-    split = max(by - 2, 1)
+    split = max(by // 2, 1)
     early = max(split - 1, 1)
     whole = pl.BlockSpec(memory_space=pltpu.VMEM)
     apart = pl.BlockSpec(memory_space=pltpu.HBM)

time: 28.6 us -> 28.3 us (0.990)
  the two profiles are of different devices: /device:TPU:6 before, /device:TPU:1 now
where the time goes in v13:
time: 28.3 us; the launch traced here: 27.8 us
  Pallas kernels  17.7 us (63%)
  starting transfers between devices  6.53 us (23%)
  waiting for transfers between devices  3.45 us (12%)
    ppermute x3, starting transfers between devices, moved(): return lax.ppermute(value, 'gx', pairs)  6.53 us
    pallas_call x1, Pallas kernels, shards(): own_work(vmem(normed), masks, counts, w_qkv, w_out)  6.27 us
    pallas_call x1, Pallas kernels, shards(): pl.pallas_call(last_kernel, out_shape=(*state, pltpu.HBM((1, by, bz, p, w...  3.7 us
    ppermute x3, waiting for transfers between devices, moved(): return lax.ppermute(value, 'gx', pairs)  3.45 us
    pallas_call x1, Pallas kernels, shards(): near_work(*map(vmem, (near, w_all, qt, top, acc)), smem(plan_near))  3 us
    pallas_call x1, Pallas kernels, shards(): pl.pallas_call(far_kernel, out_shape=(*state, pltpu.VMEM((early, p, width...  2.67 us
    pallas_call x1, Pallas kernels, shards(): pl.pallas_call(gather_kernel, out_shape=(pltpu.VMEM((split, p, width), BF...  1.43 us
    pallas_call x1, Pallas kernels, shards(): tile_rest(vmem(first), vmem(rest), vmem(places), vmem(norm))  0.66 us
  transfers between devices with their start and end apart: 3, of which 2 were waited for; matrix products, arithmetic and copies ran while one was open for 0% of the time, Pallas kernels for 43%

profile of v13, /device:TPU:1, one launch (start us, length us, event | category | flops | bytes accessed | tf_op | source)
XLA Modules:
  0.0 27.8 jit_solution(17993980404740049935)
XLA Ops:
  0.0 1.4 %gather.1 = (bf16[3,128,512]{2,1,0:T(8,128)(2,1)S(1)}, bf16[3,128,512]{2,1,0:T(8,128)(2,1)S(1)}, s32[3,1,128]{2,1,0:T(1,128)S(1)}, f32[2,512]{1,0:T(2,128)S(1)}) custom-call(bf16[1,6,1,128,512]{4,3,2,1,0:T(8,128)(2,1)} %points.1, s32[1,6,1,128]{3,2,1,0:T(1,128)} %order.1, s32[6,1,16]{2,1,0:T(1,128)} %bitcast.3, f32[1,512]{1,0:T(1,128)} %bitcast.5, ...), custom_call_target="tpu_custom_call" | custom-call | tf_op jit(solution)/shard_map/gather/pallas_call | solution.py:347
  1.4 0.7 %rest.1 = (bf16[6,128,512]{2,1,0:T(8,128)(2,1)S(1)}, bf16[6,128,512]{2,1,0:T(8,128)(2,1)S(1)}, bf16[3,128,512]{2,1,0:T(8,128)(2,1)S(1)}) custom-call(bf16[3,128,512]{2,1,0:T(8,128)(2,1)S(1)} %get-tuple-element.26.first, bf16[3,128,512]{2,1,0:T(8,128)(2,1)S(1)} %get-tuple-element.27.rest, s32[3,1,128]{2,1,0:T(1,128)S(1)} %get-tuple-element.28.places, ...), custom_call_target="tpu_custom_call" | custom-call | tf_op jit(solution)/shard_map/rest/pallas_call | solution.py:378
  2.1 0.1 collective-permute-start.2
  2.2 4.5 %collective-permute-start.1 = (bf16[3,128,512]{2,1,0:T(8,128)(2,1)S(1)}, bf16[3,128,512]{2,1,0:T(8,128)(2,1)S(1)}, u32[]{:S(2)}, u32[]{:S(2)}) collective-permute-start(bf16[3,128,512]{2,1,0:T(8,128)(2,1)S(1)} %get-tuple-element.26.first), channel_id=1, source_target_pairs={{1,2},{3,4},{5,6},{7,8},{9,10},{11,12},{13,14},{2,1},{4,3},{6,5},{... | collective-permute-start | bytes 1179656 | tf_op jit(solution)/shard_map/ppermute | solution.py:383
  6.7 1.9 %collective-permute-start = (bf16[3,128,512]{2,1,0:T(8,128)(2,1)S(1)}, bf16[3,128,512]{2,1,0:T(8,128)(2,1)S(1)}, u32[]{:S(2)}, u32[]{:S(2)}) collective-permute-start(bf16[3,128,512]{2,1,0:T(8,128)(2,1)S(1)} %get-tuple-element.30), channel_id=1, source_target_pairs={{1,2},{3,4},{5,6},{7,8},{9,10},{11,12},{13,14},{2,1},{4,3},{6,5},{... | collective-permute-start | bytes 1179656 | tf_op jit(solution)/shard_map/ppermute | solution.py:383
  8.7 6.3 %own.1 = (bf16[6,4,128,256]{3,2,1,0:T(8,128)(2,1)S(1)}, f32[6,1,1024]{2,1,0:T(1,128)S(1)}, f32[6,72,1024]{2,1,0:T(8,128)S(1)}, bf16[512,1536]{1,0:T(8,128)(2,1)S...) custom-call(bf16[6,128,512]{2,1,0:T(8,128)(2,1)S(1)} %get-tuple-element.31., ...), custom_call_target="tpu_custom_call" | custom-call | tf_op jit(solution)/shard_map/own/pallas_call | solution.py:429
  14.9 0.0 collective-permute-done.2.rim
  14.9 3.0 %near.1 = (f32[6,1,1024]{2,1,0:T(1,128)S(1)}, f32[6,72,1024]{2,1,0:T(8,128)S(1)}) custom-call(bf16[6,128,512]{2,1,0:T(8,128)(2,1)S(1)} %collective-permute-done.2.rim, bf16[512,1536]{1,0:T(8,128)(2,1)S(1)} %get-tuple-element.32.w_all, bf16[6,4,128,256]{3,2,1,0:T(8,128)(2,1)S(1)} %get-tuple-element.33.qt, ...), custom_call_target="tpu_custom_call", output_to_operand_aliasing={{0}: (3, {}), {1}: (4, {})} | custom-call | tf_op jit(solution)/shard_map/near/pallas_call | solution.py:432
  17.9 1.9 %collective-permute-done.1.rim = bf16[3,128,512]{2,1,0:T(8,128)(2,1)S(1)} collective-permute-done((bf16[3,128,512]{2,1,0:T(8,128)(2,1)S(1)}, bf16[3,128,512]{2,1,0:T(8,128)(2,1)S(1)}, u32[]{:S(2)}, u32[]{:S(2)}) %collective-permute-start.1) | collective-permute-done | bytes 393248 | tf_op jit(solution)/shard_map/ppermute | solution.py:383
  19.9 2.7 %far.1 = (f32[6,1,1024]{2,1,0:T(1,128)S(1)}, f32[6,72,1024]{2,1,0:T(8,128)S(1)}, bf16[2,128,512]{2,1,0:T(8,128)(2,1)S(1)}) custom-call(bf16[3,128,512]{2,1,0:T(8,128)(2,1)S(1)} %collective-permute-done.1.rim, f32[2,512]{1,0:T(2,128)S(1)} %get-tuple-element.29.norm, ...), custom_call_target="tpu_custom_call", output_to_operand_aliasing={{0}: (4, {}), {1}: (5, {})} | custom-call | tf_op jit(solution)/shard_map/far/pallas_call | solution.py:434
  22.5 1.5 %collective-permute-done.rim = bf16[3,128,512]{2,1,0:T(8,128)(2,1)S(1)} collective-permute-done((bf16[3,128,512]{2,1,0:T(8,128)(2,1)S(1)}, bf16[3,128,512]{2,1,0:T(8,128)(2,1)S(1)}, u32[]{:S(2)}, u32[]{:S(2)}) %collective-permute-start) | collective-permute-done | bytes 393248 | tf_op jit(solution)/shard_map/ppermute | solution.py:383
  24.1 3.7 %last.1 = (f32[6,1,1024]{2,1,0:T(1,128)S(1)}, f32[6,72,1024]{2,1,0:T(8,128)S(1)}, bf16[1,6,1,128,512]{4,3,2,1,0:T(8,128)(2,1)}) custom-call(bf16[3,128,512]{2,1,0:T(8,128)(2,1)S(1)} %collective-permute-done.rim, bf16[512,1536]{1,0:T(8,128)(2,1)S(1)} %get-tuple-element.32.w_all, ...), custom_call_target="tpu_custom_call", output_to_operand_aliasing={{0}: (3, {}), {1}: (4, {})} | custom-call | tf_op jit(solution)/shard_map/last/pallas_call | solution.py:445
Async XLA Ops:
  2.1 12.8 %collective-permute-start.2 = (bf16[6,128,512]{2,1,0:T(8,128)(2,1)S(1)}, bf16[6,128,512]{2,1,0:T(8,128)(2,1)S(1)}, u32[]{:S(2)}, u32[]{:S(2)}) collective-permute-start(bf16[6,128,512]{2,1,0:T(8,128)(2,1)S(1)} %get-tuple-element.31.own), channel_id=1, source_target_pairs={{0,1},{1,0},{2,3},{3,2},{4,5},{5,4},{6,7},{7,6},{8,9},{9,8},{10,11... | collective-permute-start | bytes 2359304 | tf_op jit(solution)/shard_map/ppermute | solution.py:383
  2.2 17.7 %collective-permute-start.1 = (bf16[3,128,512]{2,1,0:T(8,128)(2,1)S(1)}, bf16[3,128,512]{2,1,0:T(8,128)(2,1)S(1)}, u32[]{:S(2)}, u32[]{:S(2)}) collective-permute-start(bf16[3,128,512]{2,1,0:T(8,128)(2,1)S(1)} %get-tuple-element.26.first), channel_id=1, source_target_pairs={{1,2},{3,4},{5,6},{7,8},{9,10},{11,12},{13,14},{2,1},{4,3},{6,5},{... | collective-permute-start | bytes 1179656 | tf_op jit(solution)/shard_map/ppermute | solution.py:383
  6.7 17.3 %collective-permute-start = (bf16[3,128,512]{2,1,0:T(8,128)(2,1)S(1)}, bf16[3,128,512]{2,1,0:T(8,128)(2,1)S(1)}, u32[]{:S(2)}, u32[]{:S(2)}) collective-permute-start(bf16[3,128,512]{2,1,0:T(8,128)(2,1)S(1)} %get-tuple-element.30), channel_id=1, source_target_pairs={{1,2},{3,4},{5,6},{7,8},{9,10},{11,12},{13,14},{2,1},{4,3},{6,5},{... | collective-permute-start | bytes 1179656 | tf_op jit(solution)/shard_map/ppermute | solution.py:383

commit v14 on v13

--- a/solution.py
+++ b/solution.py
@@ -304,14 +304,22 @@
     sems
 ):
     by, early = tiled.shape[0], held.shape[0]
+    parts = 4
+    tall = tiled.shape[1] // parts
     copies = [pltpu.make_async_copy(held.at[i], result.at[0, i, 0], sems.at[i]) for i in range(early)]
     for copy in copies:
         copy.start()
     far_work(rim, w_all, qt, plan, top, acc, keys, vals, scores, peaks)
     for i in range(early, by):
         (out[i - early],) = finish([i], tiled, acc, w_out, plan)
-        copies.append(pltpu.make_async_copy(out.at[i - early], result.at[0, i, 0], sems.at[i]))
-        copies[-1].start()
+        for c in range(parts):
+            rows = pl.ds(c * tall, tall)
+            copies.append(
+                pltpu.make_async_copy(
+                    out.at[i - early, rows], result.at[0, i, 0, rows], sems.at[early + (i - early) * parts + c]
+                )
+            )
+            copies[-1].start()
     for copy in copies:
         copy.wait()
 
@@ -451,7 +459,7 @@
             *scratch(by - split),
             *ahead,
             pltpu.VMEM((by - early, p, width), BF16),
-            pltpu.SemaphoreType.DMA((by,)),
+            pltpu.SemaphoreType.DMA((4 * by,)),
         ],
         input_output_aliases={3: 0, 4: 1},
         compiler_params=params,

time: 28.3 us -> 28.4 us (level)
  no operation moved by 1% of the time
where the time goes in v14:
time: 28.4 us; the launch traced here: 27.9 us
  Pallas kernels  17.9 us (63%)
  starting transfers between devices  6.53 us (23%)
  waiting for transfers between devices  3.45 us (12%)
    ppermute x3, starting transfers between devices, moved(): return lax.ppermute(value, 'gx', pairs)  6.53 us
    pallas_call x1, Pallas kernels, shards(): own_work(vmem(normed), masks, counts, w_qkv, w_out)  6.27 us
    pallas_call x1, Pallas kernels, shards(): pl.pallas_call(last_kernel, out_shape=(*state, pltpu.HBM((1, by, bz, p, w...  3.86 us
    ppermute x3, waiting for transfers between devices, moved(): return lax.ppermute(value, 'gx', pairs)  3.45 us
    pallas_call x1, Pallas kernels, shards(): near_work(*map(vmem, (near, w_all, qt, top, acc)), smem(plan_near))  3 us
    pallas_call x1, Pallas kernels, shards(): pl.pallas_call(far_kernel, out_shape=(*state, pltpu.VMEM((early, p, width...  2.67 us
    pallas_call x1, Pallas kernels, shards(): pl.pallas_call(gather_kernel, out_shape=(pltpu.VMEM((split, p, width), BF...  1.43 us
    pallas_call x1, Pallas kernels, shards(): tile_rest(vmem(first), vmem(rest), vmem(places), vmem(norm))  0.66 us
  transfers between devices with their start and end apart: 3, of which 2 were waited for; matrix products, arithmetic and copies ran while one was open for 0% of the time, Pallas kernels for 43%

profile of v14, /device:TPU:1, one launch (start us, length us, event | category | flops | bytes accessed | tf_op | source)
XLA Modules:
  0.0 27.9 jit_solution(6293272806012602477)
XLA Ops:
  0.0 1.4 %gather.1 = (bf16[3,128,512]{2,1,0:T(8,128)(2,1)S(1)}, bf16[3,128,512]{2,1,0:T(8,128)(2,1)S(1)}, s32[3,1,128]{2,1,0:T(1,128)S(1)}, f32[2,512]{1,0:T(2,128)S(1)}) custom-call(bf16[1,6,1,128,512]{4,3,2,1,0:T(8,128)(2,1)} %points.1, s32[1,6,1,128]{3,2,1,0:T(1,128)} %order.1, s32[6,1,16]{2,1,0:T(1,128)} %bitcast.3, f32[1,512]{1,0:T(1,128)} %bitcast.5, ...), custom_call_target="tpu_custom_call" | custom-call | tf_op jit(solution)/shard_map/gather/pallas_call | solution.py:355
  1.4 0.7 %rest.1 = (bf16[6,128,512]{2,1,0:T(8,128)(2,1)S(1)}, bf16[6,128,512]{2,1,0:T(8,128)(2,1)S(1)}, bf16[3,128,512]{2,1,0:T(8,128)(2,1)S(1)}) custom-call(bf16[3,128,512]{2,1,0:T(8,128)(2,1)S(1)} %get-tuple-element.26.first, bf16[3,128,512]{2,1,0:T(8,128)(2,1)S(1)} %get-tuple-element.27.rest, s32[3,1,128]{2,1,0:T(1,128)S(1)} %get-tuple-element.28.places, ...), custom_call_target="tpu_custom_call" | custom-call | tf_op jit(solution)/shard_map/rest/pallas_call | solution.py:386
  2.1 0.1 collective-permute-start.2
  2.2 4.5 %collective-permute-start.1 = (bf16[3,128,512]{2,1,0:T(8,128)(2,1)S(1)}, bf16[3,128,512]{2,1,0:T(8,128)(2,1)S(1)}, u32[]{:S(2)}, u32[]{:S(2)}) collective-permute-start(bf16[3,128,512]{2,1,0:T(8,128)(2,1)S(1)} %get-tuple-element.26.first), channel_id=1, source_target_pairs={{1,2},{3,4},{5,6},{7,8},{9,10},{11,12},{13,14},{2,1},{4,3},{6,5},{... | collective-permute-start | bytes 1179656 | tf_op jit(solution)/shard_map/ppermute | solution.py:391
  6.7 1.9 %collective-permute-start = (bf16[3,128,512]{2,1,0:T(8,128)(2,1)S(1)}, bf16[3,128,512]{2,1,0:T(8,128)(2,1)S(1)}, u32[]{:S(2)}, u32[]{:S(2)}) collective-permute-start(bf16[3,128,512]{2,1,0:T(8,128)(2,1)S(1)} %get-tuple-element.30), channel_id=1, source_target_pairs={{1,2},{3,4},{5,6},{7,8},{9,10},{11,12},{13,14},{2,1},{4,3},{6,5},{... | collective-permute-start | bytes 1179656 | tf_op jit(solution)/shard_map/ppermute | solution.py:391
  8.7 6.3 %own.1 = (bf16[6,4,128,256]{3,2,1,0:T(8,128)(2,1)S(1)}, f32[6,1,1024]{2,1,0:T(1,128)S(1)}, f32[6,72,1024]{2,1,0:T(8,128)S(1)}, bf16[512,1536]{1,0:T(8,128)(2,1)S...) custom-call(bf16[6,128,512]{2,1,0:T(8,128)(2,1)S(1)} %get-tuple-element.31., ...), custom_call_target="tpu_custom_call" | custom-call | tf_op jit(solution)/shard_map/own/pallas_call | solution.py:437
  14.9 0.0 collective-permute-done.2.rim
  14.9 3.0 %near.1 = (f32[6,1,1024]{2,1,0:T(1,128)S(1)}, f32[6,72,1024]{2,1,0:T(8,128)S(1)}) custom-call(bf16[6,128,512]{2,1,0:T(8,128)(2,1)S(1)} %collective-permute-done.2.rim, bf16[512,1536]{1,0:T(8,128)(2,1)S(1)} %get-tuple-element.32.w_all, bf16[6,4,128,256]{3,2,1,0:T(8,128)(2,1)S(1)} %get-tuple-element.33.qt, ...), custom_call_target="tpu_custom_call", output_to_operand_aliasing={{0}: (3, {}), {1}: (4, {})} | custom-call | tf_op jit(solution)/shard_map/near/pallas_call | solution.py:440
  17.9 1.9 %collective-permute-done.1.rim = bf16[3,128,512]{2,1,0:T(8,128)(2,1)S(1)} collective-permute-done((bf16[3,128,512]{2,1,0:T(8,128)(2,1)S(1)}, bf16[3,128,512]{2,1,0:T(8,128)(2,1)S(1)}, u32[]{:S(2)}, u32[]{:S(2)}) %collective-permute-start.1) | collective-permute-done | bytes 393248 | tf_op jit(solution)/shard_map/ppermute | solution.py:391
  19.9 2.7 %far.1 = (f32[6,1,1024]{2,1,0:T(1,128)S(1)}, f32[6,72,1024]{2,1,0:T(8,128)S(1)}, bf16[2,128,512]{2,1,0:T(8,128)(2,1)S(1)}) custom-call(bf16[3,128,512]{2,1,0:T(8,128)(2,1)S(1)} %collective-permute-done.1.rim, f32[2,512]{1,0:T(2,128)S(1)} %get-tuple-element.29.norm, ...), custom_call_target="tpu_custom_call", output_to_operand_aliasing={{0}: (4, {}), {1}: (5, {})} | custom-call | tf_op jit(solution)/shard_map/far/pallas_call | solution.py:442
  22.5 1.5 %collective-permute-done.rim = bf16[3,128,512]{2,1,0:T(8,128)(2,1)S(1)} collective-permute-done((bf16[3,128,512]{2,1,0:T(8,128)(2,1)S(1)}, bf16[3,128,512]{2,1,0:T(8,128)(2,1)S(1)}, u32[]{:S(2)}, u32[]{:S(2)}) %collective-permute-start) | collective-permute-done | bytes 393248 | tf_op jit(solution)/shard_map/ppermute | solution.py:391
  24.1 3.9 %last.1 = (f32[6,1,1024]{2,1,0:T(1,128)S(1)}, f32[6,72,1024]{2,1,0:T(8,128)S(1)}, bf16[1,6,1,128,512]{4,3,2,1,0:T(8,128)(2,1)}) custom-call(bf16[3,128,512]{2,1,0:T(8,128)(2,1)S(1)} %collective-permute-done.rim, bf16[512,1536]{1,0:T(8,128)(2,1)S(1)} %get-tuple-element.32.w_all, ...), custom_call_target="tpu_custom_call", output_to_operand_aliasing={{0}: (3, {}), {1}: (4, {})} | custom-call | tf_op jit(solution)/shard_map/last/pallas_call | solution.py:453
Async XLA Ops:
  2.1 12.8 %collective-permute-start.2 = (bf16[6,128,512]{2,1,0:T(8,128)(2,1)S(1)}, bf16[6,128,512]{2,1,0:T(8,128)(2,1)S(1)}, u32[]{:S(2)}, u32[]{:S(2)}) collective-permute-start(bf16[6,128,512]{2,1,0:T(8,128)(2,1)S(1)} %get-tuple-element.31.own), channel_id=1, source_target_pairs={{0,1},{1,0},{2,3},{3,2},{4,5},{5,4},{6,7},{7,6},{8,9},{9,8},{10,11... | collective-permute-start | bytes 2359304 | tf_op jit(solution)/shard_map/ppermute | solution.py:391
  2.2 17.7 %collective-permute-start.1 = (bf16[3,128,512]{2,1,0:T(8,128)(2,1)S(1)}, bf16[3,128,512]{2,1,0:T(8,128)(2,1)S(1)}, u32[]{:S(2)}, u32[]{:S(2)}) collective-permute-start(bf16[3,128,512]{2,1,0:T(8,128)(2,1)S(1)} %get-tuple-element.26.first), channel_id=1, source_target_pairs={{1,2},{3,4},{5,6},{7,8},{9,10},{11,12},{13,14},{2,1},{4,3},{6,5},{... | collective-permute-start | bytes 1179656 | tf_op jit(solution)/shard_map/ppermute | solution.py:391
  6.7 17.3 %collective-permute-start = (bf16[3,128,512]{2,1,0:T(8,128)(2,1)S(1)}, bf16[3,128,512]{2,1,0:T(8,128)(2,1)S(1)}, u32[]{:S(2)}, u32[]{:S(2)}) collective-permute-start(bf16[3,128,512]{2,1,0:T(8,128)(2,1)S(1)} %get-tuple-element.30), channel_id=1, source_target_pairs={{1,2},{3,4},{5,6},{7,8},{9,10},{11,12},{13,14},{2,1},{4,3},{6,5},{... | collective-permute-start | bytes 1179656 | tf_op jit(solution)/shard_map/ppermute | solution.py:391
